TPU v7x, 32 devices: a whole 2x2x4 slice. The times are simulated.
32 devices in a mesh: fsdp: 8 (over z, y), tensor: 4 (over x, core).
Axes of the slice: x: 2, y: 2, z: 4, core: 2. Of those that a mesh axis runs over, the one named last changes fastest.
Arguments:
- tokens: bfloat16 [64, 1024, 1024], P('fsdp', 'tensor'), may hold values from -6 to 6
- cotangent: bfloat16 [64, 1024, 1024], P('fsdp', 'tensor'), may hold values from -6 to 6
- routed_index: int32 [64, 128], P('fsdp'), may hold values from 0 to 1023, as said below
- query_weight: bfloat16 [1024, 1024], P('fsdp', 'tensor'), may hold values from -0.1875 to 0.1875
- key_weight: bfloat16 [1024, 1024], P('fsdp', 'tensor'), may hold values from -0.1875 to 0.1875
- value_weight: bfloat16 [1024, 1024], P('fsdp', 'tensor'), may hold values from -0.1875 to 0.1875
- output_weight: bfloat16 [1024, 1024], P('tensor', 'fsdp'), may hold values from -0.5 to 0.5
- up_weight: bfloat16 [1024, 4096], P('fsdp', 'tensor'), may hold values from -0.1875 to 0.1875
- down_weight: bfloat16 [4096, 1024], P('tensor', 'fsdp'), may hold values from -0.09375 to 0.09375
- router_weight: bfloat16 [1024], P('fsdp'), may hold values from -0.1875 to 0.1875
- attn_gain: bfloat16 [1024], P('fsdp'), may hold values from 0.5 to 1.5
- mlp_gain: bfloat16 [1024], P('fsdp'), may hold values from 0.5 to 1.5
Outputs:
- mixed: bfloat16 [64, 1024, 1024], P('fsdp', 'tensor')
- token_grad: bfloat16 [64, 1024, 1024], P('fsdp', 'tensor')
- query_weight_grad: float32 [1024, 1024], P('fsdp', 'tensor')
- key_weight_grad: float32 [1024, 1024], P('fsdp', 'tensor')
- value_weight_grad: float32 [1024, 1024], P('fsdp', 'tensor')
- output_weight_grad: float32 [1024, 1024], P('tensor', 'fsdp')
- up_weight_grad: float32 [1024, 4096], P('fsdp', 'tensor')
- down_weight_grad: float32 [4096, 1024], P('tensor', 'fsdp')
- router_weight_grad: float32 [1024], P('fsdp')
- attn_gain_grad: float32 [1024], P('fsdp')
- mlp_gain_grad: float32 [1024], P('fsdp')
Inputs may be any that keep to these rules, and one draw needn't show every extreme that they name: `routed_index`: each row holds 128 distinct positions of one sequence in ascending order; its first is 0 and its last is 1023.
All inputs are finite; a program needn't handle non-finite values.
Results may differ from a plain program's by a relative error of at most 0.011.
Values may be sent and summed in bfloat16 or wider, within the bound.
No kernel may reach another device: no remote copies, remote signals or barrier semaphores. Data moves between devices by JAX's collectives and lax.ppermute only.
A program may use at most 192 MiB of HBM per device.

v0:
```python
import jax
import jax.numpy as jnp
from jax import lax
from jax.sharding import PartitionSpec as P

HEAD_DIM = 64
BLOCK = 256


EPS = 1e-06
NEG = -1e30
HIGH = lax.Precision.HIGHEST


def pick_rows(values, routed_index, offset, pos_span):
    local_pos = routed_index - offset
    inside = (local_pos >= 0) & (local_pos < pos_span)
    safe_pos = jnp.clip(local_pos, 0, pos_span - 1)
    chosen = jnp.take_along_axis(values, safe_pos[:, :, None], axis=1).astype(jnp.float32)
    return jnp.where(inside[:, :, None], chosen, jnp.zeros_like(chosen))


def place_target(routed_index, offset, pos_span):
    local_pos = routed_index - offset
    inside = (local_pos >= 0) & (local_pos < pos_span)
    return jnp.where(inside, local_pos, pos_span)


def place_rows(values, new_rows, target):
    seq_ids = jnp.arange(values.shape[0], dtype=jnp.int32)[:, None]
    return values.at[seq_ids, target].set(new_rows, mode="drop")


def rms_scale(inputs):
    return lax.rsqrt(jnp.mean(inputs * inputs, axis=-1, keepdims=True) + EPS)


def norm_back(grad_out, inputs, scale_rows, gain):
    normal = inputs * scale_rows
    grad_norm = grad_out * gain
    grad_in = scale_rows * (
        grad_norm - normal * jnp.mean(grad_norm * normal, axis=-1, keepdims=True)
    )
    return (grad_in, jnp.sum(grad_out * normal, axis=0))


def attend_scores(query_heads, key_heads, allowed, score_scale):
    scores = (
        jnp.einsum("sqhe,skhe->shqk", query_heads, key_heads, preferred_element_type=jnp.float32)
        * score_scale
    )
    return jnp.where(allowed[:, None], scores, NEG)


def shards(
    tokens,
    cotangent,
    routed_index,
    query_weight,
    key_weight,
    value_weight,
    output_weight,
    up_weight,
    down_weight,
    router_weight,
    attn_gain,
    mlp_gain,
):
    tensor_count = lax.axis_size("tensor")
    tensor_rank = lax.axis_index("tensor")
    seq_count, pos_span, model_width = tokens.shape
    routed = routed_index.shape[1]
    share_rows = routed // tensor_count
    offset = tensor_rank * pos_span
    score_scale = HEAD_DIM ** (-0.5)
    strided = (seq_count, share_rows, tensor_count, model_width)
    mine = (seq_count, share_rows, 1, model_width)
    picked_tokens = pick_rows(tokens, routed_index, offset, pos_span).reshape(strided)
    picked_grads = pick_rows(cotangent, routed_index, offset, pos_span).reshape(strided)
    token_share, grad_share = (
        lax.psum_scatter(
            picked_tokens.astype(jnp.bfloat16), "tensor", scatter_dimension=2, tiled=True
        ).astype(jnp.float32),
        lax.psum_scatter(
            picked_grads.astype(jnp.bfloat16), "tensor", scatter_dimension=2, tiled=True
        ).astype(jnp.float32),
    )
    flat_tokens = token_share.reshape(-1, model_width)
    grad_flat = grad_share.reshape(-1, model_width)
    full_params = (
        lax.all_gather(query_weight, "fsdp", axis=0, tiled=True),
        lax.all_gather(key_weight, "fsdp", axis=0, tiled=True),
        lax.all_gather(value_weight, "fsdp", axis=0, tiled=True),
        lax.all_gather(output_weight, "fsdp", axis=1, tiled=True),
        lax.all_gather(up_weight, "fsdp", axis=0, tiled=True),
        lax.all_gather(down_weight, "fsdp", axis=1, tiled=True),
        lax.all_gather(router_weight, "fsdp", axis=0, tiled=True),
        lax.all_gather(attn_gain, "fsdp", axis=0, tiled=True),
        lax.all_gather(mlp_gain, "fsdp", axis=0, tiled=True),
    )
    (
        query_full,
        key_full,
        value_full,
        output_full,
        up_full,
        down_full,
        router_full,
        first_gain,
        second_gain,
    ) = full_params
    router_logit = jnp.dot(flat_tokens, router_full.astype(jnp.float32), precision=HIGH)
    gate_value = jax.nn.sigmoid(router_logit)
    first_scale = rms_scale(flat_tokens)
    first_normed = (flat_tokens * first_scale * first_gain.astype(jnp.float32)).astype(jnp.bfloat16)
    normed_all = lax.all_gather(first_normed.reshape(mine), "tensor", axis=2, tiled=True).reshape(
        -1, model_width
    )
    local_width = query_full.shape[1]
    heads_local = local_width // HEAD_DIM
    head_shape = (seq_count, routed, heads_local, HEAD_DIM)
    query_heads = (
        jnp.dot(normed_all, query_full, preferred_element_type=jnp.float32)
        .astype(jnp.bfloat16)
        .reshape(head_shape)
    )
    key_heads = (
        jnp.dot(normed_all, key_full, preferred_element_type=jnp.float32)
        .astype(jnp.bfloat16)
        .reshape(head_shape)
    )
    value_heads = (
        jnp.dot(normed_all, value_full, preferred_element_type=jnp.float32)
        .astype(jnp.bfloat16)
        .reshape(head_shape)
    )
    blocks = routed_index // BLOCK
    allowed = blocks[:, None, :] <= blocks[:, :, None]
    scores = attend_scores(query_heads, key_heads, allowed, score_scale)
    top_score = jnp.max(scores, axis=-1, keepdims=True)
    log_total = top_score + jnp.log(jnp.sum(jnp.exp(scores - top_score), axis=-1, keepdims=True))
    attn_probs = jnp.exp(scores - log_total).astype(jnp.bfloat16)
    context = (
        jnp.einsum("shqk,skhe->sqhe", attn_probs, value_heads, preferred_element_type=jnp.float32)
        .astype(jnp.bfloat16)
        .reshape(-1, local_width)
    )
    attn_part = jnp.dot(context, output_full, preferred_element_type=jnp.float32)
    attn_share = lax.psum_scatter(
        attn_part.reshape(strided), "tensor", scatter_dimension=2, tiled=True
    ).reshape(-1, model_width)
    hidden_in = flat_tokens + attn_share
    second_scale = rms_scale(hidden_in)
    second_gain_f = second_gain.astype(jnp.float32)
    second_normed = (hidden_in * second_scale * second_gain_f).astype(jnp.bfloat16)
    normed_mid = lax.all_gather(second_normed.reshape(mine), "tensor", axis=2, tiled=True).reshape(
        -1, model_width
    )
    up_value = jnp.dot(normed_mid, up_full, preferred_element_type=jnp.float32)
    activated = jax.nn.gelu(up_value).astype(jnp.bfloat16)
    mlp_part = jnp.dot(activated, down_full, preferred_element_type=jnp.float32)
    mlp_share = (
        lax.psum_scatter(
            mlp_part.reshape(strided).astype(jnp.bfloat16),
            "tensor",
            scatter_dimension=2,
            tiled=True,
        )
        .astype(jnp.float32)
        .reshape(-1, model_width)
    )
    branch = attn_share + mlp_share
    out_share = (flat_tokens + gate_value[:, None] * branch).astype(jnp.bfloat16)
    out_all = lax.all_gather(out_share.reshape(mine), "tensor", axis=2, tiled=True).reshape(
        seq_count, routed, model_width
    )
    target = place_target(routed_index, offset, pos_span)
    mixed = place_rows(tokens, out_all, target)
    back_params = (
        lax.all_gather(query_weight, "fsdp", axis=0, tiled=True),
        lax.all_gather(key_weight, "fsdp", axis=0, tiled=True),
        lax.all_gather(value_weight, "fsdp", axis=0, tiled=True),
        lax.all_gather(output_weight, "fsdp", axis=1, tiled=True),
        lax.all_gather(up_weight, "fsdp", axis=0, tiled=True),
        lax.all_gather(down_weight, "fsdp", axis=1, tiled=True),
        lax.all_gather(router_weight, "fsdp", axis=0, tiled=True),
        lax.all_gather(attn_gain, "fsdp", axis=0, tiled=True),
        lax.all_gather(mlp_gain, "fsdp", axis=0, tiled=True),
    )
    (
        query_back,
        key_back,
        value_back,
        output_back,
        up_back,
        down_back,
        router_back,
        first_gain_back,
        second_gain_back,
    ) = back_params
    gate_grad = jnp.sum(grad_flat * branch, axis=-1) * gate_value * (1.0 - gate_value)
    router_part = jnp.sum(flat_tokens * gate_grad[:, None], axis=0)
    branch_grad = gate_value[:, None] * grad_flat
    input_rows_grad = grad_flat + gate_grad[:, None] * router_back.astype(jnp.float32)
    mlp_grad_all = lax.all_gather(
        branch_grad.astype(jnp.bfloat16).reshape(mine), "tensor", axis=2, tiled=True
    ).reshape(-1, model_width)
    down_grad = jnp.einsum("rf,rd->fd", activated, mlp_grad_all, preferred_element_type=jnp.float32)
    act_grad = jnp.einsum("rd,fd->rf", mlp_grad_all, down_back, preferred_element_type=jnp.float32)
    gelu_out, gelu_back = jax.vjp(jax.nn.gelu, up_value)
    up_grad = gelu_back(act_grad)[0].astype(jnp.bfloat16)
    up_grad_weight = jnp.einsum(
        "rd,rf->df", normed_mid, up_grad, preferred_element_type=jnp.float32
    )
    mid_part = jnp.einsum("rf,df->rd", up_grad, up_back, preferred_element_type=jnp.float32)
    mid_share = lax.psum_scatter(
        mid_part.reshape(strided), "tensor", scatter_dimension=2, tiled=True
    ).reshape(-1, model_width)
    hidden_grad, second_gain_grad = norm_back(
        mid_share, hidden_in, second_scale, second_gain_back.astype(jnp.float32)
    )
    input_rows_grad = input_rows_grad + hidden_grad
    attn_grad_rows = (branch_grad + hidden_grad).astype(jnp.bfloat16)
    attn_grad_all = lax.all_gather(
        attn_grad_rows.reshape(mine), "tensor", axis=2, tiled=True
    ).reshape(-1, model_width)
    output_grad_weight = jnp.einsum(
        "rc,rd->cd", context, attn_grad_all, preferred_element_type=jnp.float32
    )
    context_grad = (
        jnp.einsum("rd,cd->rc", attn_grad_all, output_back, preferred_element_type=jnp.float32)
        .astype(jnp.bfloat16)
        .reshape(head_shape)
    )
    scores_again = attend_scores(query_heads, key_heads, allowed, score_scale)
    probs_exact = jnp.exp(scores_again - log_total)
    prob_grad = jnp.einsum(
        "sqhe,skhe->shqk", context_grad, value_heads, preferred_element_type=jnp.float32
    )
    value_grad = jnp.einsum(
        "shqk,sqhe->skhe",
        probs_exact.astype(jnp.bfloat16),
        context_grad,
        preferred_element_type=jnp.float32,
    ).astype(jnp.bfloat16)
    row_inner = jnp.sum(probs_exact * prob_grad, axis=-1, keepdims=True)
    score_grad = (probs_exact * (prob_grad - row_inner)).astype(jnp.bfloat16)
    query_grad = (
        (
            jnp.einsum("shqk,skhe->sqhe", score_grad, key_heads, preferred_element_type=jnp.float32)
            * score_scale
        )
        .astype(jnp.bfloat16)
        .reshape(-1, local_width)
    )
    key_grad = (
        (
            jnp.einsum(
                "shqk,sqhe->skhe", score_grad, query_heads, preferred_element_type=jnp.float32
            )
            * score_scale
        )
        .astype(jnp.bfloat16)
        .reshape(-1, local_width)
    )
    value_grad = value_grad.reshape(-1, local_width)
    query_grad_weight = jnp.einsum(
        "rd,rc->dc", normed_all, query_grad, preferred_element_type=jnp.float32
    )
    key_grad_weight = jnp.einsum(
        "rd,rc->dc", normed_all, key_grad, preferred_element_type=jnp.float32
    )
    value_grad_weight = jnp.einsum(
        "rd,rc->dc", normed_all, value_grad, preferred_element_type=jnp.float32
    )
    first_part = jnp.einsum("rc,dc->rd", query_grad, query_back, preferred_element_type=jnp.float32)
    first_part = first_part + jnp.einsum(
        "rc,dc->rd", key_grad, key_back, preferred_element_type=jnp.float32
    )
    first_part = first_part + jnp.einsum(
        "rc,dc->rd", value_grad, value_back, preferred_element_type=jnp.float32
    )
    first_share = lax.psum_scatter(
        first_part.reshape(strided), "tensor", scatter_dimension=2, tiled=True
    ).reshape(-1, model_width)
    norm_grad, first_gain_grad = norm_back(
        first_share, flat_tokens, first_scale, first_gain_back.astype(jnp.float32)
    )
    input_rows_grad = input_rows_grad + norm_grad
    vector_part = jnp.stack([router_part, first_gain_grad, second_gain_grad])
    rows_back, vector_all = (
        lax.all_gather(input_rows_grad.reshape(mine), "tensor", axis=2, tiled=True),
        lax.all_gather(vector_part, "tensor", axis=0, tiled=True),
    )
    vector_sum = jnp.sum(vector_all.reshape(tensor_count, 3, model_width), axis=0)
    token_grad = place_rows(
        cotangent, rows_back.reshape(seq_count, routed, model_width).astype(jnp.bfloat16), target
    )
    summed = (
        lax.psum_scatter(query_grad_weight, "fsdp", scatter_dimension=0, tiled=True),
        lax.psum_scatter(key_grad_weight, "fsdp", scatter_dimension=0, tiled=True),
        lax.psum_scatter(value_grad_weight, "fsdp", scatter_dimension=0, tiled=True),
        lax.psum_scatter(output_grad_weight, "fsdp", scatter_dimension=1, tiled=True),
        lax.psum_scatter(up_grad_weight, "fsdp", scatter_dimension=0, tiled=True),
        lax.psum_scatter(down_grad, "fsdp", scatter_dimension=1, tiled=True),
        lax.psum_scatter(vector_sum[0], "fsdp", scatter_dimension=0, tiled=True),
        lax.psum_scatter(vector_sum[1], "fsdp", scatter_dimension=0, tiled=True),
        lax.psum_scatter(vector_sum[2], "fsdp", scatter_dimension=0, tiled=True),
    )
    return (
        mixed,
        token_grad,
        summed[0],
        summed[1],
        summed[2],
        summed[3],
        summed[4],
        summed[5],
        summed[6],
        summed[7],
        summed[8],
    )


def solution(mesh):
    in_specs = (
        P("fsdp", "tensor", None),
        P("fsdp", "tensor", None),
        P("fsdp", None),
        P("fsdp", "tensor"),
        P("fsdp", "tensor"),
        P("fsdp", "tensor"),
        P("tensor", "fsdp"),
        P("fsdp", "tensor"),
        P("tensor", "fsdp"),
        P("fsdp"),
        P("fsdp"),
        P("fsdp"),
    )
    out_specs = (
        P("fsdp", "tensor", None),
        P("fsdp", "tensor", None),
        P("fsdp", "tensor"),
        P("fsdp", "tensor"),
        P("fsdp", "tensor"),
        P("tensor", "fsdp"),
        P("fsdp", "tensor"),
        P("tensor", "fsdp"),
        P("fsdp"),
        P("fsdp"),
        P("fsdp"),
    )
    return jax.shard_map(shards, mesh=mesh, in_specs=in_specs, out_specs=out_specs, check_vma=False)
```

profile of v0, /device:TPU:0, one launch (start us, length us, event | category | flops | bytes accessed | tf_op | source)
XLA Modules:
  0.0 1439.0 jit_solution(8234796519459619486)
XLA Ops:
  14.4 39.0 %gather_fusion = bf16[1024,1024]{1,0:T(8,128)(2,1)S(1)} fusion(bf16[8,256,1024]{2,1,0:T(8,128)(2,1)} %copy.187, s32[1024]{0:T(1024)S(1)} %or_bitcast_fusion), kind=kCustom, calls=%fused_computation.clone | custom fusion | bytes 4202496 | tf_op jit(solution)/shard_map/jit(take_along_axis)/gather | solution.py:19
  53.4 44.3 %gather_fusion.1 = bf16[1024,1024]{1,0:T(8,128)(2,1)} fusion(bf16[8,256,1024]{2,1,0:T(8,128)(2,1)} %copy.188, s32[1024]{0:T(1024)S(1)} %or_bitcast_fusion), kind=kCustom, calls=%fused_computation.1.clone | custom fusion | bytes 4202496 | tf_op jit(solution)/shard_map/jit(take_along_axis)/gather | solution.py:19
  97.6 9.0 select_convert_fusion
  109.7 21.4 %all-gather.1 = bf16[8,1,128]{2,1,0:T(2,128)(2,1)S(1)} all-gather(bf16[1,1,128]{2,1,0:T(2,128)(2,1)S(1)} %bitcast.220), channel_id=1, replica_groups=mesh['fsdp'=8,'tensor'=4] {'fsdp'}, dimensions={0}, use_global_device_ids=true | all-gather | bytes 2304 | tf_op jit(solution)/shard_map/all_gather | solution.py:98
  131.8 29.9 %all-reduce.17.cloned.1.call-done = bf16[8,32,4,1024]{3,1,2,0:T(8,128)(2,1)} async-done(((bf16[8,32,4,1024]{3,1,2,0:T(8,128)(2,1)}), bf16[8,32,4,1024]{3,1,2,0:T(8,128)(2,1)}) %all-reduce.17.cloned.1.call-update) | async-done | bytes 2097168
  165.7 31.6 %all_gather.61 = bf16[1024,256]{1,0:T(8,128)(2,1)S(1)} all-gather(bf16[128,256]{1,0:T(8,128)(2,1)S(1)} %copy-done.21), channel_id=1, replica_groups=mesh['fsdp'=8,'tensor'=4] {'fsdp'}, dimensions={0}, use_global_device_ids=true | all-gather | bytes 589824 | tf_op jit(solution)/shard_map/all_gather | solution.py:91
  197.3 31.5 %all_gather.62 = bf16[1024,256]{1,0:T(8,128)(2,1)S(1)} all-gather(bf16[128,256]{1,0:T(8,128)(2,1)S(1)} %copy-done.22), channel_id=1, replica_groups=mesh['fsdp'=8,'tensor'=4] {'fsdp'}, dimensions={0}, use_global_device_ids=true | all-gather | bytes 589824 | tf_op jit(solution)/shard_map/all_gather | solution.py:92
  228.8 33.4 %all_gather.60 = bf16[1024,256]{1,0:T(8,128)(2,1)} all-gather(bf16[128,256]{1,0:T(8,128)(2,1)S(1)} %copy-done.23), channel_id=1, replica_groups=mesh['fsdp'=8,'tensor'=4] {'fsdp'}, dimensions={0}, use_global_device_ids=true | all-gather | bytes 589824 | tf_op jit(solution)/shard_map/all_gather | solution.py:93
  262.2 28.3 %all_gather.63 = bf16[256,1024]{1,0:T(8,128)(2,1)} all-gather(bf16[256,128]{1,0:T(8,128)(2,1)S(1)} %copy-done.24), channel_id=1, replica_groups=mesh['fsdp'=8,'tensor'=4] {'fsdp'}, dimensions={1}, use_global_device_ids=true | all-gather | bytes 589824 | tf_op jit(solution)/shard_map/all_gather | solution.py:94
  316.7 19.1 %all-gather.2 = bf16[8,1,128]{2,1,0:T(2,128)(2,1)S(1)} all-gather(bf16[1,1,128]{2,1,0:T(2,128)(2,1)S(1)} %bitcast.221), channel_id=1, replica_groups=mesh['fsdp'=8,'tensor'=4] {'fsdp'}, dimensions={0}, use_global_device_ids=true | all-gather | bytes 2304 | tf_op jit(solution)/shard_map/all_gather | solution.py:99
  335.8 64.6 %all-reduce.19.cloned.1.call-done = f32[8,32,4,1024]{3,1,2,0:T(8,128)} async-done(((f32[8,32,4,1024]{3,1,2,0:T(8,128)}), f32[8,32,4,1024]{3,1,2,0:T(8,128)}) %all-reduce.19.cloned.1.call-update) | async-done | bytes 4194320
  409.2 17.3 %all-gather.15.cloned.1.call-done = bf16[8,32,4,1024]{3,1,2,0:T(8,128)(2,1)} async-done(((bf16[8,32,1,1024]{3,1,2,0:T(8,128)(2,1)}), bf16[8,32,4,1024]{3,1,2,0:T(8,128)(2,1)}) %all-gather.15.cloned.1.call-update) | async-done | bytes 2097168 | tf_op jit(solution)/shard_map/all_gather | solution.py:156
  435.1 42.7 %all-gather.17.cloned.1.call-done = bf16[1024,1024]{1,0:T(8,128)(2,1)} async-done(((bf16[128,1024]{1,0:T(8,128)(2,1)}), bf16[1024,1024]{1,0:T(8,128)(2,1)}) %all-gather.17.cloned.1.call-update) | async-done | bytes 2097168 | tf_op jit(solution)/shard_map/all_gather | solution.py:95
  484.3 45.0 %all-gather.19.cloned.1.call-done = bf16[1024,1024]{1,0:T(8,128)(2,1)} async-done(((bf16[1024,128]{1,0:T(8,128)(2,1)}), bf16[1024,1024]{1,0:T(8,128)(2,1)}) %all-gather.19.cloned.1.call-update) | async-done | bytes 2097168 | tf_op jit(solution)/shard_map/all_gather | solution.py:96
  529.3 6.9 convolution_convert_fusion
  544.6 17.6 %all-gather = bf16[8,1,128]{2,1,0:T(2,128)(2,1)S(1)} all-gather(bf16[1,1,128]{2,1,0:T(2,128)(2,1)S(1)} %bitcast.222), channel_id=1, replica_groups=mesh['fsdp'=8,'tensor'=4] {'fsdp'}, dimensions={0}, use_global_device_ids=true | all-gather | bytes 2304 | tf_op jit(solution)/shard_map/all_gather | solution.py:97
  563.5 64.5 %all-reduce.25.cloned.1.call-done = (bf16[8,32,4,1024]{3,1,2,0:T(8,128)(2,1)}, bf16[8,32,4,1024]{3,1,2,0:T(8,128)(2,1)}) async-done(((bf16[8,32,4,1024]{3,1,2,0:T(8,128)(2,1)}, bf16[8,32,4,1024]{3,1,2,0:T(8,128)(2,1)}), (bf16[8,32,4,1024]{3,1,2,0:T(8,128)(2,1)}, bf16[8,32,4,1024]{3,1,2,0:T(8,128)(2,1)})) %all-reduce.25.cloned.1.call-update) | async-done | bytes 4194320
  633.7 22.4 %all-gather.23.cloned.1.call-done = bf16[8,32,4,1024]{3,1,2,0:T(8,128)(2,1)} async-done(((bf16[8,32,1,1024]{3,1,2,0:T(8,128)(2,1)}), bf16[8,32,4,1024]{3,1,2,0:T(8,128)(2,1)}) %all-gather.23.cloned.1.call-update) | async-done | bytes 2097168 | tf_op jit(solution)/shard_map/all_gather | solution.py:205
  664.7 8.1 fusion.6
  690.3 85.6 %all-reduce.21.cloned.1.call-done = f32[8,32,4,1024]{3,1,2,0:T(8,128)} async-done(((f32[8,32,4,1024]{3,1,2,0:T(8,128)}), f32[8,32,4,1024]{3,1,2,0:T(8,128)}) %all-reduce.21.cloned.1.call-update) | async-done | bytes 4194320
  781.5 22.7 %all-gather.25.cloned.1.call-done = bf16[8,32,4,1024]{3,1,2,0:T(8,128)(2,1)} async-done(((bf16[8,32,1,1024]{3,1,2,0:T(8,128)(2,1)}), bf16[8,32,4,1024]{3,1,2,0:T(8,128)(2,1)}) %all-gather.25.cloned.1.call-update) | async-done | bytes 2097168 | tf_op jit(solution)/shard_map/all_gather | solution.py:224
  837.0 6.5 copy.109
  843.7 85.5 %all-reduce.23.cloned.1.call-done = f32[8,32,4,1024]{3,1,2,0:T(8,128)} async-done(((f32[8,32,4,1024]{3,1,2,0:T(8,128)}), f32[8,32,4,1024]{3,1,2,0:T(8,128)}) %all-reduce.23.cloned.1.call-update) | async-done | bytes 4194320
  947.7 7.7 fusion.62
  970.6 37.6 %all-reduce.9 = (f32[1024]{0:T(1024)S(1)}, f32[1024]{0:T(1024)S(1)}, f32[1024]{0:T(1024)S(1)}) all-reduce(f32[1024]{0:T(1024)S(1)} %bitcast.218, f32[1024]{0:T(1024)S(1)} %bitcast.217, f32[1024]{0:T(1024)S(1)} %bitcast.216), channel_id=14, replica_groups=mesh['fsdp'=8,'tensor'=4] {'fsdp'}, use_global_device_ids=true, to_apply=%region_26.28.clone | all-reduce | flops 3072 | bytes 24576
  1025.8 10.4 scatter_fusion
  1036.2 10.8 scatter_fusion.1
  1048.7 66.4 %reduce-scatter.29.cloned.1.call-done = f32[128,256]{1,0:T(8,128)} async-done(((f32[1024,256]{1,0:T(8,128)}), f32[128,256]{1,0:T(8,128)}) %reduce-scatter.29.cloned.1.call-update) | async-done | bytes 131088 | tf_op jit(solution)/shard_map/reduce_scatter | solution.py:302
  1115.0 66.7 %reduce-scatter.25.cloned.1.call-done = f32[128,256]{1,0:T(8,128)} async-done(((f32[1024,256]{1,0:T(8,128)}), f32[128,256]{1,0:T(8,128)}) %reduce-scatter.25.cloned.1.call-update) | async-done | bytes 131088 | tf_op jit(solution)/shard_map/reduce_scatter | solution.py:300
  1181.7 66.4 %reduce-scatter.27.cloned.1.call-done = f32[128,256]{1,0:T(8,128)} async-done(((f32[1024,256]{1,0:T(8,128)}), f32[128,256]{1,0:T(8,128)}) %reduce-scatter.27.cloned.1.call-update) | async-done | bytes 131088 | tf_op jit(solution)/shard_map/reduce_scatter | solution.py:301
  1248.1 92.0 %reduce-scatter.35.cloned.1.call-done = f32[1024,128]{1,0:T(8,128)} async-done(((f32[1024,1024]{1,0:T(8,128)}), f32[1024,128]{1,0:T(8,128)}) %reduce-scatter.35.cloned.1.call-update) | async-done | bytes 524304 | tf_op jit(solution)/shard_map/reduce_scatter | solution.py:305
  1340.1 91.9 %reduce-scatter.33.cloned.1.call-done = f32[128,1024]{1,0:T(8,128)} async-done(((f32[1024,1024]{1,0:T(8,128)}), f32[128,1024]{1,0:T(8,128)}) %reduce-scatter.33.cloned.1.call-update) | async-done | bytes 524304 | tf_op jit(solution)/shard_map/reduce_scatter | solution.py:304
  (214 shorter events, 196.6 us)
Async XLA Ops:
  7.2 154.5 %all-reduce.17.cloned.1.call-start = ((), (), s32[]{:S(2)}) async-start(), calls=%async_computation.20 | async-start | bytes 4194304
  7.2 4.8 copy-start.11
  109.1 22.1 %copy-start.33 = (u32[32]{0:T(128)S(1)}, u32[32]{0:T(128)}, u32[]{:S(2)}) copy-start(u32[32]{0:T(128)} %constant.123) | copy-start | bytes 388
  109.1 56.6 %copy-start.21 = (bf16[128,256]{1,0:T(8,128)(2,1)S(1)}, bf16[128,256]{1,0:T(8,128)(2,1)}, u32[]{:S(2)}) copy-start(bf16[128,256]{1,0:T(8,128)(2,1)} %param.17) | copy-start | bytes 196612
  109.1 88.2 %copy-start.22 = (bf16[128,256]{1,0:T(8,128)(2,1)S(1)}, bf16[128,256]{1,0:T(8,128)(2,1)}, u32[]{:S(2)}) copy-start(bf16[128,256]{1,0:T(8,128)(2,1)} %param.18) | copy-start | bytes 196612
  109.1 119.7 %copy-start.23 = (bf16[128,256]{1,0:T(8,128)(2,1)S(1)}, bf16[128,256]{1,0:T(8,128)(2,1)}, u32[]{:S(2)}) copy-start(bf16[128,256]{1,0:T(8,128)(2,1)} %param.19) | copy-start | bytes 196612
  109.1 181.3 %all-gather.13.cloned.1.call-start = ((), (), s32[]{:S(2)}) async-start(), calls=%async_computation.6 | async-start | bytes 2621440 | tf_op jit(solution)/shard_map/all_gather | solution.py:116
  161.7 100.5 %copy-start.24 = (bf16[256,128]{1,0:T(8,128)(2,1)S(1)}, bf16[256,128]{1,0:T(8,128)(2,1)}, u32[]{:S(2)}) copy-start(bf16[256,128]{1,0:T(8,128)(2,1)} %param.20) | copy-start | bytes 196612
  165.4 235.0 %all-reduce.19.cloned.1.call-start = ((), (), s32[]{:S(2)}) async-start(), calls=%async_computation.21 | async-start | bytes 8388608
  197.3 101.7 %copy-start.14 = (bf16[1024,256]{1,0:T(8,128)(2,1)}, bf16[1024,256]{1,0:T(8,128)(2,1)S(1)}, u32[]{:S(2)}) copy-start(bf16[1024,256]{1,0:T(8,128)(2,1)S(1)} %all_gather.61) | copy-start | bytes 1572868
  228.8 67.0 %copy-start.12 = (bf16[1024,256]{1,0:T(8,128)(2,1)}, bf16[1024,256]{1,0:T(8,128)(2,1)S(1)}, u32[]{:S(2)}) copy-start(bf16[1024,256]{1,0:T(8,128)(2,1)S(1)} %all_gather.62) | copy-start | bytes 1572868
  299.0 7.7 copy-start.2
  302.6 4.1 copy-start.4
  308.2 7.9 copy-start.9
  316.1 110.4 %all-gather.15.cloned.1.call-start = ((), (), s32[]{:S(2)}) async-start(), calls=%async_computation.7 | async-start | bytes 2621440 | tf_op jit(solution)/shard_map/all_gather | solution.py:156
  403.6 74.2 %all-gather.17.cloned.1.call-start = ((), (), s32[]{:S(2)}) async-start(), calls=%async_computation.8 | async-start | bytes 2359296 | tf_op jit(solution)/shard_map/all_gather | solution.py:95
  404.2 125.1 %all-gather.19.cloned.1.call-start = ((), (), s32[]{:S(2)}) async-start(), calls=%async_computation.9 | async-start | bytes 2359296 | tf_op jit(solution)/shard_map/all_gather | solution.py:96
  404.8 223.2 %all-reduce.25.cloned.1.call-start = ((), (), s32[]{:S(2)}) async-start(), calls=%async_computation.24 | async-start | bytes 8388608
  544.0 112.2 %all-gather.23.cloned.1.call-start = ((), (), s32[]{:S(2)}) async-start(), calls=%async_computation.11 | async-start | bytes 2621440 | tf_op jit(solution)/shard_map/all_gather | solution.py:205
  633.3 142.6 %all-reduce.21.cloned.1.call-start = ((), (), s32[]{:S(2)}) async-start(), calls=%async_computation.22 | async-start | bytes 8388608
  664.7 9.4 copy-start.31
  690.2 114.0 %all-gather.25.cloned.1.call-start = ((), (), s32[]{:S(2)}) async-start(), calls=%async_computation.12 | async-start | bytes 2621440 | tf_op jit(solution)/shard_map/all_gather | solution.py:224
  781.3 147.9 %all-reduce.23.cloned.1.call-start = ((), (), s32[]{:S(2)}) async-start(), calls=%async_computation.23 | async-start | bytes 8388608
  843.5 85.7 %copy-start.1 = (bf16[8,32,1,1024]{3,1,2,0:T(8,128)(2,1)S(1)}, bf16[8,32,1,1024]{3,1,2,0:T(8,128)(2,1)}, u32[]{:S(2)}) copy-start(bf16[8,32,1,1024]{3,1,2,0:T(8,128)(2,1)} %copy-done) | copy-start | bytes 1572868
  843.6 166.4 %all-gather.21.cloned.1.call-start = ((), (), s32[]{:S(2)}) async-start(), calls=%async_computation.10 | async-start | bytes 2621440 | tf_op jit(solution)/shard_map/all_gather | solution.py:174
  933.0 84.2 %all-gather.27.cloned.1.call-start = ((), (), s32[]{:S(2)}) async-start(), calls=%async_computation.13 | async-start | bytes 2621440 | tf_op jit(solution)/shard_map/all_gather | solution.py:292
  937.1 111.5 %reduce-scatter.31.cloned.1.call-start = ((), (), s32[]{:S(2)}) async-start(), calls=%async_computation.17 | async-start | bytes 1179648 | tf_op jit(solution)/shard_map/reduce_scatter | solution.py:303
  941.1 173.9 %reduce-scatter.29.cloned.1.call-start = ((), (), s32[]{:S(2)}) async-start(), calls=%async_computation.16 | async-start | bytes 1179648 | tf_op jit(solution)/shard_map/reduce_scatter | solution.py:302
  944.0 237.7 %reduce-scatter.25.cloned.1.call-start = ((), (), s32[]{:S(2)}) async-start(), calls=%async_computation.14 | async-start | bytes 1179648 | tf_op jit(solution)/shard_map/reduce_scatter | solution.py:300
  945.9 302.3 %reduce-scatter.27.cloned.1.call-start = ((), (), s32[]{:S(2)}) async-start(), calls=%async_computation.15 | async-start | bytes 1179648 | tf_op jit(solution)/shard_map/reduce_scatter | solution.py:301
  947.7 392.4 %reduce-scatter.35.cloned.1.call-start = ((), (), s32[]{:S(2)}) async-start(), calls=%async_computation.19 | async-start | bytes 4718592 | tf_op jit(solution)/shard_map/reduce_scatter | solution.py:305
  955.4 476.6 %reduce-scatter.33.cloned.1.call-start = ((), (), s32[]{:S(2)}) async-start(), calls=%async_computation.18 | async-start | bytes 4718592 | tf_op jit(solution)/shard_map/reduce_scatter | solution.py:304
  (22 other events, 33.6 us)
Sparse Core Ops, SparseCore 0:
  109.2 52.4 all-reduce.16
  165.6 22.6 all-gather.12
  316.2 84.1 all-reduce.18
  403.7 22.7 all-gather.14
  428.5 49.2 all-gather.16
  479.7 49.5 all-gather.18
  544.1 83.8 all-reduce.24
  633.4 22.7 all-gather.22
  690.3 85.4 all-reduce.20
  781.4 22.7 all-gather.24
  843.7 85.4 all-reduce.22
  933.1 22.7 all-gather.20
  957.5 22.9 all-gather.26
  984.7 63.9 reduce-scatter.30
  1052.5 62.4 reduce-scatter.28
  1119.2 62.4 reduce-scatter.24
  1185.6 62.4 reduce-scatter.26
  1252.6 87.4 reduce-scatter.34
  1344.3 87.6 reduce-scatter.32
where the time goes:
time: 1450 us; the launch traced here: 1440 us
  waiting for transfers between devices  867 us (60%)
  blocking collectives  226 us (16%)
  local copies, waits for them, and re-layouts  220 us (15%)
  matrix products  74.1 us (5%)
  other arithmetic  34.6 us (2%)
  between operations  15.7 us (1%)
    unnamed x24, waiting for transfers between devices  332 us
    reduce_scatter x1, waiting for transfers between devices, shards(): lax.psum_scatter(down_grad, 'fsdp', scatter_dimension=1, tiled=True)  92 us
    reduce_scatter x1, waiting for transfers between devices, shards(): lax.psum_scatter(up_grad_weight, 'fsdp', scatter_dimension=0, tiled=True)  91.9 us
    gather x2, local copies, waits for them, and re-layouts, pick_rows(): jnp.take_along_axis(values, safe_pos[:, :, None], axis=1)  83.3 us
    reduce_scatter x1, waiting for transfers between devices, shards(): lax.psum_scatter(query_grad_weight, 'fsdp', scatter_dimension=0, tiled=True)  66.7 us
    reduce_scatter x1, waiting for transfers between devices, shards(): lax.psum_scatter(value_grad_weight, 'fsdp', scatter_dimension=0, tiled=True)  66.4 us
    reduce_scatter x1, waiting for transfers between devices, shards(): lax.psum_scatter(key_grad_weight, 'fsdp', scatter_dimension=0, tiled=True)  66.4 us
    all_gather x1, waiting for transfers between devices, shards(): lax.all_gather(down_weight, 'fsdp', axis=1, tiled=True)  45 us
  transfers between devices with their start and end apart: 19, of which 16 were waited for; matrix products, arithmetic and copies ran while one was open for 6% of the time, Pallas kernels for 0%

commit v1 on v0

v1 whole, which is shorter than its diff:
```python
import functools

import jax
import jax.numpy as jnp
from jax import lax
from jax.experimental import pallas as pl
from jax.experimental.pallas import tpu as pltpu
from jax.sharding import PartitionSpec as P

HEAD_DIM = 64
BLOCK = 256
EPS = 1e-06
NEG = -1e30
F32 = jnp.float32
BF16 = jnp.bfloat16
GELU_C = 0.7978845608028654
GELU_A = 0.044715

VMEM_SPEC = pl.BlockSpec(memory_space=pltpu.VMEM)
SMEM_SPEC = pl.BlockSpec(memory_space=pltpu.SMEM)
PARAMS = pltpu.CompilerParams(vmem_limit_bytes=48 << 20)


def mm(a, b):
    return jnp.dot(a, b, preferred_element_type=F32)


def mm_t(a, b):
    return lax.dot_general(a, b, (((1,), (1,)), ((), ())), preferred_element_type=F32)


def t_mm(a, b):
    return lax.dot_general(a, b, (((0,), (0,)), ((), ())), preferred_element_type=F32)


def shape(dims, dtype):
    return jax.ShapeDtypeStruct(dims, dtype)


def cost(flops, bytes_accessed):
    return pl.CostEstimate(
        flops=int(flops), bytes_accessed=int(bytes_accessed), transcendentals=0
    )


def tiles(total, width, step):
    def body(j, carry):
        step(pl.ds(pl.multiple_of(j * width, width), width), j)
        return carry

    lax.fori_loop(0, total // width, body, 0)


def pick_kernel(order, onehot, values, out):
    out[...] = mm(onehot[0], values[0]).astype(BF16)


def pick_rows(values, onehot, order):
    count = order.shape[0]
    _, routed, span = onehot.shape
    width = values.shape[2]
    return pl.pallas_call(
        pick_kernel,
        grid_spec=pltpu.PrefetchScalarGridSpec(
            num_scalar_prefetch=1,
            grid=(count,),
            in_specs=[
                pl.BlockSpec((1, routed, span), lambda i, o: (o[i], 0, 0)),
                pl.BlockSpec((1, span, width), lambda i, o: (o[i], 0, 0)),
            ],
            out_specs=pl.BlockSpec((routed, width), lambda i, o: (i, 0)),
        ),
        out_shape=shape((count * routed, width), BF16),
        compiler_params=PARAMS,
        cost_estimate=cost(2 * count * routed * span * width, count * (span + routed) * width * 2),
        name="pick_rows",
    )(order, onehot, values)


def place_kernel(order, onehot_t, r0, r1, r2, r3, base, out):
    piece = pl.program_id(0) // 2
    rows = jnp.where(
        piece < 2,
        jnp.where(piece == 0, r0[...], r1[...]),
        jnp.where(piece == 2, r2[...], r3[...]),
    )
    hot = onehot_t[0]
    taken = jnp.sum(hot.astype(F32), axis=1, keepdims=True) > 0.0
    placed = mm(hot, rows)
    out[0] = jnp.where(taken, placed, base[0].astype(F32)).astype(BF16)


def place_rows(base, onehot_t, pieces, order):
    seqs, span, width = base.shape
    routed = onehot_t.shape[2]
    per = seqs // 4

    def piece_spec(m):
        return pl.BlockSpec(
            (routed, width), lambda i, o: (jnp.clip(i - m * per, 0, per - 1), 0)
        )

    return pl.pallas_call(
        place_kernel,
        grid_spec=pltpu.PrefetchScalarGridSpec(
            num_scalar_prefetch=1,
            grid=(seqs,),
            in_specs=[pl.BlockSpec((1, span, routed), lambda i, o: (o[i], 0, 0))]
            + [piece_spec(m) for m in range(4)]
            + [pl.BlockSpec((1, span, width), lambda i, o: (o[i], 0, 0))],
            out_specs=pl.BlockSpec((1, span, width), lambda i, o: (o[i], 0, 0)),
        ),
        out_shape=shape(base.shape, BF16),
        compiler_params=PARAMS,
        cost_estimate=cost(2 * seqs * routed * span * width, 2 * seqs * span * width * 2),
        name="place_rows",
    )(order, onehot_t, *pieces, base)


def row_call(body, name, inputs, outputs, rows, width, steps=2):
    block = rows // steps
    in_specs = []
    for array, kind in inputs:
        if kind == "w":
            in_specs.append(pl.BlockSpec(array.shape, lambda i: (0, 0)))
        else:
            in_specs.append(pl.BlockSpec((block, array.shape[1]), lambda i: (i, 0)))
    out_specs = []
    out_shapes = []
    for dims, dtype, kind in outputs:
        out_shapes.append(shape(dims, dtype))
        if kind == "w":
            out_specs.append(pl.BlockSpec(dims, lambda i: (0, 0)))
        else:
            out_specs.append(pl.BlockSpec((block, dims[1]), lambda i: (i, 0)))
    return pl.pallas_call(
        body,
        grid=(steps,),
        in_specs=in_specs,
        out_specs=out_specs,
        out_shape=out_shapes,
        compiler_params=PARAMS,
        cost_estimate=cost(20 * rows * width, 2 * rows * width * (len(inputs) + len(outputs))),
        name=name,
    )(*[array for array, _ in inputs])


def row_mean(x):
    return jnp.mean(x, axis=-1, keepdims=True)


def total3(a, b, c):
    return a[...].astype(F32) + b[...].astype(F32) + c[...].astype(F32)


def lanes(col):
    return jnp.broadcast_to(col, (col.shape[0], 128))


def fold(x):
    return jnp.sum(x.reshape(-1, 8, x.shape[1]), axis=0)


def accumulate(ref, value):
    @pl.when(pl.program_id(0) == 0)
    def _():
        ref[...] = value

    @pl.when(pl.program_id(0) > 0)
    def _():
        ref[...] += value


def first_norm_body(a, b, c, vec, rows_out, normed_out, gate_out):
    rows = total3(a, b, c)
    rows_out[...] = rows.astype(BF16)
    logit = jnp.sum(rows * vec[0:1, :], axis=-1, keepdims=True)
    gate_out[...] = lanes(jax.nn.sigmoid(logit))
    scale = lax.rsqrt(row_mean(rows * rows) + EPS)
    normed_out[...] = (rows * scale * vec[1:2, :]).astype(BF16)


def cot_body(a, b, c, gate, cot_out, grad_out):
    cot = total3(a, b, c)
    cot_out[...] = cot.astype(BF16)
    grad_out[...] = (cot * gate[:, 0:1]).astype(BF16)


def second_norm_body(rows, a, b, c, vec, attn_out, normed_out):
    attn = total3(a, b, c)
    attn_out[...] = attn
    hidden = rows[...].astype(F32) + attn
    scale = lax.rsqrt(row_mean(hidden * hidden) + EPS)
    normed_out[...] = (hidden * scale * vec[2:3, :]).astype(BF16)


def second_back_body(rows, attn, cot, gate, a, b, c, vec, grad_out, hidden_out, gain_out):
    second_grad = total3(a, b, c)
    hidden = rows[...].astype(F32) + attn[...]
    scale = lax.rsqrt(row_mean(hidden * hidden) + EPS)
    normal = hidden * scale
    grad = second_grad * vec[2:3, :]
    hidden_grad = scale * (grad - normal * row_mean(grad * normal))
    hidden_out[...] = hidden_grad
    grad_out[...] = (cot[...].astype(F32) * gate[:, 0:1] + hidden_grad).astype(BF16)
    accumulate(gain_out, fold(second_grad * normal))


def out_body(rows, attn, cot, gate, a, b, c, rows_out, gate_grad_out, router_out):
    branch = attn[...] + total3(a, b, c)
    x = rows[...].astype(F32)
    g = gate[:, 0:1]
    rows_out[...] = (x + g * branch).astype(BF16)
    gate_grad = jnp.sum(cot[...].astype(F32) * branch, axis=-1, keepdims=True) * g * (1.0 - g)
    gate_grad_out[...] = lanes(gate_grad)
    accumulate(router_out, fold(x * gate_grad))


def first_back_body(
    rows, cot, gate_grad, hidden_grad, a, b, c, vec, router_part, second_part, grad_out, vec_out, acc
):
    first_grad = total3(a, b, c)
    x = rows[...].astype(F32)
    scale = lax.rsqrt(row_mean(x * x) + EPS)
    normal = x * scale
    grad = first_grad * vec[1:2, :]
    norm_grad = scale * (grad - normal * row_mean(grad * normal))
    grad_out[...] = (
        cot[...].astype(F32) + gate_grad[:, 0:1] * vec[0:1, :] + hidden_grad[...] + norm_grad
    ).astype(BF16)
    accumulate(acc, fold(first_grad * normal))

    @pl.when(pl.program_id(0) == pl.num_programs(0) - 1)
    def _():
        vec_out[0:1, :] = jnp.sum(router_part[...], axis=0, keepdims=True)
        vec_out[1:2, :] = jnp.sum(acc[...], axis=0, keepdims=True)
        vec_out[2:3, :] = jnp.sum(second_part[...], axis=0, keepdims=True)
        vec_out[3:8, :] = jnp.zeros_like(vec_out[3:8, :])


def assemble_kernel(places, *refs):
    *pieces, out = refs
    for number, piece in enumerate(pieces):
        depth = piece.shape[0]
        start = pl.multiple_of(places[number] * depth, depth)
        out[pl.ds(start, depth), :] = piece[...]


def assemble(pieces, places):
    depth, width = pieces[0].shape
    return pl.pallas_call(
        assemble_kernel,
        in_specs=[SMEM_SPEC] + [VMEM_SPEC] * len(pieces),
        out_specs=VMEM_SPEC,
        out_shape=shape((depth * len(pieces), width), BF16),
        compiler_params=PARAMS,
        cost_estimate=cost(0, 4 * depth * len(pieces) * width),
        name="assemble",
    )(places, *pieces)


def head_masks(width):
    lane = lax.broadcasted_iota(jnp.int32, (1, width), 1) // HEAD_DIM
    return [(lane == h).astype(BF16) for h in range(width // HEAD_DIM)]


def spread(x, masks):
    return jnp.concatenate([x * mask for mask in masks], axis=0)


def side_by_side(x, count):
    rows = x.shape[0] // count
    return jnp.concatenate([x[h * rows : (h + 1) * rows] for h in range(count)], axis=1)


def seq_probs(q4, k, bias, count):
    scores = mm_t(q4, k) * (HEAD_DIM**-0.5)
    scores = scores + jnp.concatenate([bias] * count, axis=0)
    top = jnp.max(scores, axis=-1, keepdims=True)
    weight = jnp.exp(scores - top)
    return weight / jnp.sum(weight, axis=-1, keepdims=True)


def attn_fwd_kernel(order, xa, xb, w, bias, qkv, ctx, pa, pb):
    half = xa.shape[0]
    local = ctx.shape[1]
    routed = bias.shape[1]
    heads = local // HEAD_DIM
    masks = head_masks(local)

    def project(cols, j):
        qkv[0:half, cols] = mm(xa[...], w[:, cols]).astype(BF16)
        qkv[half : 2 * half, cols] = mm(xb[...], w[:, cols]).astype(BF16)

    tiles(3 * local, local, project)

    def seq(rows, s):
        q = qkv[rows, 0:local]
        k = qkv[rows, local : 2 * local]
        v = qkv[rows, 2 * local : 3 * local]
        probs = seq_probs(spread(q, masks), k, bias[order[s]], heads).astype(BF16)
        ctx[rows, :] = mm(side_by_side(probs, heads), spread(v, masks)).astype(BF16)

    tiles(2 * half, routed, seq)

    def emit(cols, j):
        wo = w[cols, 3 * local : 4 * local]
        pa[:, cols] = mm_t(ctx[0:half, :], wo).astype(BF16)
        pb[:, cols] = mm_t(ctx[half : 2 * half, :], wo).astype(BF16)

    tiles(pa.shape[1], 256, emit)


def attn_fwd(xa, xb, w, bias, order, local):
    rows, width = xa.shape
    return pl.pallas_call(
        attn_fwd_kernel,
        in_specs=[SMEM_SPEC] + [VMEM_SPEC] * 4,
        out_specs=[VMEM_SPEC] * 4,
        out_shape=[
            shape((2 * rows, 3 * local), BF16),
            shape((2 * rows, local), BF16),
            shape((rows, width), BF16),
            shape((rows, width), BF16),
        ],
        compiler_params=PARAMS,
        cost_estimate=cost(16 * rows * width * local * 2, 8 * rows * width + 2 * width * width),
        name="attn_fwd",
    )(order, xa, xb, w, bias)


def attn_bwd_kernel(order, ga, gb, w, qkv, bias, dqkv, fa, fb, cg):
    half = ga.shape[0]
    local = cg.shape[1]
    routed = bias.shape[1]
    heads = local // HEAD_DIM
    masks = head_masks(local)
    wo = w[:, 3 * local : 4 * local]
    cg[0:half, :] = mm(ga[...], wo).astype(BF16)
    cg[half : 2 * half, :] = mm(gb[...], wo).astype(BF16)

    def seq(rows, s):
        q4 = spread(qkv[rows, 0:local], masks)
        k = qkv[rows, local : 2 * local]
        v = qkv[rows, 2 * local : 3 * local]
        exact = seq_probs(q4, k, bias[order[s]], heads)
        c4 = spread(cg[rows, :], masks)
        prob_grad = mm_t(c4, v)
        dqkv[rows, 2 * local : 3 * local] = t_mm(exact.astype(BF16), c4).astype(BF16)
        inner = jnp.sum(exact * prob_grad, axis=-1, keepdims=True)
        score_grad = (exact * (prob_grad - inner)).astype(BF16)
        scale = HEAD_DIM**-0.5
        dq = mm(side_by_side(score_grad, heads), spread(k, masks)) * scale
        dqkv[rows, 0:local] = dq.astype(BF16)
        dqkv[rows, local : 2 * local] = (t_mm(score_grad, q4) * scale).astype(BF16)

    tiles(2 * half, routed, seq)

    def emit(cols, j):
        wj = w[cols, 0 : 3 * local]
        fa[:, cols] = mm_t(dqkv[0:half, :], wj).astype(BF16)
        fb[:, cols] = mm_t(dqkv[half : 2 * half, :], wj).astype(BF16)

    tiles(fa.shape[1], 256, emit)


def attn_bwd(ga, gb, w, qkv, bias, order, local):
    rows, width = ga.shape
    return pl.pallas_call(
        attn_bwd_kernel,
        in_specs=[SMEM_SPEC] + [VMEM_SPEC] * 5,
        out_specs=[VMEM_SPEC] * 3,
        out_shape=[
            shape((2 * rows, 3 * local), BF16),
            shape((rows, width), BF16),
            shape((rows, width), BF16),
        ],
        scratch_shapes=[pltpu.VMEM((2 * rows, local), BF16)],
        compiler_params=PARAMS,
        cost_estimate=cost(24 * rows * width * local * 2, 8 * rows * width + 2 * width * width),
        name="attn_bwd",
    )(order, ga, gb, w, qkv, bias)


def mlp_kernel(na, nb, ga, gb, w, act, ug, da, db, ma, mb):
    rows, width = na.shape
    part, both, ff = w.shape
    depth = both // 2

    def up(cols, j):
        wu = w[:, 0:depth, cols].reshape(width, -1)
        wd = w[:, depth:both, cols].reshape(width, -1)
        for n, g, at in ((na, ga, 0), (nb, gb, rows)):
            x = mm(n[...], wu)
            inner = jnp.tanh(GELU_C * (x + GELU_A * (x * x * x)))
            half_in = 0.5 * (1.0 + inner)
            act[at : at + rows, cols] = (x * half_in).astype(BF16)
            slope = half_in + (0.5 * GELU_C) * x * (1.0 - inner * inner) * (
                1.0 + (3.0 * GELU_A) * (x * x)
            )
            ug[at : at + rows, cols] = (mm(g[...], wd) * slope).astype(BF16)

    tiles(ff, 256, up)
    group = part * 256 // width

    def back(cols, j):
        wu = w[pl.ds(j * group, group), 0:depth, :].reshape(256, -1)
        da[:, cols] = mm_t(ug[0:rows, :], wu).astype(BF16)
        db[:, cols] = mm_t(ug[rows : 2 * rows, :], wu).astype(BF16)

    tiles(width, 256, back)

    def down(cols, j):
        wd = w[pl.ds(j * group, group), depth:both, :].reshape(256, -1)
        ma[:, cols] = mm_t(act[0:rows, :], wd).astype(BF16)
        mb[:, cols] = mm_t(act[rows : 2 * rows, :], wd).astype(BF16)

    tiles(width, 256, down)


def mlp_both(na, nb, ga, gb, w):
    rows, width = na.shape
    ff = w.shape[2]
    return pl.pallas_call(
        mlp_kernel,
        in_specs=[VMEM_SPEC] * 5,
        out_specs=[VMEM_SPEC] * 6,
        out_shape=[shape((2 * rows, ff), BF16)] * 2 + [shape((rows, width), BF16)] * 4,
        compiler_params=PARAMS,
        cost_estimate=cost(16 * rows * width * ff, 24 * rows * width + 4 * width * ff),
        name="mlp",
    )(na, nb, ga, gb, w)


def grads_kernel(info, *refs, jobs, count):
    per_job = []
    at = 0
    for pieces, halves in jobs:
        per_job.append((refs[at : at + pieces], refs[at + pieces : at + pieces + halves]))
        at += pieces + halves
    sends = refs[at : at + count]
    keeps = refs[at + count : at + 2 * count]
    xt = refs[at + 2 * count]
    depth = 128
    low = info[count] == 0
    for o in range(count):
        cols = pl.ds(pl.multiple_of(info[o] * 256, 256), 256)
        row = 0
        lane = 0
        for xs, ys in per_job:
            step = xs[0].shape[0]
            for m, x in enumerate(xs):
                xt[:, m * step : (m + 1) * step] = x[:, cols].T
            wide = ys[0].shape[1]
            if lane + wide > sends[0].shape[1]:
                row, lane = row + depth, 0

            def block(ncols, j, ys=ys, row=row, lane=lane, o=o):
                size = ys[0].shape[0]
                out = mm(xt[:, 0:size], ys[0][:, ncols]) + mm(
                    xt[:, size : 2 * size], ys[1][:, ncols]
                )
                first, second = out[0:depth], out[depth:256]
                dst = pl.ds(pl.multiple_of(j * 256, 256) + lane, 256)
                sends[o][row : row + depth, dst] = jnp.where(low, second, first).astype(BF16)
                keeps[o][row : row + depth, dst] = jnp.where(low, first, second)

            tiles(wide, 256, block)
            lane += wide


def grad_blocks(jobs, info, rows, width, count, name):
    args = [a for xs, ys in jobs for a in list(xs) + list(ys)]
    total = sum(x.shape[0] for x in jobs[0][0])
    out = pl.pallas_call(
        functools.partial(
            grads_kernel, jobs=[(len(xs), len(ys)) for xs, ys in jobs], count=count
        ),
        in_specs=[SMEM_SPEC] + [VMEM_SPEC] * len(args),
        out_specs=[VMEM_SPEC] * (2 * count),
        out_shape=[shape((rows, width), BF16)] * count + [shape((rows, width), F32)] * count,
        scratch_shapes=[pltpu.VMEM((256, total), BF16)],
        compiler_params=PARAMS,
        cost_estimate=cost(4 * count * rows * width * total, 6 * count * rows * width),
        name=name,
    )(info, *args)
    return out[:count], out[count:]


def swap(x, axis, mask):
    size = lax.axis_size(axis)
    return lax.ppermute(x, axis, [(i, i ^ mask) for i in range(size)])


def gather_rows(own):
    second = swap(own, "tensor", 2)
    first = swap(own, "tensor", 1)
    return own, first, second, swap(second, "tensor", 1)


def scatter_far(near, diag):
    got = swap(diag, "tensor", 1)
    return swap((near.astype(F32) + got.astype(F32)).astype(BF16), "tensor", 2)


def z_perm(size, step, shift):
    places = size // step
    return [
        (((f // step + shift) % places) * step + f % step, f) for f in range(size)
    ]


def fsdp_gather(piece):
    size = lax.axis_size("fsdp")
    me = lax.axis_index("fsdp")
    if size != 8:
        return lax.all_gather(piece, "fsdp", axis=0, tiled=True)
    got = [piece] + [lax.ppermute(piece, "fsdp", z_perm(size, 2, o)) for o in (1, 3, 2)]
    near = [me] + [(me + 2 * o) % size for o in (1, 3, 2)]
    pieces = got + [swap(g, "fsdp", 1) for g in got]
    places = jnp.stack(near + [n ^ 1 for n in near])
    return assemble(pieces, places)


def fsdp_finish(sends, keeps, shifts):
    size = lax.axis_size("fsdp")
    got = [swap(s, "fsdp", 1) for s in sends]
    total = None
    parts = []
    for o, keep, g in zip(shifts, keeps, got):
        both = keep + g.astype(F32)
        if o == 0:
            total = both
        else:
            parts.append(lax.ppermute(both.astype(BF16), "fsdp", z_perm(size, 2, 4 - o)))
    for part in parts:
        total = total + part.astype(F32)
    return total


def shards(
    tokens,
    cotangent,
    routed_index,
    query_weight,
    key_weight,
    value_weight,
    output_weight,
    up_weight,
    down_weight,
    router_weight,
    attn_gain,
    mlp_gain,
):
    fsdp = lax.axis_size("fsdp")
    me_f = lax.axis_index("fsdp")
    me_t = lax.axis_index("tensor")
    seqs, span, width = tokens.shape
    routed = routed_index.shape[1]
    per = seqs // lax.axis_size("tensor")
    local = query_weight.shape[1]
    depth = query_weight.shape[0]
    rows = per * routed

    up_down = lax.all_gather(
        jnp.concatenate([up_weight, down_weight.T], axis=0), "fsdp", axis=0, tiled=True
    ).reshape(fsdp, 2 * depth, -1)
    attn_piece = jnp.concatenate(
        [query_weight, key_weight, value_weight, output_weight.T], axis=1
    )
    small = jnp.stack([router_weight, attn_gain, mlp_gain])
    if fsdp == 8:
        vec = jnp.zeros((8, width), BF16)
        vec = lax.dynamic_update_slice(vec, small, (0, me_f * depth))
        for mask in (1, 2, 4):
            vec = vec + swap(vec, "fsdp", mask)
    else:
        vec = lax.all_gather(small, "fsdp", axis=1, tiled=True)
        vec = jnp.concatenate([vec, jnp.zeros((5, width), BF16)], axis=0)
    vec = vec.astype(F32)
    attn_w = fsdp_gather(attn_piece)

    place = routed_index - me_t * span
    positions = jnp.arange(span, dtype=jnp.int32)
    onehot = (place[:, :, None] == positions[None, None, :]).astype(BF16)
    onehot_t = (place[:, None, :] == positions[None, :, None]).astype(BF16)
    blocks = routed_index // BLOCK
    bias = jnp.where(blocks[:, None, :] <= blocks[:, :, None], 0.0, NEG).astype(F32)
    order = jnp.stack([(me_t ^ m) * per + j for m in range(4) for j in range(per)])
    order_keep = jnp.concatenate([order[0:per], order[2 * per : 3 * per]])
    order_send = jnp.concatenate([order[per : 2 * per], order[3 * per :]])
    order_near = order[: 2 * per]
    order_far = order[2 * per :]

    def take(values):
        got = swap(pick_rows(values, onehot, order_send), "tensor", 1)
        keep = pick_rows(values, onehot, order_keep)
        far = swap(keep[rows:] + got[rows:], "tensor", 2)
        return keep, got, far

    row_shape = ((rows, width), BF16, "r")
    f32_shape = ((rows, width), F32, "r")
    gate_shape = ((rows, 128), F32, "r")
    vec_shape = ((8, width), F32, "w")

    def row_step(body, name, ins, outs):
        return row_call(body, name, ins, outs, rows, width)

    def r(*arrays):
        return [(a, "r") for a in arrays]

    tok = take(tokens)
    own_rows, normed, gate = row_step(
        first_norm_body, "first_norm", r(*tok) + [(vec, "w")], [row_shape, row_shape, gate_shape]
    )
    n0, n1, n2, n3 = gather_rows(normed)
    cot, mlp_grad = row_step(
        cot_body, "cot_rows", r(*take(cotangent), gate), [row_shape, row_shape]
    )
    g0, g1, g2, g3 = gather_rows(mlp_grad)

    qkv_far, ctx_far, p2, p3 = attn_fwd(n2, n3, attn_w, bias, order_far, local)
    attn_x = scatter_far(p2, p3)
    qkv_near, ctx_near, p0, p1 = attn_fwd(n0, n1, attn_w, bias, order_near, local)
    attn_c = swap(p1, "tensor", 1)
    attn, second = row_step(
        second_norm_body,
        "second_norm",
        r(own_rows, p0, attn_c, attn_x) + [(vec, "w")],
        [f32_shape, row_shape],
    )
    s0, s1, s2, s3 = gather_rows(second)

    act_far, ug_far, d2, d3, m2, m3 = mlp_both(s2, s3, g2, g3, up_down)
    second_x = scatter_far(d2, d3)
    act_near, ug_near, d0, d1, m0, m1 = mlp_both(s0, s1, g0, g1, up_down)
    second_c = swap(d1, "tensor", 1)
    attn_grad, hidden_grad, second_part = row_step(
        second_back_body,
        "second_back",
        r(own_rows, attn, cot, gate, d0, second_c, second_x) + [(vec, "w")],
        [row_shape, f32_shape, vec_shape],
    )
    a0, a1, a2, a3 = gather_rows(attn_grad)
    mlp_x = scatter_far(m2, m3)
    mlp_c = swap(m1, "tensor", 1)
    out_rows, gate_grad, router_part = row_step(
        out_body,
        "out_rows",
        r(own_rows, attn, cot, gate, m0, mlp_c, mlp_x),
        [row_shape, gate_shape, vec_shape],
    )
    mixed = place_rows(tokens, onehot_t, gather_rows(out_rows), order)

    shifts = (1, 3, 2, 0)
    if fsdp == 8:
        zi = me_f // 2
        info = jnp.stack([(zi + o) % 4 for o in shifts] + [me_f % 2])
        sends, keeps = grad_blocks(
            [
                ((s0, s1, s2, s3), (ug_near, ug_far)),
                ((g0, g1, g2, g3), (act_near, act_far)),
            ],
            info,
            2 * depth,
            up_weight.shape[1],
            4,
            "mlp_grads",
        )
        mlp_sum = fsdp_finish(sends, keeps, shifts)
    else:

        def dense(xs, ys):
            return t_mm(jnp.concatenate(xs, axis=0), jnp.concatenate(ys, axis=0))

        def reduced(x):
            return lax.psum_scatter(x, "fsdp", scatter_dimension=0, tiled=True)

        mlp_sum = jnp.concatenate(
            [
                reduced(dense((s0, s1, s2, s3), (ug_near, ug_far))),
                reduced(dense((g0, g1, g2, g3), (act_near, act_far))),
            ],
            axis=0,
        )

    dqkv_far, f2, f3 = attn_bwd(a2, a3, attn_w, qkv_far, bias, order_far, local)
    first_x = scatter_far(f2, f3)
    dqkv_near, f0, f1 = attn_bwd(a0, a1, attn_w, qkv_near, bias, order_near, local)
    first_c = swap(f1, "tensor", 1)
    half = rows // 2
    grad_rows, vec_part = pl.pallas_call(
        first_back_body,
        grid=(2,),
        in_specs=[
            pl.BlockSpec((half, width), lambda i: (i, 0)),
            pl.BlockSpec((half, width), lambda i: (i, 0)),
            pl.BlockSpec((half, 128), lambda i: (i, 0)),
        ]
        + [pl.BlockSpec((half, width), lambda i: (i, 0))] * 4
        + [pl.BlockSpec((8, width), lambda i: (0, 0))] * 3,
        out_specs=[
            pl.BlockSpec((half, width), lambda i: (i, 0)),
            pl.BlockSpec((8, width), lambda i: (0, 0)),
        ],
        out_shape=[shape((rows, width), BF16), shape((8, width), F32)],
        scratch_shapes=[pltpu.VMEM((8, width), F32)],
        compiler_params=PARAMS,
        cost_estimate=cost(30 * rows * width, 20 * rows * width),
        name="first_back",
    )(own_rows, cot, gate_grad, hidden_grad, f0, first_c, first_x, vec, router_part, second_part)
    token_grad = place_rows(cotangent, onehot_t, gather_rows(grad_rows), order)

    if fsdp == 8:
        sends, keeps = grad_blocks(
            [
                ((n0, n1, n2, n3), (dqkv_near, dqkv_far)),
                ((a0, a1, a2, a3), (ctx_near, ctx_far)),
            ],
            info,
            depth,
            4 * local,
            4,
            "attn_grads",
        )
        attn_sum = fsdp_finish(sends, keeps, shifts)
        vec_sum = vec_part
        for axis, mask in (("tensor", 1), ("tensor", 2), ("fsdp", 1)):
            vec_sum = vec_sum + swap(vec_sum, axis, mask)
        around = [lax.ppermute(vec_sum, "fsdp", z_perm(fsdp, 2, o)) for o in (1, 3, 2)]
        vec_sum = vec_sum + around[0] + around[1] + around[2]
    else:
        attn_sum = jnp.concatenate(
            [
                reduced(dense((n0, n1, n2, n3), (dqkv_near, dqkv_far))),
                reduced(dense((a0, a1, a2, a3), (ctx_near, ctx_far))),
            ],
            axis=1,
        )
        vec_sum = lax.psum(vec_part, ("fsdp", "tensor"))
    vec_own = lax.dynamic_slice(vec_sum, (0, me_f * depth), (3, depth))

    return (
        mixed,
        token_grad,
        attn_sum[:, 0:local],
        attn_sum[:, local : 2 * local],
        attn_sum[:, 2 * local : 3 * local],
        attn_sum[:, 3 * local :].T,
        mlp_sum[0:depth],
        mlp_sum[depth:].T,
        vec_own[0],
        vec_own[1],
        vec_own[2],
    )


def solution(mesh):
    in_specs = (
        P("fsdp", "tensor", None),
        P("fsdp", "tensor", None),
        P("fsdp", None),
        P("fsdp", "tensor"),
        P("fsdp", "tensor"),
        P("fsdp", "tensor"),
        P("tensor", "fsdp"),
        P("fsdp", "tensor"),
        P("tensor", "fsdp"),
        P("fsdp"),
        P("fsdp"),
        P("fsdp"),
    )
    out_specs = (
        P("fsdp", "tensor", None),
        P("fsdp", "tensor", None),
        P("fsdp", "tensor"),
        P("fsdp", "tensor"),
        P("fsdp", "tensor"),
        P("tensor", "fsdp"),
        P("fsdp", "tensor"),
        P("tensor", "fsdp"),
        P("fsdp"),
        P("fsdp"),
        P("fsdp"),
    )
    return jax.shard_map(shards, mesh=mesh, in_specs=in_specs, out_specs=out_specs, check_vma=False)
```

time: 1450 us -> 379 us (0.26)
  waiting for transfers between devices: 867 us -> 147 us
  blocking collectives: 226 us -> 0 us
  local copies, waits for them, and re-layouts: 220 us -> 34.9 us
  Pallas kernels: 0 us -> 108 us
  matrix products: 74.1 us -> 0 us
  starting transfers between devices: 1.78 us -> 57.2 us
  other arithmetic: 34.6 us -> 15.3 us
    reduce_scatter x6 -> x0, waiting for transfers between devices: 385 us -> none  [the longest x1 92 us: shards(): lax.psum_scatter(down_grad, 'fsdp', scatter_dimension=1, tiled=True)]
    unnamed x24 -> x1, waiting for transfers between devices: 332 us -> 0.02 us
    all_gather x8 -> x0, blocking collectives: 188 us -> none  [the longest x1 33.4 us: shards(): lax.all_gather(value_weight, 'fsdp', axis=0, tiled=True)]
    all_gather x8 -> x1, waiting for transfers between devices: 150 us -> 0.01 us  [shards(): lax.all_gather(jnp.concatenate([up_weight, down_weight.T], axis=0), 'fsdp...]
    ppermute x0 -> x64, waiting for transfers between devices: none -> 147 us  [the longest x52 79.7 us: swap(): return lax.ppermute(x, axis, [(i, i ^ mask) for i in range(size)])]
    pallas_call x0 -> x21, Pallas kernels: none -> 108 us  [the longest x2 25.5 us: grad_blocks(): pl.pallas_call(functools.partial(grads_kernel, jobs=[(len(xs), len(ys)) f...]
    gather x2 -> x0, local copies, waits for them, and re-layouts: 83.3 us -> none  [pick_rows(): jnp.take_along_axis(values, safe_pos[:, :, None], axis=1)]
    dot_general x25 -> x0, matrix products: 74.1 us -> none  [the longest x1 8.09 us: shards(): jnp.einsum('rd,fd->rf', mlp_grad_all, down_back, preferred_element_type=j...]
  transfers between devices with their start and end apart: 19 -> 65, of which waited for: 16 -> 22; matrix products, arithmetic and copies ran while one was open for 6% -> 7% of each run, Pallas kernels for 0% -> 26%
where the time goes in v1:
time: 379 us; the launch traced here: 377 us
  waiting for transfers between devices  147 us (39%)
  Pallas kernels  108 us (28%)
  starting transfers between devices  57.2 us (15%)
  local copies, waits for them, and re-layouts  34.9 us (9%)
  other arithmetic  15.3 us (4%)
  between operations  14.8 us (4%)
    ppermute x52, waiting for transfers between devices, swap(): return lax.ppermute(x, axis, [(i, i ^ mask) for i in range(size)])  79.7 us
    ppermute x52, starting transfers between devices, swap(): return lax.ppermute(x, axis, [(i, i ^ mask) for i in range(size)])  39.1 us
    ppermute x3, waiting for transfers between devices, fsdp_gather(): lax.ppermute(piece, 'fsdp', z_perm(size, 2, o))  32.8 us
    ppermute x6, waiting for transfers between devices, fsdp_finish(): lax.ppermute(both.astype(BF16), 'fsdp', z_perm(size, 2, 4 - o))  31 us
    pallas_call x2, Pallas kernels, grad_blocks(): pl.pallas_call(functools.partial(grads_kernel, jobs=[(len(xs), len(ys)) f...  25.5 us
    unnamed x120, local copies, waits for them, and re-layouts  25.4 us
    pallas_call x2, Pallas kernels, mlp_both(): pl.pallas_call(mlp_kernel, in_specs=[VMEM_SPEC] * 5, out_specs=[VMEM_SPEC...  22.2 us
    pallas_call x2, Pallas kernels, place_rows(): pl.pallas_call(place_kernel, grid_spec=pltpu.PrefetchScalarGridSpec(num_s...  16.1 us
  transfers between devices with their start and end apart: 65, of which 22 were waited for; matrix products, arithmetic and copies ran while one was open for 7% of the time, Pallas kernels for 26%

profile of v1, /device:TPU:0, one launch (start us, length us, event | category | flops | bytes accessed | tf_op | source)
XLA Modules:
  0.0 377.4 jit_solution(13059778092865797173)
XLA Ops:
  13.4 2.7 pick_rows.5
  32.3 2.8 collective-permute-start.4
  43.3 4.8 %collective-permute-start.6 = (bf16[128,1024]{1,0:T(8,128)(2,1)S(1)}, bf16[128,1024]{1,0:T(8,128)(2,1)S(1)}, u32[]{:S(2)}, u32[]{:S(2)}) collective-permute-start(bf16[128,1024]{1,0:T(8,128)(2,1)S(1)} %pad_maximum_fusion.1.refs_0_), channel_id=1, source_target_pairs={{8,0},{12,4},{16,8},{20,12},{24,16},{28,20},{0,24},{4,28},{9,1},{1... | collective-permute-start | bytes 786440 | tf_op jit(solution)/shard_map/ppermute | solution.py:518
  50.3 2.7 pick_rows.7
  55.3 14.3 %collective-permute-done.7.refs_2_ = bf16[128,1024]{1,0:T(8,128)(2,1)} collective-permute-done((bf16[128,1024]{1,0:T(8,128)(2,1)S(1)}, bf16[128,1024]{1,0:T(8,128)(2,1)}, u32[]{:S(2)}, u32[]{:S(2)}) %collective-permute-start.7) | collective-permute-done | bytes 262176 | tf_op jit(solution)/shard_map/ppermute | solution.py:518
  71.4 18.5 %collective-permute-done.8.refs_3_ = bf16[128,1024]{1,0:T(8,128)(2,1)} collective-permute-done((bf16[128,1024]{1,0:T(8,128)(2,1)S(1)}, bf16[128,1024]{1,0:T(8,128)(2,1)}, u32[]{:S(2)}, u32[]{:S(2)}) %collective-permute-start.8) | collective-permute-done | bytes 262176 | tf_op jit(solution)/shard_map/ppermute | solution.py:518
  93.0 6.3 %collective-permute-done.11.refs_6_ = bf16[128,1024]{1,0:T(8,128)(2,1)} collective-permute-done((bf16[128,1024]{1,0:T(8,128)(2,1)}, bf16[128,1024]{1,0:T(8,128)(2,1)}, u32[]{:S(2)}, u32[]{:S(2)}) %collective-permute-start.11) | collective-permute-done | bytes 262176 | tf_op jit(solution)/shard_map/ppermute | solution.py:492
  99.4 4.8 %collective-permute-done.12.refs_7_ = bf16[128,1024]{1,0:T(8,128)(2,1)} collective-permute-done((bf16[128,1024]{1,0:T(8,128)(2,1)}, bf16[128,1024]{1,0:T(8,128)(2,1)}, u32[]{:S(2)}, u32[]{:S(2)}) %collective-permute-start.12) | collective-permute-done | bytes 262176 | tf_op jit(solution)/shard_map/ppermute | solution.py:492
  106.6 6.9 %attn_fwd.3 = (bf16[512,768]{1,0:T(8,128)(2,1)S(1)}, bf16[512,256]{1,0:T(8,128)(2,1)S(1)}, bf16[256,1024]{1,0:T(8,128)(2,1)S(1)}, bf16[256,1024]{1,0:T(8,128)(2,1)S(1)}) custom-call(s32[4]{0:T(128)S(1)} %add_add_fusion.1.order, bf16[256,1024]{1,0:T(8,128)(2,1)} %collective-permute-done.14.xa.refs_2_, bf16[256,1024]{1,0:T(8,128)(2,1)} %collective-permute-done.15.xb.refs_3_, ...), custom_call_target="tpu_custom_call" | custom-call | flops 2147483648 | bytes 4194304 | tf_op jit(solution)/shard_map/attn_fwd/pallas_call | solution.py:316
  118.9 6.0 %attn_fwd.2 = (bf16[512,768]{1,0:T(8,128)(2,1)S(1)}, bf16[512,256]{1,0:T(8,128)(2,1)S(1)}, bf16[256,1024]{1,0:T(8,128)(2,1)S(1)}, bf16[256,1024]{1,0:T(8,128)(2,1)S(1)}) custom-call(s32[4]{0:T(128)S(1)} %pad_add_fusion.2.order, bf16[256,1024]{1,0:T(8,128)(2,1)} %get-tuple-element.69.xa.refs_0_, bf16[256,1024]{1,0:T(8,128)(2,1)S(1)} %collective-permute-done.5.xb.refs_1_, ...), custom_call_target="tpu_custom_call" | custom-call | flops 2147483648 | bytes 4194304 | tf_op jit(solution)/shard_map/attn_fwd/pallas_call | solution.py:316
  125.8 6.3 %collective-permute-done.19.c = bf16[256,1024]{1,0:T(8,128)(2,1)S(1)} collective-permute-done((bf16[256,1024]{1,0:T(8,128)(2,1)S(1)}, bf16[256,1024]{1,0:T(8,128)(2,1)S(1)}, u32[]{:S(2)}, u32[]{:S(2)}) %collective-permute-start.19) | collective-permute-done | bytes 524320 | tf_op jit(solution)/shard_map/ppermute | solution.py:492
  134.6 8.7 %collective-permute-done.17.c = bf16[256,1024]{1,0:T(8,128)(2,1)S(1)} collective-permute-done((bf16[256,1024]{1,0:T(8,128)(2,1)S(1)}, bf16[256,1024]{1,0:T(8,128)(2,1)S(1)}, u32[]{:S(2)}, u32[]{:S(2)}) %collective-permute-start.17) | collective-permute-done | bytes 524320 | tf_op jit(solution)/shard_map/ppermute | solution.py:492
  146.1 8.5 %collective-permute-done.25.ga.refs_8_ = bf16[256,1024]{1,0:T(8,128)(2,1)S(1)} collective-permute-done((bf16[256,1024]{1,0:T(8,128)(2,1)}, bf16[256,1024]{1,0:T(8,128)(2,1)S(1)}, u32[]{:S(2)}, u32[]{:S(2)}) %collective-permute-start.25) | collective-permute-done | bytes 524320 | tf_op jit(solution)/shard_map/ppermute | solution.py:492
  154.6 10.4 %collective-permute-done.23.na.refs_2_ = bf16[256,1024]{1,0:T(8,128)(2,1)S(1)} collective-permute-done((bf16[256,1024]{1,0:T(8,128)(2,1)}, bf16[256,1024]{1,0:T(8,128)(2,1)S(1)}, u32[]{:S(2)}, u32[]{:S(2)}) %collective-permute-start.23) | collective-permute-done | bytes 524320 | tf_op jit(solution)/shard_map/ppermute | solution.py:492
  165.6 6.4 %copy.25 = bf16[2048,1024]{1,0:T(8,128)(2,1)} copy(bf16[2048,1024]{0,1:T(8,128)(2,1)} %all-gather.2.cloned.1.call-done) | data formatting | bytes 8388608 | tf_op jit(solution)/shard_map/all_gather | solution.py:565
  174.1 11.0 %mlp.3 = (bf16[512,1024]{1,0:T(8,128)(2,1)S(1)}, bf16[512,1024]{1,0:T(8,128)(2,1)}, bf16[256,1024]{1,0:T(8,128)(2,1)S(1)}, bf16[256,1024]{1,0:T(8,128)(2,1)}, bf...) custom-call(bf16[256,1024]{1,0:T(8,128)(2,1)S(1)} %copy-done.28, ...), custom_call_target="tpu_custom_call" | custom-call | flops 4294967296 | bytes 10485760 | tf_op jit(solution)/shard_map/mlp/pallas_call | solution.py:424
  186.7 11.2 %mlp.2 = (bf16[512,1024]{1,0:T(8,128)(2,1)S(1)}, bf16[512,1024]{1,0:T(8,128)(2,1)}, bf16[256,1024]{1,0:T(8,128)(2,1)S(1)}, bf16[256,1024]{1,0:T(8,128)(2,1)S(1)}...) custom-call(bf16[256,1024]{1,0:T(8,128)(2,1)} %get-tuple-element.77.na.refs_0_, ...), custom_call_target="tpu_custom_call" | custom-call | flops 4294967296 | bytes 10485760 | tf_op jit(solution)/shard_map/mlp/pallas_call | solution.py:424
  202.0 16.8 %mlp_grads.1 = (bf16[256,1024]{1,0:T(8,128)(2,1)}, bf16[256,1024]{1,0:T(8,128)(2,1)S(1)}, bf16[256,1024]{1,0:T(8,128)(2,1)S(1)}, bf16[256,1024]{1,0:T(8,128)(2,1...) custom-call(s32[5]{0:T(128)S(1)} %stack.117.info, ...), custom_call_target="tpu_custom_call" | custom-call | flops 4294967296 | bytes 6291456 | tf_op jit(solution)/shard_map/mlp_grads/pallas_call | solution.py:475
  224.6 9.5 %collective-permute-done.52 = bf16[256,1024]{1,0:T(8,128)(2,1)} collective-permute-done((bf16[256,1024]{1,0:T(8,128)(2,1)}, bf16[256,1024]{1,0:T(8,128)(2,1)}, u32[]{:S(2)}, u32[]{:S(2)}) %collective-permute-start.52) | collective-permute-done | bytes 524320 | tf_op jit(solution)/shard_map/ppermute | solution.py:492
  238.9 6.3 %collective-permute-done.54 = bf16[256,1024]{1,0:T(8,128)(2,1)S(1)} collective-permute-done((bf16[256,1024]{1,0:T(8,128)(2,1)}, bf16[256,1024]{1,0:T(8,128)(2,1)S(1)}, u32[]{:S(2)}, u32[]{:S(2)}) %collective-permute-start.54) | collective-permute-done | bytes 524320 | tf_op jit(solution)/shard_map/ppermute | solution.py:492
  247.1 7.3 %attn_bwd.3 = (bf16[512,768]{1,0:T(8,128)(2,1)S(1)}, bf16[256,1024]{1,0:T(8,128)(2,1)S(1)}, bf16[256,1024]{1,0:T(8,128)(2,1)S(1)}) custom-call(s32[4]{0:T(128)S(1)} %add_add_fusion.1.order, bf16[256,1024]{1,0:T(8,128)(2,1)} %collective-permute-done.37.ga.refs_8_, bf16[256,1024]{1,0:T(8,128)(2,1)S(1)} %collective-permute-done.38.gb.refs_9_, ...), custom_call_target="tpu_custom_call" | custom-call | flops 3221225472 | bytes 4194304 | tf_op jit(solution)/shard_map/attn_bwd/pallas_call | solution.py:369
  256.6 3.2 collective-permute-start.53
  259.8 3.1 collective-permute-start.55
  264.2 7.0 %attn_bwd.2 = (bf16[512,768]{1,0:T(8,128)(2,1)S(1)}, bf16[256,1024]{1,0:T(8,128)(2,1)S(1)}, bf16[256,1024]{1,0:T(8,128)(2,1)S(1)}) custom-call(s32[4]{0:T(128)S(1)} %pad_add_fusion.2.order, bf16[256,1024]{1,0:T(8,128)(2,1)} %get-tuple-element.90.ga.refs_6_, bf16[256,1024]{1,0:T(8,128)(2,1)S(1)} %collective-permute-done.35.gb.refs_7_, ...), custom_call_target="tpu_custom_call" | custom-call | flops 3221225472 | bytes 4194304 | tf_op jit(solution)/shard_map/attn_bwd/pallas_call | solution.py:369
  272.2 8.7 %attn_grads.1 = (bf16[128,1024]{1,0:T(8,128)(2,1)S(1)}, bf16[128,1024]{1,0:T(8,128)(2,1)S(1)}, bf16[128,1024]{1,0:T(8,128)(2,1)S(1)}, bf16[128,1024]{1,0:T(8,128...) custom-call(s32[5]{0:T(128)S(1)} %stack.117.info, ...), custom_call_target="tpu_custom_call" | custom-call | flops 2147483648 | bytes 3145728 | tf_op jit(solution)/shard_map/attn_grads/pallas_call | solution.py:475
  285.3 23.8 %collective-permute-done.57 = bf16[256,1024]{1,0:T(8,128)(2,1)} collective-permute-done((bf16[256,1024]{1,0:T(8,128)(2,1)S(1)}, bf16[256,1024]{1,0:T(8,128)(2,1)}, u32[]{:S(2)}, u32[]{:S(2)}) %collective-permute-start.57) | collective-permute-done | bytes 524320 | tf_op jit(solution)/shard_map/ppermute | solution.py:535
  314.0 9.0 %collective-permute-done.40.c = bf16[256,1024]{1,0:T(8,128)(2,1)S(1)} collective-permute-done((bf16[256,1024]{1,0:T(8,128)(2,1)S(1)}, bf16[256,1024]{1,0:T(8,128)(2,1)S(1)}, u32[]{:S(2)}, u32[]{:S(2)}) %collective-permute-start.40) | collective-permute-done | bytes 524320 | tf_op jit(solution)/shard_map/ppermute | solution.py:492
  328.8 3.8 %collective-permute-start.48 = (bf16[128,1024]{1,0:T(8,128)(2,1)}, bf16[128,1024]{1,0:T(8,128)(2,1)}, u32[]{:S(2)}, u32[]{:S(2)}) collective-permute-start(bf16[128,1024]{1,0:T(8,128)(2,1)} %add_convert_fusion.8), channel_id=1, source_target_pairs={{8,0},{12,4},{16,8},{20,12},{24,16},{28,20},{0,24},{4,28},{9,1},{1... | collective-permute-start | bytes 786440 | tf_op jit(solution)/shard_map/ppermute | solution.py:535
  337.8 8.1 %place_rows.2 = bf16[8,256,1024]{2,1,0:T(8,128)(2,1)} custom-call(s32[8]{0:T(128)S(1)} %stack.96.order, bf16[8,256,128]{2,1,0:T(8,128)(2,1)S(1)} %fusion.onehot_t, bf16[256,1024]{1,0:T(8,128)(2,1)S(1)} %get-tuple-element.83.r0, bf16[256,1024]{1,0:T(8,128)(2,1)S(1)} %copy-done.8, bf16[256,1024]{1,0:T(8,128)(2,1)S(1)} %collective-permute-done.30.r2, ...), custom_call_target="tpu_custom_call" | custom-call | flops 536870912 | bytes 8388608 | tf_op jit(solution)/shard_map/place_rows/pallas_call | solution.py:103
  347.7 5.2 %collective-permute-done.50 = bf16[128,1024]{1,0:T(8,128)(2,1)} collective-permute-done((bf16[128,1024]{1,0:T(8,128)(2,1)}, bf16[128,1024]{1,0:T(8,128)(2,1)}, u32[]{:S(2)}, u32[]{:S(2)}) %collective-permute-start.50) | collective-permute-done | bytes 262176 | tf_op jit(solution)/shard_map/ppermute | solution.py:535
  358.3 2.6 collective-permute-done.62
  362.4 8.1 %place_rows.3 = bf16[8,256,1024]{2,1,0:T(8,128)(2,1)} custom-call(s32[8]{0:T(128)S(1)} %stack.96.order, bf16[8,256,128]{2,1,0:T(8,128)(2,1)S(1)} %fusion.onehot_t, bf16[256,1024]{1,0:T(8,128)(2,1)S(1)} %get-tuple-element.99.r0, bf16[256,1024]{1,0:T(8,128)(2,1)S(1)} %collective-permute-done.41.r1, bf16[256,1024]{1,0:T(8,128)(2,1)S(1)} %collective-permute-done.42.r2, ...), custom_call_target="tpu_custom_call" | custom-call | flops 536870912 | bytes 8388608 | tf_op jit(solution)/shard_map/place_rows/pallas_call | solution.py:103
  (282 shorter events, 107.6 us)
Async XLA Ops:
  7.2 158.4 %all-gather.2.cloned.1.call-start = ((), (), s32[]{:S(2)}) async-start(), calls=%async_computation | async-start | bytes 4718592 | tf_op jit(solution)/shard_map/all_gather | solution.py:565
  53.0 64.2 %collective-permute-start.18 = (bf16[512,1024]{1,0:T(8,128)(2,1)}, bf16[512,1024]{1,0:T(8,128)(2,1)S(1)}, u32[]{:S(2)}, u32[]{:S(2)}) collective-permute-start(bf16[512,1024]{1,0:T(8,128)(2,1)} %pick_rows.7), channel_id=1, source_target_pairs={{0,1},{1,0},{2,3},{3,2},{4,5},{5,4},{6,7},{7,6},{8,9},{9,8},{10,11... | collective-permute-start | bytes 3145736 | tf_op jit(solution)/shard_map/ppermute | solution.py:492
  53.0 36.9 %collective-permute-start.8 = (bf16[128,1024]{1,0:T(8,128)(2,1)S(1)}, bf16[128,1024]{1,0:T(8,128)(2,1)}, u32[]{:S(2)}, u32[]{:S(2)}) collective-permute-start(bf16[128,1024]{1,0:T(8,128)(2,1)S(1)} %pad_maximum_fusion.1.refs_0_), channel_id=1, source_target_pairs={{16,0},{20,4},{24,8},{28,12},{0,16},{4,20},{8,24},{12,28},{17,1},{... | collective-permute-start | bytes 786440 | tf_op jit(solution)/shard_map/ppermute | solution.py:518
  53.6 37.9 %collective-permute-start.9 = (bf16[128,1024]{1,0:T(8,128)(2,1)S(1)}, bf16[128,1024]{1,0:T(8,128)(2,1)S(1)}, u32[]{:S(2)}, u32[]{:S(2)}) collective-permute-start(bf16[128,1024]{1,0:T(8,128)(2,1)S(1)} %pad_maximum_fusion.1.refs_0_), channel_id=1, source_target_pairs={{0,4},{4,0},{8,12},{12,8},{16,20},{20,16},{24,28},{28,24},{1,5},{5... | collective-permute-start | bytes 786440 | tf_op jit(solution)/shard_map/ppermute | solution.py:492
  55.3 51.3 %collective-permute-start.15 = (bf16[256,1024]{1,0:T(8,128)(2,1)}, bf16[256,1024]{1,0:T(8,128)(2,1)}, u32[]{:S(2)}, u32[]{:S(2)}) collective-permute-start(bf16[256,1024]{1,0:T(8,128)(2,1)} %collective-permute-done.14.xa.refs_2_), channel_id=1, source_target_pairs={{0,1},{1,0},{2,3},{3,2},{4,5},{5,4},{6,7},{7,6},{8,9},{9,8},{10,11... | collective-permute-start | bytes 1572872 | tf_op jit(solution)/shard_map/ppermute | solution.py:492
  69.6 23.4 %collective-permute-start.10 = (bf16[128,1024]{1,0:T(8,128)(2,1)S(1)}, bf16[128,1024]{1,0:T(8,128)(2,1)}, u32[]{:S(2)}, u32[]{:S(2)}) collective-permute-start(bf16[128,1024]{1,0:T(8,128)(2,1)S(1)} %collective-permute-done.6.refs_1_), channel_id=1, source_target_pairs={{0,4},{4,0},{8,12},{12,8},{16,20},{20,16},{24,28},{28,24},{1,5},{5... | collective-permute-start | bytes 786440 | tf_op jit(solution)/shard_map/ppermute | solution.py:492
  125.3 18.1 %collective-permute-start.17 = (bf16[256,1024]{1,0:T(8,128)(2,1)S(1)}, bf16[256,1024]{1,0:T(8,128)(2,1)S(1)}, u32[]{:S(2)}, u32[]{:S(2)}) collective-permute-start(bf16[256,1024]{1,0:T(8,128)(2,1)S(1)} %add_convert_fusion.6), channel_id=1, source_target_pairs={{0,2},{1,3},{2,0},{3,1},{4,6},{5,7},{6,4},{7,5},{8,10},{9,11},{10,... | collective-permute-start | bytes 1572872 | tf_op jit(solution)/shard_map/ppermute | solution.py:492
  133.1 21.5 %collective-permute-start.25 = (bf16[256,1024]{1,0:T(8,128)(2,1)}, bf16[256,1024]{1,0:T(8,128)(2,1)S(1)}, u32[]{:S(2)}, u32[]{:S(2)}) collective-permute-start(bf16[256,1024]{1,0:T(8,128)(2,1)} %get-tuple-element.78.ga.refs_6_), channel_id=1, source_target_pairs={{0,2},{1,3},{2,0},{3,1},{4,6},{5,7},{6,4},{7,5},{8,10},{9,11},{10,... | collective-permute-start | bytes 1572872 | tf_op jit(solution)/shard_map/ppermute | solution.py:492
  144.6 20.4 %collective-permute-start.23 = (bf16[256,1024]{1,0:T(8,128)(2,1)}, bf16[256,1024]{1,0:T(8,128)(2,1)S(1)}, u32[]{:S(2)}, u32[]{:S(2)}) collective-permute-start(bf16[256,1024]{1,0:T(8,128)(2,1)} %get-tuple-element.77.na.refs_0_), channel_id=1, source_target_pairs={{0,2},{1,3},{2,0},{3,1},{4,6},{5,7},{6,4},{7,5},{8,10},{9,11},{10,... | collective-permute-start | bytes 1572872 | tf_op jit(solution)/shard_map/ppermute | solution.py:492
  165.0 21.6 %collective-permute-start.21 = (bf16[256,1024]{1,0:T(8,128)(2,1)}, bf16[256,1024]{1,0:T(8,128)(2,1)}, u32[]{:S(2)}, u32[]{:S(2)}) collective-permute-start(bf16[256,1024]{1,0:T(8,128)(2,1)} %get-tuple-element.78.ga.refs_6_), channel_id=1, source_target_pairs={{0,1},{1,0},{2,3},{3,2},{4,5},{5,4},{6,7},{7,6},{8,9},{9,8},{10,11... | collective-permute-start | bytes 1572872 | tf_op jit(solution)/shard_map/ppermute | solution.py:492
  165.5 21.1 %collective-permute-start.20 = (bf16[256,1024]{1,0:T(8,128)(2,1)}, bf16[256,1024]{1,0:T(8,128)(2,1)}, u32[]{:S(2)}, u32[]{:S(2)}) collective-permute-start(bf16[256,1024]{1,0:T(8,128)(2,1)} %get-tuple-element.77.na.refs_0_), channel_id=1, source_target_pairs={{0,1},{1,0},{2,3},{3,2},{4,5},{5,4},{6,7},{7,6},{8,9},{9,8},{10,11... | collective-permute-start | bytes 1572872 | tf_op jit(solution)/shard_map/ppermute | solution.py:492
  198.8 21.4 %collective-permute-start.32 = (bf16[256,1024]{1,0:T(8,128)(2,1)S(1)}, bf16[256,1024]{1,0:T(8,128)(2,1)S(1)}, u32[]{:S(2)}, u32[]{:S(2)}) collective-permute-start(bf16[256,1024]{1,0:T(8,128)(2,1)S(1)} %get-tuple-element.86), channel_id=1, source_target_pairs={{0,1},{1,0},{2,3},{3,2},{4,5},{5,4},{6,7},{7,6},{8,9},{9,8},{10,11... | collective-permute-start | bytes 1572872 | tf_op jit(solution)/shard_map/ppermute | solution.py:492
  200.4 19.9 %collective-permute-start.34 = (bf16[256,1024]{1,0:T(8,128)(2,1)S(1)}, bf16[256,1024]{1,0:T(8,128)(2,1)S(1)}, u32[]{:S(2)}, u32[]{:S(2)}) collective-permute-start(bf16[256,1024]{1,0:T(8,128)(2,1)S(1)} %add_convert_fusion.4), channel_id=1, source_target_pairs={{0,2},{1,3},{2,0},{3,1},{4,6},{5,7},{6,4},{7,5},{8,10},{9,11},{10,... | collective-permute-start | bytes 1572872 | tf_op jit(solution)/shard_map/ppermute | solution.py:492
  223.8 32.8 %collective-permute-start.22 = (bf16[256,1024]{1,0:T(8,128)(2,1)}, bf16[256,1024]{1,0:T(8,128)(2,1)S(1)}, u32[]{:S(2)}, u32[]{:S(2)}) collective-permute-start(bf16[256,1024]{1,0:T(8,128)(2,1)} %copy-done.31), channel_id=1, source_target_pairs={{0,1},{1,0},{2,3},{3,2},{4,5},{5,4},{6,7},{7,6},{8,9},{9,8},{10,11... | collective-permute-start | bytes 1572872 | tf_op jit(solution)/shard_map/ppermute | solution.py:492
  224.1 21.1 %collective-permute-start.54 = (bf16[256,1024]{1,0:T(8,128)(2,1)}, bf16[256,1024]{1,0:T(8,128)(2,1)S(1)}, u32[]{:S(2)}, u32[]{:S(2)}) collective-permute-start(bf16[256,1024]{1,0:T(8,128)(2,1)} %copy-done.34), channel_id=1, source_target_pairs={{0,4},{4,0},{8,12},{12,8},{16,20},{20,16},{24,28},{28,24},{1,5},{5... | collective-permute-start | bytes 1572872 | tf_op jit(solution)/shard_map/ppermute | solution.py:492
  234.1 22.4 %collective-permute-start.56 = (bf16[256,1024]{1,0:T(8,128)(2,1)}, bf16[256,1024]{1,0:T(8,128)(2,1)S(1)}, u32[]{:S(2)}, u32[]{:S(2)}) collective-permute-start(bf16[256,1024]{1,0:T(8,128)(2,1)} %copy-done.32), channel_id=1, source_target_pairs={{0,4},{4,0},{8,12},{12,8},{16,20},{20,16},{24,28},{28,24},{1,5},{5... | collective-permute-start | bytes 1572872 | tf_op jit(solution)/shard_map/ppermute | solution.py:492
  236.9 43.9 %collective-permute-start.51 = (bf16[256,1024]{1,0:T(8,128)(2,1)}, bf16[256,1024]{1,0:T(8,128)(2,1)S(1)}, u32[]{:S(2)}, u32[]{:S(2)}) collective-permute-start(bf16[256,1024]{1,0:T(8,128)(2,1)} %copy-done.30), channel_id=1, source_target_pairs={{0,4},{4,0},{8,12},{12,8},{16,20},{20,16},{24,28},{28,24},{1,5},{5... | collective-permute-start | bytes 1572872 | tf_op jit(solution)/shard_map/ppermute | solution.py:492
  245.9 17.8 %collective-permute-start.35 = (bf16[256,1024]{1,0:T(8,128)(2,1)}, bf16[256,1024]{1,0:T(8,128)(2,1)S(1)}, u32[]{:S(2)}, u32[]{:S(2)}) collective-permute-start(bf16[256,1024]{1,0:T(8,128)(2,1)} %get-tuple-element.90.ga.refs_6_), channel_id=1, source_target_pairs={{0,1},{1,0},{2,3},{3,2},{4,5},{5,4},{6,7},{7,6},{8,9},{9,8},{10,11... | collective-permute-start | bytes 1572872 | tf_op jit(solution)/shard_map/ppermute | solution.py:492
  256.4 24.7 %collective-permute-start.39 = (bf16[256,1024]{1,0:T(8,128)(2,1)S(1)}, bf16[256,1024]{1,0:T(8,128)(2,1)S(1)}, u32[]{:S(2)}, u32[]{:S(2)}) collective-permute-start(bf16[256,1024]{1,0:T(8,128)(2,1)S(1)} %get-tuple-element.96), channel_id=1, source_target_pairs={{0,1},{1,0},{2,3},{3,2},{4,5},{5,4},{6,7},{7,6},{8,9},{9,8},{10,11... | collective-permute-start | bytes 1572872 | tf_op jit(solution)/shard_map/ppermute | solution.py:492
  256.6 24.8 %collective-permute-start.53 = (bf16[256,1024]{1,0:T(8,128)(2,1)S(1)}, bf16[256,1024]{1,0:T(8,128)(2,1)S(1)}, u32[]{:S(2)}, u32[]{:S(2)}) collective-permute-start(bf16[256,1024]{1,0:T(8,128)(2,1)S(1)} %add_convert_fusion.2), channel_id=1, source_target_pairs={{24,0},{28,4},{0,8},{4,12},{8,16},{12,20},{16,24},{20,28},{25,1},{... | collective-permute-start | bytes 1572872 | tf_op jit(solution)/shard_map/ppermute | solution.py:535
  259.8 25.3 %collective-permute-start.55 = (bf16[256,1024]{1,0:T(8,128)(2,1)S(1)}, bf16[256,1024]{1,0:T(8,128)(2,1)S(1)}, u32[]{:S(2)}, u32[]{:S(2)}) collective-permute-start(bf16[256,1024]{1,0:T(8,128)(2,1)S(1)} %add_convert_fusion.1), channel_id=1, source_target_pairs={{8,0},{12,4},{16,8},{20,12},{24,16},{28,20},{0,24},{4,28},{9,1},{1... | collective-permute-start | bytes 1572872 | tf_op jit(solution)/shard_map/ppermute | solution.py:535
  263.7 45.4 %collective-permute-start.57 = (bf16[256,1024]{1,0:T(8,128)(2,1)S(1)}, bf16[256,1024]{1,0:T(8,128)(2,1)}, u32[]{:S(2)}, u32[]{:S(2)}) collective-permute-start(bf16[256,1024]{1,0:T(8,128)(2,1)S(1)} %add_convert_fusion), channel_id=1, source_target_pairs={{16,0},{20,4},{24,8},{28,12},{0,16},{4,20},{8,24},{12,28},{17,1},{... | collective-permute-start | bytes 1572872 | tf_op jit(solution)/shard_map/ppermute | solution.py:535
  280.9 30.2 %collective-permute-start.30 = (bf16[256,1024]{1,0:T(8,128)(2,1)S(1)}, bf16[256,1024]{1,0:T(8,128)(2,1)S(1)}, u32[]{:S(2)}, u32[]{:S(2)}) collective-permute-start(bf16[256,1024]{1,0:T(8,128)(2,1)S(1)} %get-tuple-element.83.r0), channel_id=1, source_target_pairs={{0,2},{1,3},{2,0},{3,1},{4,6},{5,7},{6,4},{7,5},{8,10},{9,11},{10,... | collective-permute-start | bytes 1572872 | tf_op jit(solution)/shard_map/ppermute | solution.py:492
  281.2 30.0 %collective-permute-start.36 = (bf16[256,1024]{1,0:T(8,128)(2,1)S(1)}, bf16[256,1024]{1,0:T(8,128)(2,1)S(1)}, u32[]{:S(2)}, u32[]{:S(2)}) collective-permute-start(bf16[256,1024]{1,0:T(8,128)(2,1)S(1)} %get-tuple-element.93), channel_id=1, source_target_pairs={{0,1},{1,0},{2,3},{3,2},{4,5},{5,4},{6,7},{7,6},{8,9},{9,8},{10,11... | collective-permute-start | bytes 1572872 | tf_op jit(solution)/shard_map/ppermute | solution.py:492
  281.4 30.3 %collective-permute-start.45 = (bf16[128,1024]{1,0:T(8,128)(2,1)S(1)}, bf16[128,1024]{1,0:T(8,128)(2,1)S(1)}, u32[]{:S(2)}, u32[]{:S(2)}) collective-permute-start(bf16[128,1024]{1,0:T(8,128)(2,1)S(1)} %get-tuple-element.107), channel_id=1, source_target_pairs={{0,4},{4,0},{8,12},{12,8},{16,20},{20,16},{24,28},{28,24},{1,5},{5... | collective-permute-start | bytes 786440 | tf_op jit(solution)/shard_map/ppermute | solution.py:492
  285.1 39.1 %collective-permute-start.47 = (bf16[128,1024]{1,0:T(8,128)(2,1)S(1)}, bf16[128,1024]{1,0:T(8,128)(2,1)S(1)}, u32[]{:S(2)}, u32[]{:S(2)}) collective-permute-start(bf16[128,1024]{1,0:T(8,128)(2,1)S(1)} %get-tuple-element.109), channel_id=1, source_target_pairs={{0,4},{4,0},{8,12},{12,8},{16,20},{20,16},{24,28},{28,24},{1,5},{5... | collective-permute-start | bytes 786440 | tf_op jit(solution)/shard_map/ppermute | solution.py:492
  311.2 21.4 %collective-permute-start.31 = (bf16[256,1024]{1,0:T(8,128)(2,1)S(1)}, bf16[256,1024]{1,0:T(8,128)(2,1)S(1)}, u32[]{:S(2)}, u32[]{:S(2)}) collective-permute-start(bf16[256,1024]{1,0:T(8,128)(2,1)S(1)} %collective-permute-done.30.r2), channel_id=1, source_target_pairs={{0,1},{1,0},{2,3},{3,2},{4,5},{5,4},{6,7},{7,6},{8,9},{9,8},{10,11... | collective-permute-start | bytes 1572872 | tf_op jit(solution)/shard_map/ppermute | solution.py:492
  323.1 22.9 %collective-permute-start.44 = (bf16[128,1024]{1,0:T(8,128)(2,1)}, bf16[128,1024]{1,0:T(8,128)(2,1)}, u32[]{:S(2)}, u32[]{:S(2)}) collective-permute-start(bf16[128,1024]{1,0:T(8,128)(2,1)} %get-tuple-element.105), channel_id=1, source_target_pairs={{0,4},{4,0},{8,12},{12,8},{16,20},{20,16},{24,28},{28,24},{1,5},{5... | collective-permute-start | bytes 786440 | tf_op jit(solution)/shard_map/ppermute | solution.py:492
  325.5 22.2 %collective-permute-start.46 = (bf16[128,1024]{1,0:T(8,128)(2,1)}, bf16[128,1024]{1,0:T(8,128)(2,1)}, u32[]{:S(2)}, u32[]{:S(2)}) collective-permute-start(bf16[128,1024]{1,0:T(8,128)(2,1)} %add_convert_fusion.9), channel_id=1, source_target_pairs={{24,0},{28,4},{0,8},{4,12},{8,16},{12,20},{16,24},{20,28},{25,1},{... | collective-permute-start | bytes 786440 | tf_op jit(solution)/shard_map/ppermute | solution.py:535
  328.8 18.9 %collective-permute-start.48 = (bf16[128,1024]{1,0:T(8,128)(2,1)}, bf16[128,1024]{1,0:T(8,128)(2,1)}, u32[]{:S(2)}, u32[]{:S(2)}) collective-permute-start(bf16[128,1024]{1,0:T(8,128)(2,1)} %add_convert_fusion.8), channel_id=1, source_target_pairs={{8,0},{12,4},{16,8},{20,12},{24,16},{28,20},{0,24},{4,28},{9,1},{1... | collective-permute-start | bytes 786440 | tf_op jit(solution)/shard_map/ppermute | solution.py:535
  333.4 19.5 %collective-permute-start.50 = (bf16[128,1024]{1,0:T(8,128)(2,1)}, bf16[128,1024]{1,0:T(8,128)(2,1)}, u32[]{:S(2)}, u32[]{:S(2)}) collective-permute-start(bf16[128,1024]{1,0:T(8,128)(2,1)} %add_convert_fusion.7), channel_id=1, source_target_pairs={{16,0},{20,4},{24,8},{28,12},{0,16},{4,20},{8,24},{12,28},{17,1},{... | collective-permute-start | bytes 786440 | tf_op jit(solution)/shard_map/ppermute | solution.py:535
  333.4 23.0 %collective-permute-start.42 = (bf16[256,1024]{1,0:T(8,128)(2,1)S(1)}, bf16[256,1024]{1,0:T(8,128)(2,1)S(1)}, u32[]{:S(2)}, u32[]{:S(2)}) collective-permute-start(bf16[256,1024]{1,0:T(8,128)(2,1)S(1)} %get-tuple-element.99.r0), channel_id=1, source_target_pairs={{0,2},{1,3},{2,0},{3,1},{4,6},{5,7},{6,4},{7,5},{8,10},{9,11},{10,... | collective-permute-start | bytes 1572872 | tf_op jit(solution)/shard_map/ppermute | solution.py:492
  (91 other events, 965.1 us)
Sparse Core Ops, SparseCore 0:
  10.3 96.1 all-gather.1

commit v2 on v1

v2 whole, which is shorter than its diff:
```python
import functools

import jax
import jax.numpy as jnp
from jax import lax
from jax.experimental import pallas as pl
from jax.experimental.pallas import tpu as pltpu
from jax.sharding import PartitionSpec as P

HEAD_DIM = 64
BLOCK = 256
EPS = 1e-06
NEG = -1e30
F32 = jnp.float32
BF16 = jnp.bfloat16
GELU_C = 0.7978845608028654
GELU_A = 0.044715

VMEM_SPEC = pl.BlockSpec(memory_space=pltpu.VMEM)
SMEM_SPEC = pl.BlockSpec(memory_space=pltpu.SMEM)
HBM_SPEC = pl.BlockSpec(memory_space=pltpu.HBM)


def mm(a, b):
    return jnp.dot(a, b, preferred_element_type=F32)


def mm_t(a, b):
    return lax.dot_general(a, b, (((1,), (1,)), ((), ())), preferred_element_type=F32)


def t_mm(a, b):
    return lax.dot_general(a, b, (((0,), (0,)), ((), ())), preferred_element_type=F32)


def shape(dims, dtype):
    return jax.ShapeDtypeStruct(dims, dtype)


def after(value, *others):
    return lax.optimization_barrier((value,) + others)[0]


COST = pl.CostEstimate(flops=1, bytes_accessed=1, transcendentals=0)


def in_hbm(value):
    return pltpu.with_memory_space_constraint(value, pltpu.HBM)


def params(mib):
    return pltpu.CompilerParams(vmem_limit_bytes=max(mib, 48) << 20)


def tiles(total, width, step):
    def body(j, carry):
        step(pl.ds(pl.multiple_of(j * width, width), width), j)
        return carry

    lax.fori_loop(0, total // width, body, 0)


def pick_kernel(order, onehot, values, out, buf, sems):
    routed = onehot.shape[1]
    count = buf.shape[0]
    copies = [
        pltpu.make_async_copy(values.at[order[i]], buf.at[i], sems.at[i]) for i in range(count)
    ]
    for copy in copies:
        copy.start()
    for i, copy in enumerate(copies):
        copy.wait()
        out[i * routed : (i + 1) * routed, :] = mm(onehot[order[i]], buf[i]).astype(BF16)


def pick_rows(values, onehot, order):
    count = order.shape[0]
    _, routed, span = onehot.shape
    width = values.shape[2]
    return pl.pallas_call(
        pick_kernel,
        in_specs=[SMEM_SPEC, VMEM_SPEC, HBM_SPEC],
        out_specs=VMEM_SPEC,
        out_shape=shape((count * routed, width), BF16),
        scratch_shapes=[
            pltpu.VMEM((count, span, width), BF16),
            pltpu.SemaphoreType.DMA((count,)),
        ],
        compiler_params=params(8),
        cost_estimate=COST,
        name="pick_rows",
    )(order, onehot, in_hbm(values))


def place_kernel(order, onehot_t, *refs, blocks):
    out, buf, sums, loads, stores = refs[-5:]
    row_refs = refs[:blocks]
    base = refs[blocks]
    count = buf.shape[0]
    routed = onehot_t.shape[2]
    found = [(ref, at) for ref in row_refs for at in range(0, ref.shape[0], routed)]
    reads = [
        pltpu.make_async_copy(base.at[order[i]], buf.at[i], loads.at[i]) for i in range(count)
    ]
    writes = [
        pltpu.make_async_copy(sums.at[i], out.at[order[i]], stores.at[i]) for i in range(count)
    ]
    for copy in reads:
        copy.start()
    for i in range(count):
        ref, at = found[i]
        rows = ref[at : at + routed, :]
        hot = onehot_t[order[i]]
        keep = 1.0 - jnp.sum(hot.astype(F32), axis=1, keepdims=True)
        reads[i].wait()
        sums[i] = buf[i] * keep.astype(BF16) + mm(hot, rows).astype(BF16)
        writes[i].start()
    for copy in writes:
        copy.wait()


def place_rows(base, onehot_t, rows, order, into=None):
    _, span, width = base.shape
    count = order.shape[0]
    extra = [] if into is None else [into]
    return pl.pallas_call(
        functools.partial(place_kernel, blocks=len(rows)),
        in_specs=[SMEM_SPEC, VMEM_SPEC]
        + [VMEM_SPEC] * len(rows)
        + [HBM_SPEC] * (1 + len(extra)),
        out_specs=HBM_SPEC,
        out_shape=shape(base.shape, BF16),
        scratch_shapes=[
            pltpu.VMEM((count, span, width), BF16),
            pltpu.VMEM((count, span, width), BF16),
            pltpu.SemaphoreType.DMA((count,)),
            pltpu.SemaphoreType.DMA((count,)),
        ],
        input_output_aliases={3 + len(rows): 0} if extra else {},
        compiler_params=params(8),
        cost_estimate=COST,
        name="place_rows",
    )(order, onehot_t, *rows, in_hbm(base), *extra)


def row_call(body, name, inputs, outputs, rows, width, steps=2):
    block = rows // steps
    in_specs = []
    for array, kind in inputs:
        if kind == "w":
            in_specs.append(pl.BlockSpec(array.shape, lambda i: (0, 0)))
        elif kind == "h":
            in_specs.append(pl.BlockSpec((block, array.shape[1]), lambda i: (0, 0)))
        else:
            in_specs.append(pl.BlockSpec((block, array.shape[1]), lambda i: (i, 0)))
    out_specs = []
    out_shapes = []
    for dims, dtype, kind in outputs:
        out_shapes.append(shape(dims, dtype))
        if kind == "w":
            out_specs.append(pl.BlockSpec(dims, lambda i: (0, 0)))
        else:
            out_specs.append(pl.BlockSpec((block, dims[1]), lambda i: (i, 0)))
    return pl.pallas_call(
        body,
        grid=(steps,),
        in_specs=in_specs,
        out_specs=out_specs,
        out_shape=out_shapes,
        compiler_params=params(10),
        cost_estimate=COST,
        name=name,
    )(*[array for array, _ in inputs])


def row_mean(x):
    return jnp.mean(x, axis=-1, keepdims=True)


def total3(a, b0, b1, c):
    b = jnp.where(pl.program_id(0) == 0, b0[...].astype(F32), b1[...].astype(F32))
    return a[...].astype(F32) + b + c[...].astype(F32)


def lanes(col):
    return jnp.broadcast_to(col, (col.shape[0], 128))


def fold(x):
    return jnp.sum(x.reshape(-1, 8, x.shape[1]), axis=0)


def accumulate(ref, value):
    @pl.when(pl.program_id(0) == 0)
    def _():
        ref[...] = value

    @pl.when(pl.program_id(0) > 0)
    def _():
        ref[...] += value


def first_norm_body(a, b0, b1, c, vec, rows_out, normed_out, gate_out):
    rows = total3(a, b0, b1, c)
    rows_out[...] = rows.astype(BF16)
    logit = jnp.sum(rows * vec[0:1, :], axis=-1, keepdims=True)
    gate_out[...] = lanes(jax.nn.sigmoid(logit))
    scale = lax.rsqrt(row_mean(rows * rows) + EPS)
    normed_out[...] = (rows * scale * vec[1:2, :]).astype(BF16)


def cot_body(a, b0, b1, c, gate, cot_out, grad_out):
    cot = total3(a, b0, b1, c)
    cot_out[...] = cot.astype(BF16)
    grad_out[...] = (cot * gate[:, 0:1]).astype(BF16)


def second_norm_body(rows, a, b0, b1, c, vec, attn_out, normed_out):
    attn = total3(a, b0, b1, c)
    attn_out[...] = attn
    hidden = rows[...].astype(F32) + attn
    scale = lax.rsqrt(row_mean(hidden * hidden) + EPS)
    normed_out[...] = (hidden * scale * vec[2:3, :]).astype(BF16)


def second_back_body(rows, attn, cot, gate, a, b0, b1, c, vec, grad_out, hidden_out, gain_out):
    second_grad = total3(a, b0, b1, c)
    hidden = rows[...].astype(F32) + attn[...]
    scale = lax.rsqrt(row_mean(hidden * hidden) + EPS)
    normal = hidden * scale
    grad = second_grad * vec[2:3, :]
    hidden_grad = scale * (grad - normal * row_mean(grad * normal))
    hidden_out[...] = hidden_grad
    grad_out[...] = (cot[...].astype(F32) * gate[:, 0:1] + hidden_grad).astype(BF16)
    accumulate(gain_out, fold(second_grad * normal))


def out_body(rows, attn, cot, gate, a, b0, b1, c, rows_out, gate_grad_out, router_out):
    branch = attn[...] + total3(a, b0, b1, c)
    x = rows[...].astype(F32)
    g = gate[:, 0:1]
    rows_out[...] = (x + g * branch).astype(BF16)
    gate_grad = jnp.sum(cot[...].astype(F32) * branch, axis=-1, keepdims=True) * g * (1.0 - g)
    gate_grad_out[...] = lanes(gate_grad)
    accumulate(router_out, fold(x * gate_grad))


def first_back_body(
    rows, cot, gate_grad, hidden_grad, a, b0, b1, c, vec, router_part, second_part, grad_out, vec_out, acc
):
    first_grad = total3(a, b0, b1, c)
    x = rows[...].astype(F32)
    scale = lax.rsqrt(row_mean(x * x) + EPS)
    normal = x * scale
    grad = first_grad * vec[1:2, :]
    norm_grad = scale * (grad - normal * row_mean(grad * normal))
    grad_out[...] = (
        cot[...].astype(F32) + gate_grad[:, 0:1] * vec[0:1, :] + hidden_grad[...] + norm_grad
    ).astype(BF16)
    accumulate(acc, fold(first_grad * normal))

    @pl.when(pl.program_id(0) == pl.num_programs(0) - 1)
    def _():
        vec_out[0:1, :] = jnp.sum(router_part[...], axis=0, keepdims=True)
        vec_out[1:2, :] = jnp.sum(acc[...], axis=0, keepdims=True)
        vec_out[2:3, :] = jnp.sum(second_part[...], axis=0, keepdims=True)
        vec_out[3:8, :] = jnp.zeros_like(vec_out[3:8, :])


def pack_mlp_kernel(up, down, out, buf, sems):
    depth = up.shape[0]
    copies = [
        pltpu.make_async_copy(up, out.at[0:depth, :], sems.at[0]),
        pltpu.make_async_copy(down, buf, sems.at[1]),
    ]
    for copy in copies:
        copy.start()
    copies[1].wait()
    out[depth : 2 * depth, :] = buf[...].T
    copies[0].wait()


def pack_attn_kernel(q, k, v, o, small, out, buf, sems):
    depth, local = q.shape
    copies = [
        pltpu.make_async_copy(
            x, out.at[0:depth, i * local : (i + 1) * local], sems.at[i]
        )
        for i, x in enumerate((q, k, v))
    ]
    copies.append(pltpu.make_async_copy(o, buf, sems.at[3]))
    for copy in copies:
        copy.start()
    out[depth:, :] = jnp.zeros_like(out[depth:, :])
    out[depth:, 0:depth] = small[...]
    copies[3].wait()
    out[0:depth, 3 * local : 4 * local] = buf[...].T
    for copy in copies[:3]:
        copy.wait()


def pack_mlp(up, down):
    return pl.pallas_call(
        pack_mlp_kernel,
        in_specs=[HBM_SPEC] * 2,
        out_specs=VMEM_SPEC,
        out_shape=shape((2 * up.shape[0], up.shape[1]), BF16),
        scratch_shapes=[pltpu.VMEM(down.shape, BF16), pltpu.SemaphoreType.DMA((2,))],
        compiler_params=params(4),
        cost_estimate=COST,
        name="pack_mlp",
    )(in_hbm(up), in_hbm(down))


def pack_attn(q, k, v, o, small):
    depth, local = q.shape
    return pl.pallas_call(
        pack_attn_kernel,
        in_specs=[HBM_SPEC] * 4 + [VMEM_SPEC],
        out_specs=VMEM_SPEC,
        out_shape=shape((depth + 16, 4 * local), BF16),
        scratch_shapes=[pltpu.VMEM(o.shape, BF16), pltpu.SemaphoreType.DMA((4,))],
        compiler_params=params(4),
        cost_estimate=COST,
        name="pack_attn",
    )(in_hbm(q), in_hbm(k), in_hbm(v), in_hbm(o), small)


def finish_mlp_kernel(total, up_out, down_out):
    depth = up_out.shape[0]
    total = total[...].astype(F32)
    up_out[...] = total[0:depth]
    down_out[...] = total[depth:].T


def finish_attn_kernel(own, got, p1, p2, p3, q_out, k_out, v_out, o_out):
    local = q_out.shape[1]
    total = own[...] + got[...].astype(F32)
    for part in (p1, p2, p3):
        total = total + part[...].astype(F32)
    q_out[...] = total[:, 0:local]
    k_out[...] = total[:, local : 2 * local]
    v_out[...] = total[:, 2 * local : 3 * local]
    o_out[...] = total[:, 3 * local :].T


def finish(body, name, dims, *arrays):
    return pl.pallas_call(
        body,
        in_specs=[VMEM_SPEC] * len(arrays),
        out_specs=[VMEM_SPEC] * len(dims),
        out_shape=[shape(d, F32) for d in dims],
        compiler_params=params(8),
        cost_estimate=COST,
        name=name,
    )(*arrays)


def join_kernel(places, *refs):
    *pieces, out, vec = refs
    depth = out.shape[0] // (len(pieces) - 1)
    vec[...] = jnp.zeros_like(vec)
    for number, piece in enumerate(pieces):
        if number > 0:
            out[(number - 1) * depth : number * depth, :] = piece[0:depth, :]
        place = places[number] * 2 + places[4]
        lanes_at = pl.ds(pl.multiple_of(place * depth, depth), depth)
        vec[:, lanes_at] = piece[depth : depth + 16, 0:depth]


def join(pieces, places, depth):
    width = pieces[0].shape[1]
    return pl.pallas_call(
        join_kernel,
        in_specs=[SMEM_SPEC] + [VMEM_SPEC] * len(pieces),
        out_specs=[VMEM_SPEC] * 2,
        out_shape=[
            shape((depth * (len(pieces) - 1), width), BF16),
            shape((16, width), BF16),
        ],
        compiler_params=params(6),
        cost_estimate=COST,
        name="join",
    )(places, *pieces)


def assemble_kernel(places, near_own, near, far_own, far, out):
    depth = 128
    for side, halves in enumerate(((near_own, near), (far_own, far))):
        for number in range(4):
            ref = halves[min(number, 1)]
            row = max(number - 1, 0) * depth
            place = places[number] * 2 + (places[4] ^ side)
            at = pl.multiple_of(place * depth, depth)
            out[pl.ds(at, depth), :] = ref[row : row + depth, :]


def assemble(near_own, near, far_own, far, places):
    rows, width = near.shape
    return pl.pallas_call(
        assemble_kernel,
        in_specs=[SMEM_SPEC] + [VMEM_SPEC] * 4,
        out_specs=VMEM_SPEC,
        out_shape=shape((rows * 8 // 3, width), BF16),
        compiler_params=params(6),
        cost_estimate=COST,
        name="assemble",
    )(places, near_own, near, far_own, far)


def head_masks(width):
    lane = lax.broadcasted_iota(jnp.int32, (1, width), 1) // HEAD_DIM
    return [(lane == h).astype(BF16) for h in range(width // HEAD_DIM)]


def spread(x, masks):
    return jnp.concatenate([x * mask for mask in masks], axis=0)


def side_by_side(x, count):
    rows = x.shape[0] // count
    return jnp.concatenate([x[h * rows : (h + 1) * rows] for h in range(count)], axis=1)


def seq_probs(q4, k, bias, count):
    scores = mm_t(q4, k) * (HEAD_DIM**-0.5)
    scores = scores + jnp.concatenate([bias] * count, axis=0)
    top = jnp.max(scores, axis=-1, keepdims=True)
    weight = jnp.exp(scores - top)
    return weight / jnp.sum(weight, axis=-1, keepdims=True)


def fill(ref, parts):
    at = 0
    for part in parts:
        ref[at : at + part.shape[0], :] = part[...]
        at += part.shape[0]


def attn_fwd_kernel(order, xa, *refs, parts):
    w, bias, qkv, ctx, pa, pb, xb = refs[parts:]
    fill(xb, refs[:parts])
    half = xa.shape[0]
    local = ctx.shape[1]
    routed = bias.shape[1]
    heads = local // HEAD_DIM
    masks = head_masks(local)

    def project(cols, j):
        qkv[0:half, cols] = mm(xa[...], w[:, cols]).astype(BF16)
        qkv[half : 2 * half, cols] = mm(xb[...], w[:, cols]).astype(BF16)

    tiles(3 * local, local, project)

    def seq(rows, s):
        q = qkv[rows, 0:local]
        k = qkv[rows, local : 2 * local]
        v = qkv[rows, 2 * local : 3 * local]
        probs = seq_probs(spread(q, masks), k, bias[order[s]], heads).astype(BF16)
        ctx[rows, :] = mm(side_by_side(probs, heads), spread(v, masks)).astype(BF16)

    tiles(2 * half, routed, seq)

    def emit(cols, j):
        wo = w[cols, 3 * local : 4 * local]
        pa[:, cols] = mm_t(ctx[0:half, :], wo).astype(BF16)
        pb[:, cols] = mm_t(ctx[half : 2 * half, :], wo).astype(BF16)

    tiles(pa.shape[1], 256, emit)


def attn_fwd(xa, xb, w, bias, order, local):
    rows, width = xa.shape
    return pl.pallas_call(
        functools.partial(attn_fwd_kernel, parts=len(xb)),
        in_specs=[SMEM_SPEC] + [VMEM_SPEC] * (3 + len(xb)),
        out_specs=[VMEM_SPEC] * 4,
        out_shape=[
            shape((2 * rows, 3 * local), BF16),
            shape((2 * rows, local), BF16),
            shape((rows, width), BF16),
            shape((rows, width), BF16),
        ],
        scratch_shapes=[pltpu.VMEM((rows, width), BF16)],
        compiler_params=params(12),
        cost_estimate=COST,
        name="attn_fwd",
    )(order, xa, *xb, w, bias)


def attn_bwd_kernel(order, ga, *refs, parts):
    w, qkv, bias, dqkv, fa, fb, cg, gb = refs[parts:]
    fill(gb, refs[:parts])
    half = ga.shape[0]
    local = cg.shape[1]
    routed = bias.shape[1]
    heads = local // HEAD_DIM
    masks = head_masks(local)
    wo = w[:, 3 * local : 4 * local]
    cg[0:half, :] = mm(ga[...], wo).astype(BF16)
    cg[half : 2 * half, :] = mm(gb[...], wo).astype(BF16)

    def seq(rows, s):
        q4 = spread(qkv[rows, 0:local], masks)
        k = qkv[rows, local : 2 * local]
        v = qkv[rows, 2 * local : 3 * local]
        exact = seq_probs(q4, k, bias[order[s]], heads)
        c4 = spread(cg[rows, :], masks)
        prob_grad = mm_t(c4, v)
        dqkv[rows, 2 * local : 3 * local] = t_mm(exact.astype(BF16), c4).astype(BF16)
        inner = jnp.sum(exact * prob_grad, axis=-1, keepdims=True)
        score_grad = (exact * (prob_grad - inner)).astype(BF16)
        scale = HEAD_DIM**-0.5
        dq = mm(side_by_side(score_grad, heads), spread(k, masks)) * scale
        dqkv[rows, 0:local] = dq.astype(BF16)
        dqkv[rows, local : 2 * local] = (t_mm(score_grad, q4) * scale).astype(BF16)

    tiles(2 * half, routed, seq)

    def emit(cols, j):
        wj = w[cols, 0 : 3 * local]
        fa[:, cols] = mm_t(dqkv[0:half, :], wj).astype(BF16)
        fb[:, cols] = mm_t(dqkv[half : 2 * half, :], wj).astype(BF16)

    tiles(fa.shape[1], 256, emit)


def attn_bwd(ga, gb, w, qkv, bias, order, local):
    rows, width = ga.shape
    return pl.pallas_call(
        functools.partial(attn_bwd_kernel, parts=len(gb)),
        in_specs=[SMEM_SPEC] + [VMEM_SPEC] * (4 + len(gb)),
        out_specs=[VMEM_SPEC] * 3,
        out_shape=[
            shape((2 * rows, 3 * local), BF16),
            shape((rows, width), BF16),
            shape((rows, width), BF16),
        ],
        scratch_shapes=[pltpu.VMEM((2 * rows, local), BF16), pltpu.VMEM((rows, width), BF16)],
        compiler_params=params(12),
        cost_estimate=COST,
        name="attn_bwd",
    )(order, ga, *gb, w, qkv, bias)


def mlp_kernel(na, ga, *refs, parts):
    w, act, ug, da, db, ma, mb, nb, gb = refs[2 * parts :]
    fill(nb, refs[:parts])
    fill(gb, refs[parts : 2 * parts])
    rows, width = na.shape
    part, both, ff = w.shape
    depth = both // 2

    def up(cols, j):
        wu = w[:, 0:depth, cols].reshape(width, -1)
        wd = w[:, depth:both, cols].reshape(width, -1)
        for n, g, at in ((na, ga, 0), (nb, gb, rows)):
            x = mm(n[...], wu)
            inner = jnp.tanh(GELU_C * (x + GELU_A * (x * x * x)))
            half_in = 0.5 * (1.0 + inner)
            act[at : at + rows, cols] = (x * half_in).astype(BF16)
            slope = half_in + (0.5 * GELU_C) * x * (1.0 - inner * inner) * (
                1.0 + (3.0 * GELU_A) * (x * x)
            )
            ug[at : at + rows, cols] = (mm(g[...], wd) * slope).astype(BF16)

    tiles(ff, 256, up)
    group = part * 256 // width

    def back(cols, j):
        wu = w[pl.ds(j * group, group), 0:depth, :].reshape(256, -1)
        da[:, cols] = mm_t(ug[0:rows, :], wu).astype(BF16)
        db[:, cols] = mm_t(ug[rows : 2 * rows, :], wu).astype(BF16)

    tiles(width, 256, back)

    def down(cols, j):
        wd = w[pl.ds(j * group, group), depth:both, :].reshape(256, -1)
        ma[:, cols] = mm_t(act[0:rows, :], wd).astype(BF16)
        mb[:, cols] = mm_t(act[rows : 2 * rows, :], wd).astype(BF16)

    tiles(width, 256, down)


def mlp_both(na, nb, ga, gb, w):
    rows, width = na.shape
    ff = w.shape[2]
    return pl.pallas_call(
        functools.partial(mlp_kernel, parts=len(nb)),
        in_specs=[VMEM_SPEC] * (3 + 2 * len(nb)),
        out_specs=[VMEM_SPEC] * 6,
        out_shape=[shape((2 * rows, ff), BF16)] * 2 + [shape((rows, width), BF16)] * 4,
        scratch_shapes=[pltpu.VMEM((rows, width), BF16)] * 2,
        compiler_params=params(16),
        cost_estimate=COST,
        name="mlp",
    )(na, ga, *nb, *gb, w)


def turn(xt, pieces, cols):
    at = 0
    for piece in pieces:
        size = piece.shape[0]
        xt[:, at : at + size] = piece[:, cols].T
        at += size


def mlp_grads_kernel(*refs, depth, pieces):
    normed, grads = refs[:pieces], refs[pieces : 2 * pieces]
    un, uf, an, af, out, xt = refs[2 * pieces :]
    half = un.shape[0]
    width = normed[0].shape[1]
    group = 256 // depth

    def columns(cols, z):
        for side, (xs, near, far) in enumerate(((normed, un, uf), (grads, an, af))):
            turn(xt, xs, cols)

            def block(ncols, j, near=near, far=far, side=side):
                total = mm(xt[:, 0:half], near[:, ncols])
                total = total + mm(xt[:, half:], far[:, ncols])
                for i in range(group):
                    at = pl.multiple_of((z * group + i) * 2 * depth + side * depth, depth)
                    part = total[i * depth : (i + 1) * depth]
                    out[pl.ds(at, depth), ncols] = part.astype(BF16)

            tiles(near.shape[1], 256, block)

    tiles(width, 256, columns)


def mlp_grads(normed, grads, ug, act, depth):
    width = normed[0].shape[1]
    rows, ff = ug[0].shape
    return pl.pallas_call(
        functools.partial(mlp_grads_kernel, depth=depth, pieces=len(normed)),
        in_specs=[VMEM_SPEC] * (2 * len(normed) + 4),
        out_specs=VMEM_SPEC,
        out_shape=shape((2 * width, ff), BF16),
        scratch_shapes=[pltpu.VMEM((256, 2 * rows), BF16)],
        compiler_params=params(20),
        cost_estimate=COST,
        name="mlp_grads",
    )(*normed, *grads, *ug, *act)


def attn_grads_kernel(info, *refs, pieces):
    normed, grads = refs[:pieces], refs[pieces : 2 * pieces]
    dn, df, cn, cf, first, others, *keeps, xt = refs[2 * pieces :]
    half = dn.shape[0]
    local = cn.shape[1]
    depth = first.shape[0]
    count = len(keeps)
    low = info[count] == 0
    for o in range(count):
        cols = pl.ds(pl.multiple_of(info[o] * 256, 256), 256)
        send, row = (first, 0) if o == 0 else (others, (o - 1) * depth)
        for lane, wide, xs, near, far in (
            (0, 3 * local, normed, dn, df),
            (3 * local, local, grads, cn, cf),
        ):
            turn(xt, xs, cols)

            def block(ncols, j, near=near, far=far, lane=lane, send=send, row=row, o=o):
                total = mm(xt[:, 0:half], near[:, ncols])
                total = total + mm(xt[:, half:], far[:, ncols])
                one, two = total[0:depth], total[depth : 2 * depth]
                dst = pl.ds(pl.multiple_of(j * 256, 256) + lane, 256)
                send[row : row + depth, dst] = jnp.where(low, two, one).astype(BF16)
                keeps[o][:, dst] = jnp.where(low, one, two)

            tiles(wide, 256, block)


def attn_grads(normed, grads, dqkv, ctx, info, depth):
    rows, local = ctx[0].shape
    count = info.shape[0] - 1
    first, others, *keeps = pl.pallas_call(
        functools.partial(attn_grads_kernel, pieces=len(normed)),
        in_specs=[SMEM_SPEC] + [VMEM_SPEC] * (2 * len(normed) + 4),
        out_specs=[VMEM_SPEC] * (2 + count),
        out_shape=[
            shape((depth, 4 * local), BF16),
            shape(((count - 1) * depth, 4 * local), BF16),
        ]
        + [shape((depth, 4 * local), F32)] * count,
        scratch_shapes=[pltpu.VMEM((256, 2 * rows), BF16)],
        compiler_params=params(14),
        cost_estimate=COST,
        name="attn_grads",
    )(info, *normed, *grads, *dqkv, *ctx)
    return first, others, keeps


def swap(x, axis, mask):
    size = lax.axis_size(axis)
    return lax.ppermute(x, axis, [(i, i ^ mask) for i in range(size)])


def halves(x):
    step = x.shape[0] // 2
    return x[:step], x[step:]


def pair_swap(x):
    return tuple(swap(h, "tensor", 1) for h in halves(x))


def pair_sum(near, diag):
    return jnp.concatenate(
        [
            (n.astype(F32) + g.astype(F32)).astype(BF16)
            for n, g in zip(halves(near), pair_swap(diag))
        ],
        axis=0,
    )


def z_perm(size, shift):
    places = size // 2
    return [((f // 2 + shift) % places * 2 + f % 2, f) for f in range(size)]


def z_move(x, shift):
    return lax.ppermute(x, "fsdp", z_perm(lax.axis_size("fsdp"), shift))


SHIFTS = (2, 1, 3)


def shards(
    tokens,
    cotangent,
    routed_index,
    query_weight,
    key_weight,
    value_weight,
    output_weight,
    up_weight,
    down_weight,
    router_weight,
    attn_gain,
    mlp_gain,
):
    fsdp = lax.axis_size("fsdp")
    grid = fsdp == 8
    me_f = lax.axis_index("fsdp")
    me_t = lax.axis_index("tensor")
    seqs, span, width = tokens.shape
    routed = routed_index.shape[1]
    per = seqs // lax.axis_size("tensor")
    local = query_weight.shape[1]
    depth = query_weight.shape[0]
    ff = up_weight.shape[1]
    rows = per * routed

    place = routed_index - me_t * span
    positions = jnp.arange(span, dtype=jnp.int32)
    onehot = (place[:, :, None] == positions[None, None, :]).astype(BF16)
    order = jnp.stack([(me_t ^ m) * per + j for m in range(4) for j in range(per)])
    order_keep = jnp.concatenate([order[0:per], order[2 * per : 3 * per]])
    order_send = jnp.concatenate([order[per : 2 * per], order[3 * per :]])
    order_near = order[: 2 * per]
    order_far = order[2 * per :]

    row_shape = ((rows, width), BF16, "r")
    f32_shape = ((rows, width), F32, "r")
    gate_shape = ((rows, 128), F32, "r")
    vec_shape = ((8, width), F32, "w")

    def row_step(body, name, ins, outs):
        return row_call(body, name, ins, outs, rows, width)

    def r(*arrays):
        found = []
        for a in arrays:
            found += [(h, "h") for h in a] if isinstance(a, tuple) else [(a, "r")]
        return found

    zi = me_f // 2
    yi = me_f % 2

    small = jnp.stack([router_weight, attn_gain, mlp_gain])
    if grid:
        small = jnp.concatenate([small, jnp.zeros((13, depth), BF16)], axis=0)
        attn_piece = pack_attn(query_weight, key_weight, value_weight, output_weight, small)
        z_pieces = [z_move(attn_piece, o) for o in SHIFTS]
        far_own = swap(attn_piece, "fsdp", 1)
        z_at = jnp.stack([zi] + [(zi + o) % (fsdp // 2) for o in SHIFTS] + [yi])
    else:
        attn_piece = jnp.concatenate(
            [query_weight, key_weight, value_weight, output_weight.T], axis=1
        )
        z_pieces = []
        vec = lax.all_gather(small, "fsdp", axis=1, tiled=True)
        vec = jnp.concatenate([vec, jnp.zeros((5, width), BF16)], axis=0).astype(F32)
    tok_send = pick_rows(tokens, onehot, after(order_send, attn_piece))
    tok_got = pair_swap(tok_send)
    tok_keep = pick_rows(tokens, onehot, after(order_keep, tok_send))
    tok_sum = tok_keep[rows:] + tok_got[1]
    tok_far = [swap(h, "tensor", 2) for h in halves(tok_sum)]
    cot_send = pick_rows(cotangent, onehot, after(order_send, tok_sum))
    cot_got = pair_swap(cot_send)
    cot_keep = pick_rows(cotangent, onehot, after(order_keep, cot_send))
    cot_sum = cot_keep[rows:] + cot_got[1]
    cot_far = [swap(h, "tensor", 2) for h in halves(cot_sum)]
    if grid:
        mlp_piece = pack_mlp(up_weight, after(down_weight, cot_keep))
        gated = [after(z, mlp_piece, *tok_far, *cot_far) for z in z_pieces]
        near_w, vec_near = join([attn_piece] + gated, z_at, depth)
        vec = vec_near + swap(vec_near, "fsdp", 1)
        far_w = swap(after(near_w, vec), "fsdp", 1)
        vec = vec[0:8].astype(F32)
        mlp_piece = after(mlp_piece, near_w)
    else:
        mlp_piece = jnp.concatenate([up_weight, down_weight.T], axis=0)
    up_down = lax.all_gather(mlp_piece, "fsdp", axis=0, tiled=True)
    up_down = up_down.reshape(fsdp, 2 * depth, ff)

    def with_halves(body):
        def whole(keep, got, far0, far1, *rest):
            far = jnp.where(pl.program_id(0) == 0, far0[...], far1[...])
            return body(keep, got, got, far, *rest)

        return whole

    own_rows, n0, gate = row_step(
        with_halves(first_norm_body),
        "first_norm",
        [(tok_keep, "r"), (tok_got[0], "r")] + r(tuple(tok_far)) + [(vec, "w")],
        [row_shape, row_shape, gate_shape],
    )
    n2 = swap(n0, "tensor", 2)
    n1 = swap(n0, "tensor", 1)
    cot, g0 = row_step(
        with_halves(cot_body),
        "cot_rows",
        [(cot_keep, "r"), (cot_got[0], "r")] + r(tuple(cot_far)) + [(after(gate, n0), "r")],
        [row_shape, row_shape],
    )
    g2 = swap(after(g0, n2), "tensor", 2)
    g1 = swap(g0, "tensor", 1)
    blocks = after(routed_index, g0) // BLOCK
    bias = jnp.where(blocks[:, None, :] <= blocks[:, :, None], 0.0, NEG).astype(F32)
    if grid:
        attn_w = assemble(attn_piece, after(near_w, g0), far_own, far_w, z_at)
    else:
        attn_w = lax.all_gather(attn_piece, "fsdp", axis=0, tiled=True)
    n3 = pair_swap(after(n2, attn_w))

    qkv_far, ctx_far, p2, p3 = attn_fwd(n2, n3, attn_w, bias, order_far, local)
    attn_sum = pair_sum(p2, p3)
    attn_x = swap(attn_sum, "tensor", 2)
    qkv_near, ctx_near, p0, p1 = attn_fwd(
        after(n0, attn_sum), (n1,), attn_w, bias, order_near, local
    )
    attn_c = pair_swap(p1)
    attn, s0 = row_step(
        second_norm_body,
        "second_norm",
        r(own_rows, p0, attn_c, attn_x) + [(vec, "w")],
        [f32_shape, row_shape],
    )
    s2 = swap(s0, "tensor", 2)
    s1 = swap(s0, "tensor", 1)
    s3 = pair_swap(s2)
    g3 = pair_swap(after(g2, s0))

    act_far, ug_far, d2, d3, m2, m3 = mlp_both(s2, s3, g2, g3, up_down)
    second_sum = pair_sum(d2, d3)
    second_x = swap(second_sum, "tensor", 2)
    act_near, ug_near, d0, d1, m0, m1 = mlp_both(
        after(s0, second_sum), (s1,), g0, (g1,), up_down
    )
    second_c = pair_swap(d1)

    attn_grad, hidden_grad, second_part = row_step(
        second_back_body,
        "second_back",
        r(own_rows, attn, cot, gate, d0, second_c, second_x) + [(vec, "w")],
        [row_shape, f32_shape, vec_shape],
    )
    a0 = attn_grad
    a2 = swap(a0, "tensor", 2)
    a1 = swap(a0, "tensor", 1)
    mlp_all = mlp_grads(
        (after(s0, a0), s1, s2, *s3),
        (g0, g1, g2, *g3),
        (ug_near, ug_far),
        (act_near, act_far),
        depth,
    )
    a2 = after(a2, mlp_all)
    mlp_total = lax.psum_scatter(after(mlp_all, a2), "fsdp", scatter_dimension=0, tiled=True)
    a3 = pair_swap(a2)
    mlp_c = pair_swap(after(m1, mlp_all))
    mlp_sum = pair_sum(m2, after(m3, mlp_all))
    mlp_x = swap(after(mlp_sum, a2), "tensor", 2)

    def to_z(keep, got, shift):
        return z_move((keep + got.astype(F32)).astype(BF16), 4 - shift)

    dqkv_far, f2, f3 = attn_bwd(a2, a3, attn_w, qkv_far, bias, order_far, local)
    first_sum = pair_sum(f2, f3)
    first_x = swap(first_sum, "tensor", 2)
    dqkv_near, f0, f1 = attn_bwd(
        after(a0, first_sum), (a1,), attn_w, qkv_near, bias, order_near, local
    )
    first_c = pair_swap(f1)
    out_rows, gate_grad, router_part = row_step(
        out_body,
        "out_rows",
        r(own_rows, attn, cot, gate, m0, mlp_c, after(mlp_x, f1)),
        [row_shape, gate_shape, vec_shape],
    )
    o2 = swap(out_rows, "tensor", 2)
    o1 = swap(out_rows, "tensor", 1)

    attn_args = (
        (n0, n1, n2, *n3),
        (a0, a1, a2, *a3),
        (dqkv_near, dqkv_far),
        (ctx_near, ctx_far),
    )
    if grid:
        info = jnp.stack([(zi + o) % (fsdp // 2) for o in SHIFTS + (0,)] + [yi])
        first_b, other_b, keeps = attn_grads(*attn_args, after(info, out_rows), depth)
        first_y = swap(first_b, "fsdp", 1)
        other_y = swap(other_b, "fsdp", 1)
        first_x = after(first_x, first_b)

    half = rows // 2
    grad_rows, vec_part = pl.pallas_call(
        first_back_body,
        grid=(2,),
        in_specs=[
            pl.BlockSpec((half, width), lambda i: (i, 0)),
            pl.BlockSpec((half, width), lambda i: (i, 0)),
            pl.BlockSpec((half, 128), lambda i: (i, 0)),
        ]
        + [pl.BlockSpec((half, width), lambda i: (i, 0))] * 2
        + [pl.BlockSpec((half, width), lambda i: (0, 0))] * 2
        + [pl.BlockSpec((half, width), lambda i: (i, 0))]
        + [pl.BlockSpec((8, width), lambda i: (0, 0))] * 3,
        out_specs=[
            pl.BlockSpec((half, width), lambda i: (i, 0)),
            pl.BlockSpec((8, width), lambda i: (0, 0)),
        ],
        out_shape=[shape((rows, width), BF16), shape((8, width), F32)],
        scratch_shapes=[pltpu.VMEM((8, width), F32)],
        compiler_params=params(12),
        cost_estimate=COST,
        name="first_back",
    )(own_rows, cot, gate_grad, hidden_grad, f0, *first_c, first_x, vec, router_part, second_part)
    t2 = swap(grad_rows, "tensor", 2)
    t1 = swap(grad_rows, "tensor", 1)
    onehot_t = (
        after(place, grad_rows)[:, None, :] == positions[None, :, None]
    ).astype(BF16)
    o3 = pair_swap(after(o2, grad_rows))
    mixed = place_rows(tokens, onehot_t, [after(out_rows, grad_rows), o1], order_near)
    if grid:
        z_first = to_z(keeps[0], after(first_y, grad_rows), SHIFTS[0])
    mixed = place_rows(tokens, onehot_t, [o2, *o3], order_far, mixed)
    near_gate = mixed
    if grid:
        other_y = after(other_y, near_gate)
        z_second = to_z(keeps[1], other_y[0:depth], SHIFTS[1])
        z_third = to_z(keeps[2], other_y[depth : 2 * depth], SHIFTS[2])
    token_grad = place_rows(cotangent, onehot_t, [after(grad_rows, near_gate), t1], order_near)
    t3 = pair_swap(after(t2, token_grad))
    token_grad = place_rows(cotangent, onehot_t, [t2, *t3], order_far, token_grad)
    up_grad, down_grad = finish(
        finish_mlp_kernel, "finish_mlp", [(depth, ff), (ff, depth)], after(mlp_total, token_grad)
    )

    if grid:
        vec_sum = vec_part
        for axis, mask in (("tensor", 1), ("tensor", 2)):
            vec_sum = vec_sum + swap(vec_sum, axis, mask)
        vec_sum = vec_sum + after(swap(vec_sum, "fsdp", 1), token_grad)
        vec_sum = vec_sum + z_move(vec_sum, 1) + z_move(vec_sum, 3) + z_move(vec_sum, 2)
        wide = (depth, local)
        attn_out = finish(
            finish_attn_kernel,
            "finish_attn",
            [wide, wide, wide, (local, depth)],
            keeps[3],
            after(other_y[2 * depth :], token_grad),
            z_first,
            z_second,
            z_third,
        )
    else:

        def reduced(xs, ys):
            x = t_mm(jnp.concatenate(xs, axis=0), jnp.concatenate(ys, axis=0))
            return lax.psum_scatter(x, "fsdp", scatter_dimension=0, tiled=True)

        qkv_grad = reduced(attn_args[0], attn_args[2])
        o_grad = reduced(attn_args[1], attn_args[3])
        attn_out = jnp.split(qkv_grad, 3, axis=1) + [o_grad.T]
        vec_sum = lax.psum(vec_part, ("fsdp", "tensor"))
    vec_own = lax.dynamic_slice(vec_sum, (0, me_f * depth), (3, depth))

    return (mixed, token_grad, *attn_out, up_grad, down_grad, vec_own[0], vec_own[1], vec_own[2])


def solution(mesh):
    in_specs = (
        P("fsdp", "tensor", None),
        P("fsdp", "tensor", None),
        P("fsdp", None),
        P("fsdp", "tensor"),
        P("fsdp", "tensor"),
        P("fsdp", "tensor"),
        P("tensor", "fsdp"),
        P("fsdp", "tensor"),
        P("tensor", "fsdp"),
        P("fsdp"),
        P("fsdp"),
        P("fsdp"),
    )
    out_specs = (
        P("fsdp", "tensor", None),
        P("fsdp", "tensor", None),
        P("fsdp", "tensor"),
        P("fsdp", "tensor"),
        P("fsdp", "tensor"),
        P("tensor", "fsdp"),
        P("fsdp", "tensor"),
        P("tensor", "fsdp"),
        P("fsdp"),
        P("fsdp"),
        P("fsdp"),
    )
    return jax.shard_map(shards, mesh=mesh, in_specs=in_specs, out_specs=out_specs, check_vma=False)
```

time: 379 us -> 314 us (0.83)
  waiting for transfers between devices: 147 us -> 90.7 us
  local copies, waits for them, and re-layouts: 34.9 us -> 24.5 us
  other arithmetic: 15.3 us -> 6.08 us
  starting transfers between devices: 57.2 us -> 63.7 us
  Pallas kernels: 108 us -> 112 us
    ppermute x12 -> x9, waiting for transfers between devices: 67.7 us -> 9.81 us  [z_move(): return lax.ppermute(x, 'fsdp', z_perm(lax.axis_size('fsdp'), shift))]
    ppermute x12 -> x9, starting transfers between devices: 18 us -> 26.9 us  [z_move(): return lax.ppermute(x, 'fsdp', z_perm(lax.axis_size('fsdp'), shift))]
    unnamed x120 -> x140, local copies, waits for them, and re-layouts: 25.4 us -> 16.9 us
    slice x0 -> x19, local copies, waits for them, and re-layouts: none -> 6.77 us  [the longest x18 5.81 us: halves(): return (x[:step], x[step:])]
    all_gather x1 -> x0, local copies, waits for them, and re-layouts: 6.39 us -> none  [shards(): lax.all_gather(jnp.concatenate([up_weight, down_weight.T], axis=0), 'fsdp...]
    convert_element_type x12 -> x8, other arithmetic: 7.29 us -> 2.12 us  [the longest x4 1.78 us: pair_sum(): (n.astype(F32) + g.astype(F32)).astype(BF16)]
    ppermute x52 -> x60, starting transfers between devices: 39.1 us -> 36.7 us  [swap(): return lax.ppermute(x, axis, [(i, i ^ mask) for i in range(size)])]
    pallas_call x15 -> x22, Pallas kernels: 101 us -> 103 us  [the longest x2 21 us: mlp_both(): pl.pallas_call(functools.partial(mlp_kernel, parts=len(nb)), in_specs=[VM...]
  transfers between devices with their start and end apart: 65 -> 71, of which waited for: 22 -> 30; matrix products, arithmetic and copies ran while one was open for 7% -> 3% of each run, Pallas kernels for 26% -> 29%
where the time goes in v2:
time: 314 us; the launch traced here: 312 us
  Pallas kernels  112 us (36%)
  waiting for transfers between devices  90.7 us (29%)
  starting transfers between devices  63.7 us (20%)
  local copies, waits for them, and re-layouts  24.5 us (8%)
  between operations  15.1 us (5%)
  other arithmetic  6.08 us (2%)
    ppermute x60, waiting for transfers between devices, swap(): return lax.ppermute(x, axis, [(i, i ^ mask) for i in range(size)])  80.9 us
    ppermute x60, starting transfers between devices, swap(): return lax.ppermute(x, axis, [(i, i ^ mask) for i in range(size)])  36.7 us
    ppermute x9, starting transfers between devices, z_move(): return lax.ppermute(x, 'fsdp', z_perm(lax.axis_size('fsdp'), shift))  26.9 us
    pallas_call x2, Pallas kernels, mlp_both(): pl.pallas_call(functools.partial(mlp_kernel, parts=len(nb)), in_specs=[VM...  21 us
    unnamed x140, local copies, waits for them, and re-layouts  16.9 us
    pallas_call x1, Pallas kernels, mlp_grads(): pl.pallas_call(functools.partial(mlp_grads_kernel, depth=depth, pieces=le...  15.7 us
    pallas_call x4, Pallas kernels, place_rows(): pl.pallas_call(functools.partial(place_kernel, blocks=len(rows)), in_spec...  15 us
    pallas_call x2, Pallas kernels, attn_bwd(): pl.pallas_call(functools.partial(attn_bwd_kernel, parts=len(gb)), in_spec...  14.3 us
  transfers between devices with their start and end apart: 71, of which 30 were waited for; matrix products, arithmetic and copies ran while one was open for 3% of the time, Pallas kernels for 29%

profile of v2, /device:TPU:0, one launch (start us, length us, event | category | flops | bytes accessed | tf_op | source)
XLA Modules:
  0.0 312.5 jit_solution(15700210485121303557)
XLA Ops:
  10.1 2.6 pick_rows.4
  14.0 2.6 pick_rows.5.keep
  16.7 2.6 pick_rows.6
  20.2 3.0 collective-permute-start.9
  28.5 2.6 pick_rows.7.keep
  41.5 5.5 %collective-permute-done.7.far1 = bf16[128,1024]{1,0:T(8,128)(2,1)S(1)} collective-permute-done((bf16[128,1024]{1,0:T(8,128)(2,1)}, bf16[128,1024]{1,0:T(8,128)(2,1)S(1)}, u32[]{:S(2)}, u32[]{:S(2)}) %collective-permute-start.7) | collective-permute-done | bytes 262176 | tf_op jit(solution)/shard_map/ppermute | solution.py:697
  47.1 4.2 %collective-permute-done.6.far0 = bf16[128,1024]{1,0:T(8,128)(2,1)} collective-permute-done((bf16[128,1024]{1,0:T(8,128)(2,1)}, bf16[128,1024]{1,0:T(8,128)(2,1)}, u32[]{:S(2)}, u32[]{:S(2)}) %collective-permute-start.6) | collective-permute-done | bytes 262176 | tf_op jit(solution)/shard_map/ppermute | solution.py:697
  55.2 2.6 collective-permute-done.10
  66.1 23.4 %collective-permute-done.13.far_own = bf16[144,1024]{1,0:T(8,128)(2,1)S(1)} collective-permute-done((bf16[144,1024]{1,0:T(8,128)(2,1)S(1)}, bf16[144,1024]{1,0:T(8,128)(2,1)S(1)}, u32[]{:S(2)}, u32[]{:S(2)}) %collective-permute-start.13) | collective-permute-done | bytes 294944 | tf_op jit(solution)/shard_map/ppermute | solution.py:697
  92.9 5.3 %attn_fwd.2 = (bf16[512,768]{1,0:T(8,128)(2,1)S(1)}, bf16[512,256]{1,0:T(8,128)(2,1)S(1)}, bf16[256,1024]{1,0:T(8,128)(2,1)S(1)}, bf16[256,1024]{1,0:T(8,128)(2,1)S(1)}) custom-call(s32[4]{0:T(128)S(1)} %add_add_fusion.order, bf16[256,1024]{1,0:T(8,128)(2,1)S(1)} %collective-permute-done.12.xa.refs_2_, ...), custom_call_target="tpu_custom_call" | custom-call | flops 1 | bytes 1 | tf_op jit(solution)/shard_map/attn_fwd/pallas_call | solution.py:474
  102.1 5.3 %attn_fwd.3 = (bf16[512,768]{1,0:T(8,128)(2,1)S(1)}, bf16[512,256]{1,0:T(8,128)(2,1)S(1)}, bf16[256,1024]{1,0:T(8,128)(2,1)S(1)}, bf16[256,1024]{1,0:T(8,128)(2,1)S(1)}) custom-call(s32[4]{0:T(128)S(1)} %pad_add_fusion.2.order, bf16[256,1024]{1,0:T(8,128)(2,1)S(1)} %get-tuple-element.126.xa.refs_0_, ...), custom_call_target="tpu_custom_call" | custom-call | flops 1 | bytes 1 | tf_op jit(solution)/shard_map/attn_fwd/pallas_call | solution.py:474
  109.5 5.8 %collective-permute-done.22.c = bf16[256,1024]{1,0:T(8,128)(2,1)S(1)} collective-permute-done((bf16[256,1024]{1,0:T(8,128)(2,1)S(1)}, bf16[256,1024]{1,0:T(8,128)(2,1)S(1)}, u32[]{:S(2)}, u32[]{:S(2)}) %collective-permute-start.22) | collective-permute-done | bytes 524320 | tf_op jit(solution)/shard_map/ppermute | solution.py:697
  118.1 8.4 %collective-permute-done.24.ga.refs_7_ = bf16[256,1024]{1,0:T(8,128)(2,1)S(1)} collective-permute-done((bf16[256,1024]{1,0:T(8,128)(2,1)S(1)}, bf16[256,1024]{1,0:T(8,128)(2,1)S(1)}, u32[]{:S(2)}, u32[]{:S(2)}) %collective-permute-start.24) | collective-permute-done | bytes 524320 | tf_op jit(solution)/shard_map/ppermute | solution.py:697
  127.1 9.8 %collective-permute-done.23.na.refs_2_ = bf16[256,1024]{1,0:T(8,128)(2,1)S(1)} collective-permute-done((bf16[256,1024]{1,0:T(8,128)(2,1)}, bf16[256,1024]{1,0:T(8,128)(2,1)S(1)}, u32[]{:S(2)}, u32[]{:S(2)}) %collective-permute-start.23) | collective-permute-done | bytes 524320 | tf_op jit(solution)/shard_map/ppermute | solution.py:697
  140.6 10.5 %mlp.2 = (bf16[512,1024]{1,0:T(8,128)(2,1)S(1)}, bf16[512,1024]{1,0:T(8,128)(2,1)}, bf16[256,1024]{1,0:T(8,128)(2,1)S(1)}, bf16[256,1024]{1,0:T(8,128)(2,1)S(1)}...) custom-call(bf16[256,1024]{1,0:T(8,128)(2,1)S(1)} %collective-permute-done.23.na.refs_2_, ...), custom_call_target="tpu_custom_call" | custom-call | flops 1 | bytes 1 | tf_op jit(solution)/shard_map/mlp/pallas_call | solution.py:588
  155.1 10.6 %mlp.3 = (bf16[512,1024]{1,0:T(8,128)(2,1)S(1)}, bf16[512,1024]{1,0:T(8,128)(2,1)}, bf16[256,1024]{1,0:T(8,128)(2,1)S(1)}, bf16[256,1024]{1,0:T(8,128)(2,1)S(1)}...) custom-call(bf16[256,1024]{1,0:T(8,128)(2,1)} %get-tuple-element.142.na.refs_0_, ...), custom_call_target="tpu_custom_call" | custom-call | flops 1 | bytes 1 | tf_op jit(solution)/shard_map/mlp/pallas_call | solution.py:588
  173.8 15.7 %mlp_grads.1 = bf16[2048,1024]{1,0:T(8,128)(2,1)} custom-call(bf16[256,1024]{1,0:T(8,128)(2,1)} %get-tuple-element.142.na.refs_0_, bf16[256,1024]{1,0:T(8,128)(2,1)S(1)} %collective-permute-done.31.refs_0_.refs_1_, bf16[256,1024]{1,0:T(8,128)(2,1)S(1)} %collective-permute-done.23.na.refs_2_, bf16[128,1024]{1,0:T(8,128)(2,1)S(1)} %copy-done.28, ...), custom_call_target="tpu_custom_call" | custom-call | flops 1 | bytes 1 | tf_op jit(solution)/shard_map/mlp_grads/pallas_call | solution.py:635
  194.1 7.1 %attn_bwd.2 = (bf16[512,768]{1,0:T(8,128)(2,1)S(1)}, bf16[256,1024]{1,0:T(8,128)(2,1)S(1)}, bf16[256,1024]{1,0:T(8,128)(2,1)S(1)}) custom-call(s32[4]{0:T(128)S(1)} %add_add_fusion.order, bf16[256,1024]{1,0:T(8,128)(2,1)S(1)} %collective-permute-done.40.ga.refs_7_, bf16[128,1024]{1,0:T(8,128)(2,1)S(1)} %collective-permute-done.42.refs_0_.refs_8_, ...), custom_call_target="tpu_custom_call" | custom-call | flops 1 | bytes 1 | tf_op jit(solution)/shard_map/attn_bwd/pallas_call | solution.py:530
  205.7 7.2 %attn_bwd.3 = (bf16[512,768]{1,0:T(8,128)(2,1)S(1)}, bf16[256,1024]{1,0:T(8,128)(2,1)S(1)}, bf16[256,1024]{1,0:T(8,128)(2,1)S(1)}) custom-call(s32[4]{0:T(128)S(1)} %pad_add_fusion.2.order, bf16[256,1024]{1,0:T(8,128)(2,1)} %get-tuple-element.156.ga.refs_5_, bf16[256,1024]{1,0:T(8,128)(2,1)S(1)} %collective-permute-done.46.refs_0_.refs_6_, ...), custom_call_target="tpu_custom_call" | custom-call | flops 1 | bytes 1 | tf_op jit(solution)/shard_map/attn_bwd/pallas_call | solution.py:530
  212.9 3.8 %collective-permute-done.41.c = bf16[256,1024]{1,0:T(8,128)(2,1)S(1)} collective-permute-done((bf16[256,1024]{1,0:T(8,128)(2,1)S(1)}, bf16[256,1024]{1,0:T(8,128)(2,1)S(1)}, u32[]{:S(2)}, u32[]{:S(2)}) %collective-permute-start.41) | collective-permute-done | bytes 524320 | tf_op jit(solution)/shard_map/ppermute | solution.py:697
  227.5 8.4 %attn_grads.1 = (bf16[128,1024]{1,0:T(8,128)(2,1)S(1)}, bf16[384,1024]{1,0:T(8,128)(2,1)}, f32[128,1024]{1,0:T(8,128)S(1)}, f32[128,1024]{1,0:T(8,128)S(1)}, f32...) custom-call(s32[5]{0:T(128)S(1)} %stack.86.info, bf16[256,1024]{1,0:T(8,128)(2,1)S(1)} %copy-done.14, ...), custom_call_target="tpu_custom_call" | custom-call | flops 1 | bytes 1 | tf_op jit(solution)/shard_map/attn_grads/pallas_call | solution.py:678
  243.0 4.7 %collective-permute-done.59 = bf16[128,1024]{1,0:T(8,128)(2,1)S(1)} collective-permute-done((bf16[128,1024]{1,0:T(8,128)(2,1)S(1)}, bf16[128,1024]{1,0:T(8,128)(2,1)S(1)}, u32[]{:S(2)}, u32[]{:S(2)}) %collective-permute-start.59) | collective-permute-done | bytes 262176 | tf_op jit(solution)/shard_map/ppermute | solution.py:697
  249.2 4.3 %place_rows.4.refs_4_ = bf16[8,256,1024]{2,1,0:T(8,128)(2,1)} custom-call(s32[4]{0:T(128)S(1)} %pad_add_fusion.2.order, bf16[8,256,128]{2,1,0:T(8,128)(2,1)S(1)} %fusion.1.onehot_t, bf16[256,1024]{1,0:T(8,128)(2,1)} %get-tuple-element.176.refs_0_, bf16[256,1024]{1,0:T(8,128)(2,1)} %collective-permute-done.53.refs_1_, bf16[8,256,1024]{2,1,0:T(8,128)(2,1)} %refs_3_.2), custom_call_target="tpu_custom_call" | custom-call | flops 1 | bytes 1 | tf_op jit(solution)/shard_map/place_rows/pallas_call | solution.py:126
  253.6 7.8 %collective-permute-start.60 = (bf16[128,1024]{1,0:T(8,128)(2,1)S(1)}, bf16[128,1024]{1,0:T(8,128)(2,1)S(1)}, u32[]{:S(2)}, u32[]{:S(2)}) collective-permute-start(bf16[128,1024]{1,0:T(8,128)(2,1)S(1)} %add_convert_fusion.2), channel_id=1, source_target_pairs={{16,0},{20,4},{24,8},{28,12},{0,16},{4,20},{8,24},{12,28},{17,1},{... | collective-permute-start | bytes 786440 | tf_op jit(solution)/shard_map/ppermute | solution.py:725
  262.5 3.6 %place_rows.5 = bf16[8,256,1024]{2,1,0:T(8,128)(2,1)} custom-call(s32[4]{0:T(128)S(1)} %add_add_fusion.order, bf16[8,256,128]{2,1,0:T(8,128)(2,1)S(1)} %fusion.1.onehot_t, bf16[256,1024]{1,0:T(8,128)(2,1)S(1)} %collective-permute-done.50.refs_0_, bf16[128,1024]{1,0:T(8,128)(2,1)S(1)} %collective-permute-done.51.refs_1_, ...), custom_call_target="tpu_custom_call", output_to_operand_aliasing={{}: (6, {})} | custom-call | flops 1 | bytes 1 | tf_op jit(solution)/shard_map/place_rows/pallas_call | solution.py:126
  268.4 3.6 %place_rows.6.refs_4_ = bf16[8,256,1024]{2,1,0:T(8,128)(2,1)} custom-call(s32[4]{0:T(128)S(1)} %pad_add_fusion.2.order, bf16[8,256,128]{2,1,0:T(8,128)(2,1)S(1)} %fusion.1.onehot_t, bf16[256,1024]{1,0:T(8,128)(2,1)S(1)} %get-tuple-element.177.refs_0_, bf16[256,1024]{1,0:T(8,128)(2,1)S(1)} %collective-permute-done.55.refs_1_, bf16[8,256,1024]{2,1,0:T(8,128)(2,1)} %refs_3_.3), custom_call_target="tpu_custom_call" | custom-call | flops 1 | bytes 1 | tf_op jit(solution)/shard_map/place_rows/pallas_call | solution.py:126
  274.1 3.0 collective-permute-start.61
  277.1 2.4 collective-permute-start.65
  279.5 3.6 %place_rows.7 = bf16[8,256,1024]{2,1,0:T(8,128)(2,1)} custom-call(s32[4]{0:T(128)S(1)} %add_add_fusion.order, bf16[8,256,128]{2,1,0:T(8,128)(2,1)S(1)} %fusion.1.onehot_t, bf16[256,1024]{1,0:T(8,128)(2,1)S(1)} %collective-permute-done.54.refs_0_, bf16[128,1024]{1,0:T(8,128)(2,1)S(1)} %collective-permute-done.56.refs_1_, ...), custom_call_target="tpu_custom_call", output_to_operand_aliasing={{}: (6, {})} | custom-call | flops 1 | bytes 1 | tf_op jit(solution)/shard_map/place_rows/pallas_call | solution.py:126
  283.2 4.9 %collective-permute-start.68 = (f32[8,1024]{1,0:T(8,128)S(1)}, f32[8,1024]{1,0:T(8,128)S(1)}, u32[]{:S(2)}, u32[]{:S(2)}) collective-permute-start(f32[8,1024]{1,0:T(8,128)S(1)} %add.138), channel_id=1, source_target_pairs={{16,0},{20,4},{24,8},{28,12},{0,16},{4,20},{8,24},{12,28},{17,1},{... | collective-permute-start | bytes 98312 | tf_op jit(solution)/shard_map/ppermute | solution.py:725
  288.1 3.8 %collective-permute-start.66 = (f32[8,1024]{1,0:T(8,128)S(1)}, f32[8,1024]{1,0:T(8,128)S(1)}, u32[]{:S(2)}, u32[]{:S(2)}) collective-permute-start(f32[8,1024]{1,0:T(8,128)S(1)} %add.138), channel_id=1, source_target_pairs={{8,0},{12,4},{16,8},{20,12},{24,16},{28,20},{0,24},{4,28},{9,1},{1... | collective-permute-start | bytes 98312 | tf_op jit(solution)/shard_map/ppermute | solution.py:725
  292.9 8.3 %collective-permute-done.62.p3 = bf16[128,1024]{1,0:T(8,128)(2,1)S(1)} collective-permute-done((bf16[128,1024]{1,0:T(8,128)(2,1)S(1)}, bf16[128,1024]{1,0:T(8,128)(2,1)S(1)}, u32[]{:S(2)}, u32[]{:S(2)}) %collective-permute-start.62) | collective-permute-done | bytes 262176 | tf_op jit(solution)/shard_map/ppermute | solution.py:725
  (331 shorter events, 100.4 us)
Async XLA Ops:
  7.2 132.5 %all-gather.2.cloned.1.call-start = ((), (), s32[]{:S(2)}) async-start(), calls=%async_computation.1 | async-start | bytes 4718592 | tf_op jit(solution)/shard_map/all_gather | solution.py:817
  23.2 28.1 %collective-permute-start.8 = (bf16[144,1024]{1,0:T(8,128)(2,1)S(1)}, bf16[144,1024]{1,0:T(8,128)(2,1)S(1)}, u32[]{:S(2)}, u32[]{:S(2)}) collective-permute-start(bf16[144,1024]{1,0:T(8,128)(2,1)S(1)} %pack_attn.1.refs_0_.near_own), channel_id=1, source_target_pairs={{8,0},{12,4},{16,8},{20,12},{24,16},{28,20},{0,24},{4,28},{9,1},{1... | collective-permute-start | bytes 884744 | tf_op jit(solution)/shard_map/ppermute | solution.py:725
  25.2 26.1 %collective-permute-start.4 = (bf16[144,1024]{1,0:T(8,128)(2,1)S(1)}, bf16[144,1024]{1,0:T(8,128)(2,1)S(1)}, u32[]{:S(2)}, u32[]{:S(2)}) collective-permute-start(bf16[144,1024]{1,0:T(8,128)(2,1)S(1)} %pack_attn.1.refs_0_.near_own), channel_id=1, source_target_pairs={{16,0},{20,4},{24,8},{28,12},{0,16},{4,20},{8,24},{12,28},{17,1},{... | collective-permute-start | bytes 884744 | tf_op jit(solution)/shard_map/ppermute | solution.py:725
  33.1 14.0 %collective-permute-start.7 = (bf16[128,1024]{1,0:T(8,128)(2,1)}, bf16[128,1024]{1,0:T(8,128)(2,1)S(1)}, u32[]{:S(2)}, u32[]{:S(2)}) collective-permute-start(bf16[128,1024]{1,0:T(8,128)(2,1)} %get-tuple-element.239), channel_id=1, source_target_pairs={{0,2},{1,3},{2,0},{3,1},{4,6},{5,7},{6,4},{7,5},{8,10},{9,11},{10,... | collective-permute-start | bytes 786440 | tf_op jit(solution)/shard_map/ppermute | solution.py:697
  36.5 14.8 %collective-permute-start.6 = (bf16[128,1024]{1,0:T(8,128)(2,1)}, bf16[128,1024]{1,0:T(8,128)(2,1)}, u32[]{:S(2)}, u32[]{:S(2)}) collective-permute-start(bf16[128,1024]{1,0:T(8,128)(2,1)} %get-tuple-element.240), channel_id=1, source_target_pairs={{0,2},{1,3},{2,0},{3,1},{4,6},{5,7},{6,4},{7,5},{8,10},{9,11},{10,... | collective-permute-start | bytes 786440 | tf_op jit(solution)/shard_map/ppermute | solution.py:697
  53.5 250.1 %reduce-scatter.2.cloned.1.call-start = ((), (), s32[]{:S(2)}) async-start(), calls=%async_computation.2 | async-start | bytes 4718592 | tf_op jit(solution)/shard_map/reduce_scatter | solution.py:894
  58.6 31.0 %collective-permute-start.14 = (bf16[384,1024]{1,0:T(8,128)(2,1)}, bf16[384,1024]{1,0:T(8,128)(2,1)S(1)}, u32[]{:S(2)}, u32[]{:S(2)}) collective-permute-start(bf16[384,1024]{1,0:T(8,128)(2,1)} %get-tuple-element.121.near), channel_id=1, source_target_pairs={{0,4},{4,0},{8,12},{12,8},{16,20},{20,16},{24,28},{28,24},{1,5},{5... | collective-permute-start | bytes 2359304 | tf_op jit(solution)/shard_map/ppermute | solution.py:697
  62.6 28.2 %collective-permute-start.12 = (bf16[256,1024]{1,0:T(8,128)(2,1)S(1)}, bf16[256,1024]{1,0:T(8,128)(2,1)S(1)}, u32[]{:S(2)}, u32[]{:S(2)}) collective-permute-start(bf16[256,1024]{1,0:T(8,128)(2,1)S(1)} %get-tuple-element.126.xa.refs_0_), channel_id=1, source_target_pairs={{0,2},{1,3},{2,0},{3,1},{4,6},{5,7},{6,4},{7,5},{8,10},{9,11},{10,... | collective-permute-start | bytes 1572872 | tf_op jit(solution)/shard_map/ppermute | solution.py:697
  64.2 25.3 %collective-permute-start.13 = (bf16[144,1024]{1,0:T(8,128)(2,1)S(1)}, bf16[144,1024]{1,0:T(8,128)(2,1)S(1)}, u32[]{:S(2)}, u32[]{:S(2)}) collective-permute-start(bf16[144,1024]{1,0:T(8,128)(2,1)S(1)} %pack_attn.1.refs_0_.near_own), channel_id=1, source_target_pairs={{0,4},{4,0},{8,12},{12,8},{16,20},{20,16},{24,28},{28,24},{1,5},{5... | collective-permute-start | bytes 884744 | tf_op jit(solution)/shard_map/ppermute | solution.py:697
  100.5 14.8 %collective-permute-start.22 = (bf16[256,1024]{1,0:T(8,128)(2,1)S(1)}, bf16[256,1024]{1,0:T(8,128)(2,1)S(1)}, u32[]{:S(2)}, u32[]{:S(2)}) collective-permute-start(bf16[256,1024]{1,0:T(8,128)(2,1)S(1)} %pad_maximum_fusion), channel_id=1, source_target_pairs={{0,2},{1,3},{2,0},{3,1},{4,6},{5,7},{6,4},{7,5},{8,10},{9,11},{10,... | collective-permute-start | bytes 1572872 | tf_op jit(solution)/shard_map/ppermute | solution.py:697
  108.1 18.4 %collective-permute-start.24 = (bf16[256,1024]{1,0:T(8,128)(2,1)S(1)}, bf16[256,1024]{1,0:T(8,128)(2,1)S(1)}, u32[]{:S(2)}, u32[]{:S(2)}) collective-permute-start(bf16[256,1024]{1,0:T(8,128)(2,1)S(1)} %get-tuple-element.131.ga.refs_5_), channel_id=1, source_target_pairs={{0,2},{1,3},{2,0},{3,1},{4,6},{5,7},{6,4},{7,5},{8,10},{9,11},{10,... | collective-permute-start | bytes 1572872 | tf_op jit(solution)/shard_map/ppermute | solution.py:697
  116.6 20.3 %collective-permute-start.23 = (bf16[256,1024]{1,0:T(8,128)(2,1)}, bf16[256,1024]{1,0:T(8,128)(2,1)S(1)}, u32[]{:S(2)}, u32[]{:S(2)}) collective-permute-start(bf16[256,1024]{1,0:T(8,128)(2,1)} %get-tuple-element.142.na.refs_0_), channel_id=1, source_target_pairs={{0,2},{1,3},{2,0},{3,1},{4,6},{5,7},{6,4},{7,5},{8,10},{9,11},{10,... | collective-permute-start | bytes 1572872 | tf_op jit(solution)/shard_map/ppermute | solution.py:697
  153.5 15.7 %collective-permute-start.35 = (bf16[256,1024]{1,0:T(8,128)(2,1)S(1)}, bf16[256,1024]{1,0:T(8,128)(2,1)S(1)}, u32[]{:S(2)}, u32[]{:S(2)}) collective-permute-start(bf16[256,1024]{1,0:T(8,128)(2,1)S(1)} %pad_maximum_fusion.1), channel_id=1, source_target_pairs={{0,2},{1,3},{2,0},{3,1},{4,6},{5,7},{6,4},{7,5},{8,10},{9,11},{10,... | collective-permute-start | bytes 1572872 | tf_op jit(solution)/shard_map/ppermute | solution.py:697
  172.5 17.0 %collective-permute-start.40 = (bf16[256,1024]{1,0:T(8,128)(2,1)}, bf16[256,1024]{1,0:T(8,128)(2,1)S(1)}, u32[]{:S(2)}, u32[]{:S(2)}) collective-permute-start(bf16[256,1024]{1,0:T(8,128)(2,1)} %get-tuple-element.156.ga.refs_5_), channel_id=1, source_target_pairs={{0,2},{1,3},{2,0},{3,1},{4,6},{5,7},{6,4},{7,5},{8,10},{9,11},{10,... | collective-permute-start | bytes 1572872 | tf_op jit(solution)/shard_map/ppermute | solution.py:697
  192.0 13.6 %collective-permute-start.46 = (bf16[256,1024]{1,0:T(8,128)(2,1)}, bf16[256,1024]{1,0:T(8,128)(2,1)S(1)}, u32[]{:S(2)}, u32[]{:S(2)}) collective-permute-start(bf16[256,1024]{1,0:T(8,128)(2,1)} %get-tuple-element.156.ga.refs_5_), channel_id=1, source_target_pairs={{0,1},{1,0},{2,3},{3,2},{4,5},{5,4},{6,7},{7,6},{8,9},{9,8},{10,11... | collective-permute-start | bytes 1572872 | tf_op jit(solution)/shard_map/ppermute | solution.py:697
  201.9 14.8 %collective-permute-start.41 = (bf16[256,1024]{1,0:T(8,128)(2,1)S(1)}, bf16[256,1024]{1,0:T(8,128)(2,1)S(1)}, u32[]{:S(2)}, u32[]{:S(2)}) collective-permute-start(bf16[256,1024]{1,0:T(8,128)(2,1)S(1)} %pad_maximum_fusion.2), channel_id=1, source_target_pairs={{0,2},{1,3},{2,0},{3,1},{4,6},{5,7},{6,4},{7,5},{8,10},{9,11},{10,... | collective-permute-start | bytes 1572872 | tf_op jit(solution)/shard_map/ppermute | solution.py:697
  202.8 14.0 %collective-permute-start.37 = (bf16[128,1024]{1,0:T(8,128)(2,1)S(1)}, bf16[128,1024]{1,0:T(8,128)(2,1)S(1)}, u32[]{:S(2)}, u32[]{:S(2)}) collective-permute-start(bf16[128,1024]{1,0:T(8,128)(2,1)S(1)} %get-tuple-element.219), channel_id=1, source_target_pairs={{0,1},{1,0},{2,3},{3,2},{4,5},{5,4},{6,7},{7,6},{8,9},{9,8},{10,11... | collective-permute-start | bytes 786440 | tf_op jit(solution)/shard_map/ppermute | solution.py:697
  202.9 13.9 %collective-permute-start.36 = (bf16[128,1024]{1,0:T(8,128)(2,1)S(1)}, bf16[128,1024]{1,0:T(8,128)(2,1)S(1)}, u32[]{:S(2)}, u32[]{:S(2)}) collective-permute-start(bf16[128,1024]{1,0:T(8,128)(2,1)S(1)} %get-tuple-element.220), channel_id=1, source_target_pairs={{0,1},{1,0},{2,3},{3,2},{4,5},{5,4},{6,7},{7,6},{8,9},{9,8},{10,11... | collective-permute-start | bytes 786440 | tf_op jit(solution)/shard_map/ppermute | solution.py:697
  204.4 33.8 %collective-permute-start.49 = (bf16[256,1024]{1,0:T(8,128)(2,1)}, bf16[256,1024]{1,0:T(8,128)(2,1)}, u32[]{:S(2)}, u32[]{:S(2)}) collective-permute-start(bf16[256,1024]{1,0:T(8,128)(2,1)} %pad_maximum_fusion.3), channel_id=1, source_target_pairs={{0,2},{1,3},{2,0},{3,1},{4,6},{5,7},{6,4},{7,5},{8,10},{9,11},{10,... | collective-permute-start | bytes 1572872 | tf_op jit(solution)/shard_map/ppermute | solution.py:697
  218.3 23.4 %collective-permute-start.50 = (bf16[256,1024]{1,0:T(8,128)(2,1)}, bf16[256,1024]{1,0:T(8,128)(2,1)S(1)}, u32[]{:S(2)}, u32[]{:S(2)}) collective-permute-start(bf16[256,1024]{1,0:T(8,128)(2,1)} %get-tuple-element.176.refs_0_), channel_id=1, source_target_pairs={{0,2},{1,3},{2,0},{3,1},{4,6},{5,7},{6,4},{7,5},{8,10},{9,11},{10,... | collective-permute-start | bytes 1572872 | tf_op jit(solution)/shard_map/ppermute | solution.py:697
  220.0 16.7 %collective-permute-start.48 = (bf16[128,1024]{1,0:T(8,128)(2,1)}, bf16[128,1024]{1,0:T(8,128)(2,1)}, u32[]{:S(2)}, u32[]{:S(2)}) collective-permute-start(bf16[128,1024]{1,0:T(8,128)(2,1)} %get-tuple-element.207), channel_id=1, source_target_pairs={{0,1},{1,0},{2,3},{3,2},{4,5},{5,4},{6,7},{7,6},{8,9},{9,8},{10,11... | collective-permute-start | bytes 786440 | tf_op jit(solution)/shard_map/ppermute | solution.py:697
  220.0 27.8 %collective-permute-start.53 = (bf16[256,1024]{1,0:T(8,128)(2,1)}, bf16[256,1024]{1,0:T(8,128)(2,1)}, u32[]{:S(2)}, u32[]{:S(2)}) collective-permute-start(bf16[256,1024]{1,0:T(8,128)(2,1)} %get-tuple-element.176.refs_0_), channel_id=1, source_target_pairs={{0,1},{1,0},{2,3},{3,2},{4,5},{5,4},{6,7},{7,6},{8,9},{9,8},{10,11... | collective-permute-start | bytes 1572872 | tf_op jit(solution)/shard_map/ppermute | solution.py:697
  220.5 18.2 %collective-permute-start.47 = (bf16[128,1024]{1,0:T(8,128)(2,1)}, bf16[128,1024]{1,0:T(8,128)(2,1)}, u32[]{:S(2)}, u32[]{:S(2)}) collective-permute-start(bf16[128,1024]{1,0:T(8,128)(2,1)} %get-tuple-element.208), channel_id=1, source_target_pairs={{0,1},{1,0},{2,3},{3,2},{4,5},{5,4},{6,7},{7,6},{8,9},{9,8},{10,11... | collective-permute-start | bytes 786440 | tf_op jit(solution)/shard_map/ppermute | solution.py:697
  238.2 30.2 %collective-permute-start.58 = (bf16[384,1024]{1,0:T(8,128)(2,1)}, bf16[384,1024]{1,0:T(8,128)(2,1)S(1)}, u32[]{:S(2)}, u32[]{:S(2)}) collective-permute-start(bf16[384,1024]{1,0:T(8,128)(2,1)} %get-tuple-element.180), channel_id=1, source_target_pairs={{0,4},{4,0},{8,12},{12,8},{16,20},{20,16},{24,28},{28,24},{1,5},{5... | collective-permute-start | bytes 2359304 | tf_op jit(solution)/shard_map/ppermute | solution.py:697
  241.6 26.8 %collective-permute-start.55 = (bf16[256,1024]{1,0:T(8,128)(2,1)S(1)}, bf16[256,1024]{1,0:T(8,128)(2,1)S(1)}, u32[]{:S(2)}, u32[]{:S(2)}) collective-permute-start(bf16[256,1024]{1,0:T(8,128)(2,1)S(1)} %get-tuple-element.177.refs_0_), channel_id=1, source_target_pairs={{0,1},{1,0},{2,3},{3,2},{4,5},{5,4},{6,7},{7,6},{8,9},{9,8},{10,11... | collective-permute-start | bytes 1572872 | tf_op jit(solution)/shard_map/ppermute | solution.py:697
  241.7 30.3 %collective-permute-start.54 = (bf16[256,1024]{1,0:T(8,128)(2,1)S(1)}, bf16[256,1024]{1,0:T(8,128)(2,1)S(1)}, u32[]{:S(2)}, u32[]{:S(2)}) collective-permute-start(bf16[256,1024]{1,0:T(8,128)(2,1)S(1)} %get-tuple-element.177.refs_0_), channel_id=1, source_target_pairs={{0,2},{1,3},{2,0},{3,1},{4,6},{5,7},{6,4},{7,5},{8,10},{9,11},{10,... | collective-permute-start | bytes 1572872 | tf_op jit(solution)/shard_map/ppermute | solution.py:697
  253.6 34.6 %collective-permute-start.60 = (bf16[128,1024]{1,0:T(8,128)(2,1)S(1)}, bf16[128,1024]{1,0:T(8,128)(2,1)S(1)}, u32[]{:S(2)}, u32[]{:S(2)}) collective-permute-start(bf16[128,1024]{1,0:T(8,128)(2,1)S(1)} %add_convert_fusion.2), channel_id=1, source_target_pairs={{16,0},{20,4},{24,8},{28,12},{0,16},{4,20},{8,24},{12,28},{17,1},{... | collective-permute-start | bytes 786440 | tf_op jit(solution)/shard_map/ppermute | solution.py:725
  272.8 28.4 %collective-permute-start.62 = (bf16[128,1024]{1,0:T(8,128)(2,1)S(1)}, bf16[128,1024]{1,0:T(8,128)(2,1)S(1)}, u32[]{:S(2)}, u32[]{:S(2)}) collective-permute-start(bf16[128,1024]{1,0:T(8,128)(2,1)S(1)} %get-tuple-element.201), channel_id=1, source_target_pairs={{8,0},{12,4},{16,8},{20,12},{24,16},{28,20},{0,24},{4,28},{9,1},{1... | collective-permute-start | bytes 786440 | tf_op jit(solution)/shard_map/ppermute | solution.py:725
  274.1 27.1 %collective-permute-start.61 = (bf16[128,1024]{1,0:T(8,128)(2,1)S(1)}, bf16[128,1024]{1,0:T(8,128)(2,1)S(1)}, u32[]{:S(2)}, u32[]{:S(2)}) collective-permute-start(bf16[128,1024]{1,0:T(8,128)(2,1)S(1)} %get-tuple-element.202), channel_id=1, source_target_pairs={{24,0},{28,4},{0,8},{4,12},{8,16},{12,20},{16,24},{20,28},{25,1},{... | collective-permute-start | bytes 786440 | tf_op jit(solution)/shard_map/ppermute | solution.py:725
  283.2 19.8 %collective-permute-start.68 = (f32[8,1024]{1,0:T(8,128)S(1)}, f32[8,1024]{1,0:T(8,128)S(1)}, u32[]{:S(2)}, u32[]{:S(2)}) collective-permute-start(f32[8,1024]{1,0:T(8,128)S(1)} %add.138), channel_id=1, source_target_pairs={{16,0},{20,4},{24,8},{28,12},{0,16},{4,20},{8,24},{12,28},{17,1},{... | collective-permute-start | bytes 98312 | tf_op jit(solution)/shard_map/ppermute | solution.py:725
  288.1 14.9 %collective-permute-start.67 = (f32[8,1024]{1,0:T(8,128)S(1)}, f32[8,1024]{1,0:T(8,128)S(1)}, u32[]{:S(2)}, u32[]{:S(2)}) collective-permute-start(f32[8,1024]{1,0:T(8,128)S(1)} %add.138), channel_id=1, source_target_pairs={{24,0},{28,4},{0,8},{4,12},{8,16},{12,20},{16,24},{20,28},{25,1},{... | collective-permute-start | bytes 98312 | tf_op jit(solution)/shard_map/ppermute | solution.py:725
  288.1 14.9 %collective-permute-start.66 = (f32[8,1024]{1,0:T(8,128)S(1)}, f32[8,1024]{1,0:T(8,128)S(1)}, u32[]{:S(2)}, u32[]{:S(2)}) collective-permute-start(f32[8,1024]{1,0:T(8,128)S(1)} %add.138), channel_id=1, source_target_pairs={{8,0},{12,4},{16,8},{20,12},{24,16},{28,20},{0,24},{4,28},{9,1},{1... | collective-permute-start | bytes 98312 | tf_op jit(solution)/shard_map/ppermute | solution.py:725
  (109 other events, 923.3 us)
Sparse Core Ops, SparseCore 0:
  53.6 79.0 all-gather.1
  189.7 110.3 reduce-scatter.1

commit v3 on v2

--- a/solution.py
+++ b/solution.py
@@ -49,7 +49,7 @@
 
 
 def params(mib):
-    return pltpu.CompilerParams(vmem_limit_bytes=max(mib, 48) << 20)
+    return pltpu.CompilerParams(vmem_limit_bytes=max(mib, 40) << 20)
 
 
 def tiles(total, width, step):
@@ -437,18 +437,17 @@
         at += part.shape[0]
 
 
-def attn_fwd_kernel(order, xa, *refs, parts):
-    w, bias, qkv, ctx, pa, pb, xb = refs[parts:]
-    fill(xb, refs[:parts])
-    half = xa.shape[0]
+def attn_fwd_kernel(order, *refs, parts):
+    w, bias, qkv, ctx, pa, pb, x = refs[parts:]
+    fill(x, refs[:parts])
+    half = pa.shape[0]
     local = ctx.shape[1]
     routed = bias.shape[1]
     heads = local // HEAD_DIM
     masks = head_masks(local)
 
     def project(cols, j):
-        qkv[0:half, cols] = mm(xa[...], w[:, cols]).astype(BF16)
-        qkv[half : 2 * half, cols] = mm(xb[...], w[:, cols]).astype(BF16)
+        qkv[:, cols] = mm(x[...], w[:, cols]).astype(BF16)
 
     tiles(3 * local, local, project)
 
@@ -459,12 +458,12 @@
         probs = seq_probs(spread(q, masks), k, bias[order[s]], heads).astype(BF16)
         ctx[rows, :] = mm(side_by_side(probs, heads), spread(v, masks)).astype(BF16)
 
-    tiles(2 * half, routed, seq)
+    tiles(qkv.shape[0], routed, seq)
 
     def emit(cols, j):
-        wo = w[cols, 3 * local : 4 * local]
-        pa[:, cols] = mm_t(ctx[0:half, :], wo).astype(BF16)
-        pb[:, cols] = mm_t(ctx[half : 2 * half, :], wo).astype(BF16)
+        part = mm_t(ctx[...], w[cols, 3 * local : 4 * local]).astype(BF16)
+        pa[:, cols] = part[0:half]
+        pb[:, cols] = part[half:]
 
     tiles(pa.shape[1], 256, emit)
 
@@ -472,7 +471,7 @@
 def attn_fwd(xa, xb, w, bias, order, local):
     rows, width = xa.shape
     return pl.pallas_call(
-        functools.partial(attn_fwd_kernel, parts=len(xb)),
+        functools.partial(attn_fwd_kernel, parts=1 + len(xb)),
         in_specs=[SMEM_SPEC] + [VMEM_SPEC] * (3 + len(xb)),
         out_specs=[VMEM_SPEC] * 4,
         out_shape=[
@@ -481,24 +480,22 @@
             shape((rows, width), BF16),
             shape((rows, width), BF16),
         ],
-        scratch_shapes=[pltpu.VMEM((rows, width), BF16)],
+        scratch_shapes=[pltpu.VMEM((2 * rows, width), BF16)],
         compiler_params=params(12),
         cost_estimate=COST,
         name="attn_fwd",
     )(order, xa, *xb, w, bias)
 
 
-def attn_bwd_kernel(order, ga, *refs, parts):
-    w, qkv, bias, dqkv, fa, fb, cg, gb = refs[parts:]
-    fill(gb, refs[:parts])
-    half = ga.shape[0]
+def attn_bwd_kernel(order, *refs, parts):
+    w, qkv, bias, dqkv, fa, fb, cg, g = refs[parts:]
+    fill(g, refs[:parts])
+    half = fa.shape[0]
     local = cg.shape[1]
     routed = bias.shape[1]
     heads = local // HEAD_DIM
     masks = head_masks(local)
-    wo = w[:, 3 * local : 4 * local]
-    cg[0:half, :] = mm(ga[...], wo).astype(BF16)
-    cg[half : 2 * half, :] = mm(gb[...], wo).astype(BF16)
+    cg[...] = mm(g[...], w[:, 3 * local : 4 * local]).astype(BF16)
 
     def seq(rows, s):
         q4 = spread(qkv[rows, 0:local], masks)
@@ -515,12 +512,12 @@
         dqkv[rows, 0:local] = dq.astype(BF16)
         dqkv[rows, local : 2 * local] = (t_mm(score_grad, q4) * scale).astype(BF16)
 
-    tiles(2 * half, routed, seq)
+    tiles(qkv.shape[0], routed, seq)
 
     def emit(cols, j):
-        wj = w[cols, 0 : 3 * local]
-        fa[:, cols] = mm_t(dqkv[0:half, :], wj).astype(BF16)
-        fb[:, cols] = mm_t(dqkv[half : 2 * half, :], wj).astype(BF16)
+        part = mm_t(dqkv[...], w[cols, 0 : 3 * local]).astype(BF16)
+        fa[:, cols] = part[0:half]
+        fb[:, cols] = part[half:]
 
     tiles(fa.shape[1], 256, emit)
 
@@ -528,7 +525,7 @@
 def attn_bwd(ga, gb, w, qkv, bias, order, local):
     rows, width = ga.shape
     return pl.pallas_call(
-        functools.partial(attn_bwd_kernel, parts=len(gb)),
+        functools.partial(attn_bwd_kernel, parts=1 + len(gb)),
         in_specs=[SMEM_SPEC] + [VMEM_SPEC] * (4 + len(gb)),
         out_specs=[VMEM_SPEC] * 3,
         out_shape=[
@@ -536,48 +533,51 @@
             shape((rows, width), BF16),
             shape((rows, width), BF16),
         ],
-        scratch_shapes=[pltpu.VMEM((2 * rows, local), BF16), pltpu.VMEM((rows, width), BF16)],
+        scratch_shapes=[
+            pltpu.VMEM((2 * rows, local), BF16),
+            pltpu.VMEM((2 * rows, width), BF16),
+        ],
         compiler_params=params(12),
         cost_estimate=COST,
         name="attn_bwd",
     )(order, ga, *gb, w, qkv, bias)
 
 
-def mlp_kernel(na, ga, *refs, parts):
-    w, act, ug, da, db, ma, mb, nb, gb = refs[2 * parts :]
-    fill(nb, refs[:parts])
-    fill(gb, refs[parts : 2 * parts])
-    rows, width = na.shape
+def mlp_kernel(*refs, parts):
+    w, act, ug, da, db, ma, mb, n, g = refs[2 * parts :]
+    fill(n, refs[:parts])
+    fill(g, refs[parts : 2 * parts])
+    rows, width = da.shape
     part, both, ff = w.shape
     depth = both // 2
 
     def up(cols, j):
-        wu = w[:, 0:depth, cols].reshape(width, -1)
-        wd = w[:, depth:both, cols].reshape(width, -1)
-        for n, g, at in ((na, ga, 0), (nb, gb, rows)):
-            x = mm(n[...], wu)
-            inner = jnp.tanh(GELU_C * (x + GELU_A * (x * x * x)))
-            half_in = 0.5 * (1.0 + inner)
-            act[at : at + rows, cols] = (x * half_in).astype(BF16)
-            slope = half_in + (0.5 * GELU_C) * x * (1.0 - inner * inner) * (
-                1.0 + (3.0 * GELU_A) * (x * x)
-            )
-            ug[at : at + rows, cols] = (mm(g[...], wd) * slope).astype(BF16)
+        x = mm(n[...], w[:, 0:depth, cols].reshape(width, -1))
+        inner = jnp.tanh(GELU_C * (x + GELU_A * (x * x * x)))
+        half_in = 0.5 * (1.0 + inner)
+        act[:, cols] = (x * half_in).astype(BF16)
+        slope = half_in + (0.5 * GELU_C) * x * (1.0 - inner * inner) * (
+            1.0 + (3.0 * GELU_A) * (x * x)
+        )
+        grad = mm(g[...], w[:, depth:both, cols].reshape(width, -1))
+        ug[:, cols] = (grad * slope).astype(BF16)
 
     tiles(ff, 256, up)
     group = part * 256 // width
 
     def back(cols, j):
         wu = w[pl.ds(j * group, group), 0:depth, :].reshape(256, -1)
-        da[:, cols] = mm_t(ug[0:rows, :], wu).astype(BF16)
-        db[:, cols] = mm_t(ug[rows : 2 * rows, :], wu).astype(BF16)
+        out = mm_t(ug[...], wu).astype(BF16)
+        da[:, cols] = out[0:rows]
+        db[:, cols] = out[rows:]
 
     tiles(width, 256, back)
 
     def down(cols, j):
         wd = w[pl.ds(j * group, group), depth:both, :].reshape(256, -1)
-        ma[:, cols] = mm_t(act[0:rows, :], wd).astype(BF16)
-        mb[:, cols] = mm_t(act[rows : 2 * rows, :], wd).astype(BF16)
+        out = mm_t(act[...], wd).astype(BF16)
+        ma[:, cols] = out[0:rows]
+        mb[:, cols] = out[rows:]
 
     tiles(width, 256, down)
 
@@ -586,15 +586,15 @@
     rows, width = na.shape
     ff = w.shape[2]
     return pl.pallas_call(
-        functools.partial(mlp_kernel, parts=len(nb)),
+        functools.partial(mlp_kernel, parts=1 + len(nb)),
         in_specs=[VMEM_SPEC] * (3 + 2 * len(nb)),
         out_specs=[VMEM_SPEC] * 6,
         out_shape=[shape((2 * rows, ff), BF16)] * 2 + [shape((rows, width), BF16)] * 4,
-        scratch_shapes=[pltpu.VMEM((rows, width), BF16)] * 2,
+        scratch_shapes=[pltpu.VMEM((2 * rows, width), BF16)] * 2,
         compiler_params=params(16),
         cost_estimate=COST,
         name="mlp",
-    )(na, ga, *nb, *gb, w)
+    )(na, *nb, ga, *gb, w)
 
 
 def turn(xt, pieces, cols):
@@ -610,23 +610,22 @@
     un, uf, an, af, out, xt = refs[2 * pieces :]
     half = un.shape[0]
     width = normed[0].shape[1]
-    group = 256 // depth
-
-    def columns(cols, z):
-        for side, (xs, near, far) in enumerate(((normed, un, uf), (grads, an, af))):
-            turn(xt, xs, cols)
-
-            def block(ncols, j, near=near, far=far, side=side):
-                total = mm(xt[:, 0:half], near[:, ncols])
-                total = total + mm(xt[:, half:], far[:, ncols])
-                for i in range(group):
-                    at = pl.multiple_of((z * group + i) * 2 * depth + side * depth, depth)
-                    part = total[i * depth : (i + 1) * depth]
-                    out[pl.ds(at, depth), ncols] = part.astype(BF16)
-
-            tiles(near.shape[1], 256, block)
-
-    tiles(width, 256, columns)
+    for side, (xs, near, far) in enumerate(((normed, un, uf), (grads, an, af))):
+        tiles(
+            width,
+            256,
+            lambda cols, j, xs=xs: turn(
+                xt.at[pl.ds(pl.multiple_of(j * 256, 256), 256), :], xs, cols
+            ),
+        )
+
+        def block(ncols, j, near=near, far=far, side=side):
+            total = mm(xt[:, 0:half], near[:, ncols]) + mm(xt[:, half:], far[:, ncols])
+            for f in range(width // depth):
+                at = (2 * f + side) * depth
+                out[at : at + depth, ncols] = total[f * depth : (f + 1) * depth].astype(BF16)
+
+        tiles(near.shape[1], 256, block)
 
 
 def mlp_grads(normed, grads, ug, act, depth):
@@ -637,7 +636,7 @@
         in_specs=[VMEM_SPEC] * (2 * len(normed) + 4),
         out_specs=VMEM_SPEC,
         out_shape=shape((2 * width, ff), BF16),
-        scratch_shapes=[pltpu.VMEM((256, 2 * rows), BF16)],
+        scratch_shapes=[pltpu.VMEM((width, 2 * rows), BF16)],
         compiler_params=params(20),
         cost_estimate=COST,
         name="mlp_grads",
@@ -652,24 +651,25 @@
     depth = first.shape[0]
     count = len(keeps)
     low = info[count] == 0
-    for o in range(count):
-        cols = pl.ds(pl.multiple_of(info[o] * 256, 256), 256)
-        send, row = (first, 0) if o == 0 else (others, (o - 1) * depth)
-        for lane, wide, xs, near, far in (
-            (0, 3 * local, normed, dn, df),
-            (3 * local, local, grads, cn, cf),
-        ):
-            turn(xt, xs, cols)
-
-            def block(ncols, j, near=near, far=far, lane=lane, send=send, row=row, o=o):
-                total = mm(xt[:, 0:half], near[:, ncols])
-                total = total + mm(xt[:, half:], far[:, ncols])
-                one, two = total[0:depth], total[depth : 2 * depth]
-                dst = pl.ds(pl.multiple_of(j * 256, 256) + lane, 256)
+    for lane, wide, xs, near, far in (
+        (0, 3 * local, normed, dn, df),
+        (3 * local, local, grads, cn, cf),
+    ):
+        for o in range(count):
+            cols = pl.ds(pl.multiple_of(info[o] * 256, 256), 256)
+            turn(xt.at[o * 256 : (o + 1) * 256, :], xs, cols)
+
+        def block(ncols, j, near=near, far=far, lane=lane):
+            total = mm(xt[:, 0:half], near[:, ncols]) + mm(xt[:, half:], far[:, ncols])
+            dst = pl.ds(pl.multiple_of(j * 256, 256) + lane, 256)
+            for o in range(count):
+                one = total[o * 256 : o * 256 + depth]
+                two = total[o * 256 + depth : (o + 1) * 256]
+                send, row = (first, 0) if o == 0 else (others, (o - 1) * depth)
                 send[row : row + depth, dst] = jnp.where(low, two, one).astype(BF16)
                 keeps[o][:, dst] = jnp.where(low, one, two)
 
-            tiles(wide, 256, block)
+        tiles(wide, 256, block)
 
 
 def attn_grads(normed, grads, dqkv, ctx, info, depth):
@@ -684,7 +684,7 @@
             shape(((count - 1) * depth, 4 * local), BF16),
         ]
         + [shape((depth, 4 * local), F32)] * count,
-        scratch_shapes=[pltpu.VMEM((256, 2 * rows), BF16)],
+        scratch_shapes=[pltpu.VMEM((count * 256, 2 * rows), BF16)],
         compiler_params=params(14),
         cost_estimate=COST,
         name="attn_grads",
@@ -848,7 +848,9 @@
         attn_w = lax.all_gather(attn_piece, "fsdp", axis=0, tiled=True)
     n3 = pair_swap(after(n2, attn_w))
 
-    qkv_far, ctx_far, p2, p3 = attn_fwd(n2, n3, attn_w, bias, order_far, local)
+    qkv_far, ctx_far, p2, p3 = attn_fwd(
+        after(n2, g2), n3, attn_w, bias, order_far, local
+    )
     attn_sum = pair_sum(p2, p3)
     attn_x = swap(attn_sum, "tensor", 2)
     qkv_near, ctx_near, p0, p1 = attn_fwd(

time: 314 us -> 304 us (0.968)
  Pallas kernels: 112 us -> 93.4 us
  waiting for transfers between devices: 90.7 us -> 101 us
  starting transfers between devices: 63.7 us -> 54.4 us
  local copies, waits for them, and re-layouts: 24.5 us -> 32.9 us
    ppermute x9, starting transfers between devices: 26.9 us -> 18.3 us  [z_move(): return lax.ppermute(x, 'fsdp', z_perm(lax.axis_size('fsdp'), shift))]
    unnamed x140 -> x154, local copies, waits for them, and re-layouts: 16.9 us -> 25.4 us
    pallas_call x1, Pallas kernels: 15.7 us -> 7.38 us  [mlp_grads(): pl.pallas_call(functools.partial(mlp_grads_kernel, depth=depth, pieces=le...]
    ppermute x9, waiting for transfers between devices: 9.81 us -> 16.7 us  [z_move(): return lax.ppermute(x, 'fsdp', z_perm(lax.axis_size('fsdp'), shift))]
    pallas_call x6, Pallas kernels: 46 us -> 39.1 us  [the longest x2 15.4 us: mlp_both(): pl.pallas_call(functools.partial(mlp_kernel, parts=1 + len(nb)), in_specs...]
    pallas_call x1, Pallas kernels: 8.37 us -> 4.98 us  [attn_grads(): pl.pallas_call(functools.partial(attn_grads_kernel, pieces=len(normed)),...]
  transfers between devices with their start and end apart: 71 -> 71, of which waited for: 30 -> 34; matrix products, arithmetic and copies ran while one was open for 3% -> 3% of each run, Pallas kernels for 29% -> 25%
where the time goes in v3:
time: 304 us; the launch traced here: 302 us
  waiting for transfers between devices  101 us (33%)
  Pallas kernels  93.4 us (31%)
  starting transfers between devices  54.4 us (18%)
  local copies, waits for them, and re-layouts  32.9 us (11%)
  between operations  15.2 us (5%)
  other arithmetic  5.36 us (2%)
    ppermute x60, waiting for transfers between devices, swap(): return lax.ppermute(x, axis, [(i, i ^ mask) for i in range(size)])  82.1 us
    ppermute x60, starting transfers between devices, swap(): return lax.ppermute(x, axis, [(i, i ^ mask) for i in range(size)])  36 us
    unnamed x154, local copies, waits for them, and re-layouts  25.4 us
    ppermute x9, starting transfers between devices, z_move(): return lax.ppermute(x, 'fsdp', z_perm(lax.axis_size('fsdp'), shift))  18.3 us
    ppermute x9, waiting for transfers between devices, z_move(): return lax.ppermute(x, 'fsdp', z_perm(lax.axis_size('fsdp'), shift))  16.7 us
    pallas_call x2, Pallas kernels, mlp_both(): pl.pallas_call(functools.partial(mlp_kernel, parts=1 + len(nb)), in_specs...  15.4 us
    pallas_call x4, Pallas kernels, place_rows(): pl.pallas_call(functools.partial(place_kernel, blocks=len(rows)), in_spec...  15.1 us
    pallas_call x2, Pallas kernels, attn_bwd(): pl.pallas_call(functools.partial(attn_bwd_kernel, parts=1 + len(gb)), in_...  13 us
  transfers between devices with their start and end apart: 71, of which 34 were waited for; matrix products, arithmetic and copies ran while one was open for 3% of the time, Pallas kernels for 25%

profile of v3, /device:TPU:0, one launch (start us, length us, event | category | flops | bytes accessed | tf_op | source)
XLA Modules:
  0.0 302.4 jit_solution(2675419541498417679)
XLA Ops:
  10.1 2.6 pick_rows.4
  14.0 2.6 pick_rows.5.keep
  16.7 2.6 pick_rows.6
  20.2 3.0 %collective-permute-start.9 = (bf16[144,1024]{1,0:T(8,128)(2,1)S(1)}, bf16[144,1024]{1,0:T(8,128)(2,1)S(1)}, u32[]{:S(2)}, u32[]{:S(2)}) collective-permute-start(bf16[144,1024]{1,0:T(8,128)(2,1)S(1)} %pack_attn.1.refs_0_.near_own), channel_id=1, source_target_pairs={{24,0},{28,4},{0,8},{4,12},{8,16},{12,20},{16,24},{20,28},{25,1},{... | collective-permute-start | bytes 884744 | tf_op jit(solution)/shard_map/ppermute | solution.py:725
  28.5 2.6 pick_rows.7.keep
  41.5 5.6 %collective-permute-done.7.far1 = bf16[128,1024]{1,0:T(8,128)(2,1)} collective-permute-done((bf16[128,1024]{1,0:T(8,128)(2,1)}, bf16[128,1024]{1,0:T(8,128)(2,1)}, u32[]{:S(2)}, u32[]{:S(2)}) %collective-permute-start.7) | collective-permute-done | bytes 262176 | tf_op jit(solution)/shard_map/ppermute | solution.py:697
  47.2 4.1 %collective-permute-done.6.far0 = bf16[128,1024]{1,0:T(8,128)(2,1)} collective-permute-done((bf16[128,1024]{1,0:T(8,128)(2,1)}, bf16[128,1024]{1,0:T(8,128)(2,1)}, u32[]{:S(2)}, u32[]{:S(2)}) %collective-permute-start.6) | collective-permute-done | bytes 262176 | tf_op jit(solution)/shard_map/ppermute | solution.py:697
  65.3 10.1 %collective-permute-done.12.refs_0_.refs_2_ = bf16[256,1024]{1,0:T(8,128)(2,1)S(1)} collective-permute-done((bf16[256,1024]{1,0:T(8,128)(2,1)S(1)}, bf16[256,1024]{1,0:T(8,128)(2,1)S(1)}, u32[]{:S(2)}, u32[]{:S(2)}) %collective-permute-start.12) | collective-permute-done | bytes 524320 | tf_op jit(solution)/shard_map/ppermute | solution.py:697
  76.9 11.0 %collective-permute-done.14.far_own = bf16[144,1024]{1,0:T(8,128)(2,1)S(1)} collective-permute-done((bf16[144,1024]{1,0:T(8,128)(2,1)S(1)}, bf16[144,1024]{1,0:T(8,128)(2,1)S(1)}, u32[]{:S(2)}, u32[]{:S(2)}) %collective-permute-start.14) | collective-permute-done | bytes 294944 | tf_op jit(solution)/shard_map/ppermute | solution.py:697
  91.2 5.4 %attn_fwd.2 = (bf16[512,768]{1,0:T(8,128)(2,1)S(1)}, bf16[512,256]{1,0:T(8,128)(2,1)S(1)}, bf16[256,1024]{1,0:T(8,128)(2,1)S(1)}, bf16[256,1024]{1,0:T(8,128)(2,1)S(1)}) custom-call(s32[4]{0:T(128)S(1)} %add_add_fusion.order, bf16[256,1024]{1,0:T(8,128)(2,1)S(1)} %collective-permute-done.12.refs_0_.refs_2_, ...), custom_call_target="tpu_custom_call" | custom-call | flops 1 | bytes 1 | tf_op jit(solution)/shard_map/attn_fwd/pallas_call | solution.py:473
  100.6 5.4 %attn_fwd.3 = (bf16[512,768]{1,0:T(8,128)(2,1)S(1)}, bf16[512,256]{1,0:T(8,128)(2,1)S(1)}, bf16[256,1024]{1,0:T(8,128)(2,1)S(1)}, bf16[256,1024]{1,0:T(8,128)(2,1)S(1)}) custom-call(s32[4]{0:T(128)S(1)} %pad_add_fusion.2.order, bf16[256,1024]{1,0:T(8,128)(2,1)S(1)} %get-tuple-element.129.refs_0_, bf16[256,1024]{1,0:T(8,128)(2,1)S(1)} %collective-permute-done.20.refs_1_, ...), custom_call_target="tpu_custom_call" | custom-call | flops 1 | bytes 1 | tf_op jit(solution)/shard_map/attn_fwd/pallas_call | solution.py:473
  108.0 4.9 %collective-permute-done.23.c = bf16[256,1024]{1,0:T(8,128)(2,1)S(1)} collective-permute-done((bf16[256,1024]{1,0:T(8,128)(2,1)S(1)}, bf16[256,1024]{1,0:T(8,128)(2,1)S(1)}, u32[]{:S(2)}, u32[]{:S(2)}) %collective-permute-start.23) | collective-permute-done | bytes 524320 | tf_op jit(solution)/shard_map/ppermute | solution.py:697
  115.8 11.1 %collective-permute-done.24.refs_0_.refs_2_ = bf16[256,1024]{1,0:T(8,128)(2,1)S(1)} collective-permute-done((bf16[256,1024]{1,0:T(8,128)(2,1)S(1)}, bf16[256,1024]{1,0:T(8,128)(2,1)S(1)}, u32[]{:S(2)}, u32[]{:S(2)}) %collective-permute-start.24) | collective-permute-done | bytes 524320 | tf_op jit(solution)/shard_map/ppermute | solution.py:697
  139.2 7.7 %mlp.2 = (bf16[512,1024]{1,0:T(8,128)(2,1)S(1)}, bf16[512,1024]{1,0:T(8,128)(2,1)S(1)}, bf16[256,1024]{1,0:T(8,128)(2,1)S(1)}, bf16[256,1024]{1,0:T(8,128)(2,1)S...) custom-call(bf16[256,1024]{1,0:T(8,128)(2,1)S(1)} %copy-done.6, bf16[128,1024]{1,0:T(8,128)(2,1)S(1)} %copy-done.36, ...), custom_call_target="tpu_custom_call" | custom-call | flops 1 | bytes 1 | tf_op jit(solution)/shard_map/mlp/pallas_call | solution.py:588
  150.8 7.7 %mlp.3 = (bf16[512,1024]{1,0:T(8,128)(2,1)S(1)}, bf16[512,1024]{1,0:T(8,128)(2,1)S(1)}, bf16[256,1024]{1,0:T(8,128)(2,1)S(1)}, bf16[256,1024]{1,0:T(8,128)(2,1)S...) custom-call(bf16[256,1024]{1,0:T(8,128)(2,1)S(1)} %copy-done.22, ...), custom_call_target="tpu_custom_call" | custom-call | flops 1 | bytes 1 | tf_op jit(solution)/shard_map/mlp/pallas_call | solution.py:588
  160.6 2.8 collective-permute-done.35.c
  168.1 7.4 %mlp_grads.1 = bf16[2048,1024]{1,0:T(8,128)(2,1)S(1)} custom-call(bf16[256,1024]{1,0:T(8,128)(2,1)S(1)} %copy-done.22, bf16[256,1024]{1,0:T(8,128)(2,1)S(1)} %collective-permute-done.31.refs_1_, bf16[256,1024]{1,0:T(8,128)(2,1)S(1)} %copy-done.7, bf16[128,1024]{1,0:T(8,128)(2,1)S(1)} %copy-done.37, bf16[128,1024]{1,0:T(8,128)(2,1)S(1)} %copy-done.34, ...), custom_call_target="tpu_custom_call" | custom-call | flops 1 | bytes 1 | tf_op jit(solution)/shard_map/mlp_grads/pallas_call | solution.py:634
  177.5 2.5 collective-permute-done.40.refs_0_.refs_7_
  184.9 6.6 %attn_bwd.2 = (bf16[512,768]{1,0:T(8,128)(2,1)S(1)}, bf16[256,1024]{1,0:T(8,128)(2,1)S(1)}, bf16[256,1024]{1,0:T(8,128)(2,1)S(1)}) custom-call(s32[4]{0:T(128)S(1)} %add_add_fusion.order, bf16[256,1024]{1,0:T(8,128)(2,1)} %collective-permute-done.40.refs_0_.refs_7_, bf16[128,1024]{1,0:T(8,128)(2,1)S(1)} %collective-permute-done.42.refs_1_.refs_8_, ...), custom_call_target="tpu_custom_call" | custom-call | flops 1 | bytes 1 | tf_op jit(solution)/shard_map/attn_bwd/pallas_call | solution.py:527
  196.1 6.4 %attn_bwd.3 = (bf16[512,768]{1,0:T(8,128)(2,1)S(1)}, bf16[256,1024]{1,0:T(8,128)(2,1)S(1)}, bf16[256,1024]{1,0:T(8,128)(2,1)S(1)}) custom-call(s32[4]{0:T(128)S(1)} %pad_add_fusion.2.order, bf16[256,1024]{1,0:T(8,128)(2,1)} %get-tuple-element.158.refs_0_.refs_5_, bf16[256,1024]{1,0:T(8,128)(2,1)S(1)} %collective-permute-done.46.refs_1_.refs_6_, ...), custom_call_target="tpu_custom_call" | custom-call | flops 1 | bytes 1 | tf_op jit(solution)/shard_map/attn_bwd/pallas_call | solution.py:527
  202.6 4.4 %collective-permute-done.41.c = bf16[256,1024]{1,0:T(8,128)(2,1)S(1)} collective-permute-done((bf16[256,1024]{1,0:T(8,128)(2,1)S(1)}, bf16[256,1024]{1,0:T(8,128)(2,1)S(1)}, u32[]{:S(2)}, u32[]{:S(2)}) %collective-permute-start.41) | collective-permute-done | bytes 524320 | tf_op jit(solution)/shard_map/ppermute | solution.py:697
  219.7 5.0 %attn_grads.1 = (bf16[128,1024]{1,0:T(8,128)(2,1)S(1)}, bf16[384,1024]{1,0:T(8,128)(2,1)S(1)}, f32[128,1024]{1,0:T(8,128)S(1)}, f32[128,1024]{1,0:T(8,128)S(1)},...) custom-call(s32[5]{0:T(128)S(1)} %stack.86.info, bf16[256,1024]{1,0:T(8,128)(2,1)S(1)} %copy-done.24, ...), custom_call_target="tpu_custom_call" | custom-call | flops 1 | bytes 1 | tf_op jit(solution)/shard_map/attn_grads/pallas_call | solution.py:678
  230.4 5.4 %collective-permute-done.59 = bf16[128,1024]{1,0:T(8,128)(2,1)S(1)} collective-permute-done((bf16[128,1024]{1,0:T(8,128)(2,1)S(1)}, bf16[128,1024]{1,0:T(8,128)(2,1)S(1)}, u32[]{:S(2)}, u32[]{:S(2)}) %collective-permute-start.59) | collective-permute-done | bytes 262176 | tf_op jit(solution)/shard_map/ppermute | solution.py:697
  237.3 4.3 %place_rows.4.refs_4_ = bf16[8,256,1024]{2,1,0:T(8,128)(2,1)} custom-call(s32[4]{0:T(128)S(1)} %pad_add_fusion.2.order, bf16[8,256,128]{2,1,0:T(8,128)(2,1)S(1)} %fusion.1.onehot_t, bf16[256,1024]{1,0:T(8,128)(2,1)} %get-tuple-element.178.refs_0_, bf16[256,1024]{1,0:T(8,128)(2,1)} %collective-permute-done.53.refs_1_, bf16[8,256,1024]{2,1,0:T(8,128)(2,1)} %refs_3_.2), custom_call_target="tpu_custom_call" | custom-call | flops 1 | bytes 1 | tf_op jit(solution)/shard_map/place_rows/pallas_call | solution.py:126
  241.7 3.5 %collective-permute-start.60 = (bf16[128,1024]{1,0:T(8,128)(2,1)S(1)}, bf16[128,1024]{1,0:T(8,128)(2,1)S(1)}, u32[]{:S(2)}, u32[]{:S(2)}) collective-permute-start(bf16[128,1024]{1,0:T(8,128)(2,1)S(1)} %add_convert_fusion.2), channel_id=1, source_target_pairs={{16,0},{20,4},{24,8},{28,12},{0,16},{4,20},{8,24},{12,28},{17,1},{... | collective-permute-start | bytes 786440 | tf_op jit(solution)/shard_map/ppermute | solution.py:725
  245.5 3.6 %place_rows.5 = bf16[8,256,1024]{2,1,0:T(8,128)(2,1)} custom-call(s32[4]{0:T(128)S(1)} %add_add_fusion.order, bf16[8,256,128]{2,1,0:T(8,128)(2,1)S(1)} %fusion.1.onehot_t, bf16[256,1024]{1,0:T(8,128)(2,1)S(1)} %collective-permute-done.50.refs_0_, bf16[128,1024]{1,0:T(8,128)(2,1)S(1)} %collective-permute-done.51.refs_1_, ...), custom_call_target="tpu_custom_call", output_to_operand_aliasing={{}: (6, {})} | custom-call | flops 1 | bytes 1 | tf_op jit(solution)/shard_map/place_rows/pallas_call | solution.py:126
  249.1 8.5 %collective-permute-done.58 = bf16[384,1024]{1,0:T(8,128)(2,1)S(1)} collective-permute-done((bf16[384,1024]{1,0:T(8,128)(2,1)S(1)}, bf16[384,1024]{1,0:T(8,128)(2,1)S(1)}, u32[]{:S(2)}, u32[]{:S(2)}) %collective-permute-start.58) | collective-permute-done | bytes 786464 | tf_op jit(solution)/shard_map/ppermute | solution.py:697
  257.6 3.6 %place_rows.6.refs_4_ = bf16[8,256,1024]{2,1,0:T(8,128)(2,1)} custom-call(s32[4]{0:T(128)S(1)} %pad_add_fusion.2.order, bf16[8,256,128]{2,1,0:T(8,128)(2,1)S(1)} %fusion.1.onehot_t, bf16[256,1024]{1,0:T(8,128)(2,1)S(1)} %get-tuple-element.179.refs_0_, bf16[256,1024]{1,0:T(8,128)(2,1)S(1)} %collective-permute-done.55.refs_1_, bf16[8,256,1024]{2,1,0:T(8,128)(2,1)} %refs_3_.3), custom_call_target="tpu_custom_call" | custom-call | flops 1 | bytes 1 | tf_op jit(solution)/shard_map/place_rows/pallas_call | solution.py:126
  264.7 3.6 %place_rows.7 = bf16[8,256,1024]{2,1,0:T(8,128)(2,1)} custom-call(s32[4]{0:T(128)S(1)} %add_add_fusion.order, bf16[8,256,128]{2,1,0:T(8,128)(2,1)S(1)} %fusion.1.onehot_t, bf16[256,1024]{1,0:T(8,128)(2,1)S(1)} %collective-permute-done.54.refs_0_, bf16[128,1024]{1,0:T(8,128)(2,1)S(1)} %collective-permute-done.56.refs_1_, ...), custom_call_target="tpu_custom_call", output_to_operand_aliasing={{}: (6, {})} | custom-call | flops 1 | bytes 1 | tf_op jit(solution)/shard_map/place_rows/pallas_call | solution.py:126
  268.3 2.9 collective-permute-start.68
  275.0 10.6 %collective-permute-done.62.p3 = bf16[128,1024]{1,0:T(8,128)(2,1)S(1)} collective-permute-done((bf16[128,1024]{1,0:T(8,128)(2,1)S(1)}, bf16[128,1024]{1,0:T(8,128)(2,1)S(1)}, u32[]{:S(2)}, u32[]{:S(2)}) %collective-permute-start.62) | collective-permute-done | bytes 262176 | tf_op jit(solution)/shard_map/ppermute | solution.py:725
  285.6 3.6 %collective-permute-done.61.p2 = bf16[128,1024]{1,0:T(8,128)(2,1)S(1)} collective-permute-done((bf16[128,1024]{1,0:T(8,128)(2,1)S(1)}, bf16[128,1024]{1,0:T(8,128)(2,1)S(1)}, u32[]{:S(2)}, u32[]{:S(2)}) %collective-permute-start.61) | collective-permute-done | bytes 262176 | tf_op jit(solution)/shard_map/ppermute | solution.py:725
  (345 shorter events, 116.1 us)
Async XLA Ops:
  7.2 124.9 %all-gather.2.cloned.1.call-start = ((), (), s32[]{:S(2)}) async-start(), calls=%async_computation.1 | async-start | bytes 4718592 | tf_op jit(solution)/shard_map/all_gather | solution.py:817
  23.2 28.1 %collective-permute-start.8 = (bf16[144,1024]{1,0:T(8,128)(2,1)S(1)}, bf16[144,1024]{1,0:T(8,128)(2,1)S(1)}, u32[]{:S(2)}, u32[]{:S(2)}) collective-permute-start(bf16[144,1024]{1,0:T(8,128)(2,1)S(1)} %pack_attn.1.refs_0_.near_own), channel_id=1, source_target_pairs={{8,0},{12,4},{16,8},{20,12},{24,16},{28,20},{0,24},{4,28},{9,1},{1... | collective-permute-start | bytes 884744 | tf_op jit(solution)/shard_map/ppermute | solution.py:725
  25.2 26.1 %collective-permute-start.4 = (bf16[144,1024]{1,0:T(8,128)(2,1)S(1)}, bf16[144,1024]{1,0:T(8,128)(2,1)S(1)}, u32[]{:S(2)}, u32[]{:S(2)}) collective-permute-start(bf16[144,1024]{1,0:T(8,128)(2,1)S(1)} %pack_attn.1.refs_0_.near_own), channel_id=1, source_target_pairs={{16,0},{20,4},{24,8},{28,12},{0,16},{4,20},{8,24},{12,28},{17,1},{... | collective-permute-start | bytes 884744 | tf_op jit(solution)/shard_map/ppermute | solution.py:725
  33.1 14.1 %collective-permute-start.7 = (bf16[128,1024]{1,0:T(8,128)(2,1)}, bf16[128,1024]{1,0:T(8,128)(2,1)}, u32[]{:S(2)}, u32[]{:S(2)}) collective-permute-start(bf16[128,1024]{1,0:T(8,128)(2,1)} %get-tuple-element.241), channel_id=1, source_target_pairs={{0,2},{1,3},{2,0},{3,1},{4,6},{5,7},{6,4},{7,5},{8,10},{9,11},{10,... | collective-permute-start | bytes 786440 | tf_op jit(solution)/shard_map/ppermute | solution.py:697
  36.5 14.8 %collective-permute-start.6 = (bf16[128,1024]{1,0:T(8,128)(2,1)}, bf16[128,1024]{1,0:T(8,128)(2,1)}, u32[]{:S(2)}, u32[]{:S(2)}) collective-permute-start(bf16[128,1024]{1,0:T(8,128)(2,1)} %get-tuple-element.242), channel_id=1, source_target_pairs={{0,2},{1,3},{2,0},{3,1},{4,6},{5,7},{6,4},{7,5},{8,10},{9,11},{10,... | collective-permute-start | bytes 786440 | tf_op jit(solution)/shard_map/ppermute | solution.py:697
  52.9 240.6 %reduce-scatter.2.cloned.1.call-start = ((), (), s32[]{:S(2)}) async-start(), calls=%async_computation.2 | async-start | bytes 4718592 | tf_op jit(solution)/shard_map/reduce_scatter | solution.py:896
  57.0 31.0 %collective-permute-start.15 = (bf16[384,1024]{1,0:T(8,128)(2,1)}, bf16[384,1024]{1,0:T(8,128)(2,1)S(1)}, u32[]{:S(2)}, u32[]{:S(2)}) collective-permute-start(bf16[384,1024]{1,0:T(8,128)(2,1)} %get-tuple-element.124.near), channel_id=1, source_target_pairs={{0,4},{4,0},{8,12},{12,8},{16,20},{20,16},{24,28},{28,24},{1,5},{5... | collective-permute-start | bytes 2359304 | tf_op jit(solution)/shard_map/ppermute | solution.py:697
  61.0 14.4 %collective-permute-start.12 = (bf16[256,1024]{1,0:T(8,128)(2,1)S(1)}, bf16[256,1024]{1,0:T(8,128)(2,1)S(1)}, u32[]{:S(2)}, u32[]{:S(2)}) collective-permute-start(bf16[256,1024]{1,0:T(8,128)(2,1)S(1)} %get-tuple-element.129.refs_0_), channel_id=1, source_target_pairs={{0,2},{1,3},{2,0},{3,1},{4,6},{5,7},{6,4},{7,5},{8,10},{9,11},{10,... | collective-permute-start | bytes 1572872 | tf_op jit(solution)/shard_map/ppermute | solution.py:697
  62.6 25.3 %collective-permute-start.14 = (bf16[144,1024]{1,0:T(8,128)(2,1)S(1)}, bf16[144,1024]{1,0:T(8,128)(2,1)S(1)}, u32[]{:S(2)}, u32[]{:S(2)}) collective-permute-start(bf16[144,1024]{1,0:T(8,128)(2,1)S(1)} %pack_attn.1.refs_0_.near_own), channel_id=1, source_target_pairs={{0,4},{4,0},{8,12},{12,8},{16,20},{20,16},{24,28},{28,24},{1,5},{5... | collective-permute-start | bytes 884744 | tf_op jit(solution)/shard_map/ppermute | solution.py:697
  75.4 14.6 %collective-permute-start.13 = (bf16[256,1024]{1,0:T(8,128)(2,1)S(1)}, bf16[256,1024]{1,0:T(8,128)(2,1)S(1)}, u32[]{:S(2)}, u32[]{:S(2)}) collective-permute-start(bf16[256,1024]{1,0:T(8,128)(2,1)S(1)} %get-tuple-element.120.refs_2_.refs_5_), channel_id=1, source_target_pairs={{0,2},{1,3},{2,0},{3,1},{4,6},{5,7},{6,4},{7,5},{8,10},{9,11},{10,... | collective-permute-start | bytes 1572872 | tf_op jit(solution)/shard_map/ppermute | solution.py:697
  98.9 14.0 %collective-permute-start.23 = (bf16[256,1024]{1,0:T(8,128)(2,1)S(1)}, bf16[256,1024]{1,0:T(8,128)(2,1)S(1)}, u32[]{:S(2)}, u32[]{:S(2)}) collective-permute-start(bf16[256,1024]{1,0:T(8,128)(2,1)S(1)} %pad_maximum_fusion), channel_id=1, source_target_pairs={{0,2},{1,3},{2,0},{3,1},{4,6},{5,7},{6,4},{7,5},{8,10},{9,11},{10,... | collective-permute-start | bytes 1572872 | tf_op jit(solution)/shard_map/ppermute | solution.py:697
  113.6 13.3 %collective-permute-start.24 = (bf16[256,1024]{1,0:T(8,128)(2,1)S(1)}, bf16[256,1024]{1,0:T(8,128)(2,1)S(1)}, u32[]{:S(2)}, u32[]{:S(2)}) collective-permute-start(bf16[256,1024]{1,0:T(8,128)(2,1)S(1)} %get-tuple-element.144.refs_0_), channel_id=1, source_target_pairs={{0,2},{1,3},{2,0},{3,1},{4,6},{5,7},{6,4},{7,5},{8,10},{9,11},{10,... | collective-permute-start | bytes 1572872 | tf_op jit(solution)/shard_map/ppermute | solution.py:697
  149.3 14.0 %collective-permute-start.35 = (bf16[256,1024]{1,0:T(8,128)(2,1)S(1)}, bf16[256,1024]{1,0:T(8,128)(2,1)S(1)}, u32[]{:S(2)}, u32[]{:S(2)}) collective-permute-start(bf16[256,1024]{1,0:T(8,128)(2,1)S(1)} %pad_maximum_fusion.1), channel_id=1, source_target_pairs={{0,2},{1,3},{2,0},{3,1},{4,6},{5,7},{6,4},{7,5},{8,10},{9,11},{10,... | collective-permute-start | bytes 1572872 | tf_op jit(solution)/shard_map/ppermute | solution.py:697
  166.6 13.5 %collective-permute-start.40 = (bf16[256,1024]{1,0:T(8,128)(2,1)}, bf16[256,1024]{1,0:T(8,128)(2,1)}, u32[]{:S(2)}, u32[]{:S(2)}) collective-permute-start(bf16[256,1024]{1,0:T(8,128)(2,1)} %get-tuple-element.158.refs_0_.refs_5_), channel_id=1, source_target_pairs={{0,2},{1,3},{2,0},{3,1},{4,6},{5,7},{6,4},{7,5},{8,10},{9,11},{10,... | collective-permute-start | bytes 1572872 | tf_op jit(solution)/shard_map/ppermute | solution.py:697
  192.2 14.8 %collective-permute-start.41 = (bf16[256,1024]{1,0:T(8,128)(2,1)S(1)}, bf16[256,1024]{1,0:T(8,128)(2,1)S(1)}, u32[]{:S(2)}, u32[]{:S(2)}) collective-permute-start(bf16[256,1024]{1,0:T(8,128)(2,1)S(1)} %pad_maximum_fusion.2), channel_id=1, source_target_pairs={{0,2},{1,3},{2,0},{3,1},{4,6},{5,7},{6,4},{7,5},{8,10},{9,11},{10,... | collective-permute-start | bytes 1572872 | tf_op jit(solution)/shard_map/ppermute | solution.py:697
  193.8 13.2 %collective-permute-start.37 = (bf16[128,1024]{1,0:T(8,128)(2,1)S(1)}, bf16[128,1024]{1,0:T(8,128)(2,1)S(1)}, u32[]{:S(2)}, u32[]{:S(2)}) collective-permute-start(bf16[128,1024]{1,0:T(8,128)(2,1)S(1)} %get-tuple-element.221), channel_id=1, source_target_pairs={{0,1},{1,0},{2,3},{3,2},{4,5},{5,4},{6,7},{7,6},{8,9},{9,8},{10,11... | collective-permute-start | bytes 786440 | tf_op jit(solution)/shard_map/ppermute | solution.py:697
  193.9 13.1 %collective-permute-start.36 = (bf16[128,1024]{1,0:T(8,128)(2,1)S(1)}, bf16[128,1024]{1,0:T(8,128)(2,1)S(1)}, u32[]{:S(2)}, u32[]{:S(2)}) collective-permute-start(bf16[128,1024]{1,0:T(8,128)(2,1)S(1)} %get-tuple-element.222), channel_id=1, source_target_pairs={{0,1},{1,0},{2,3},{3,2},{4,5},{5,4},{6,7},{7,6},{8,9},{9,8},{10,11... | collective-permute-start | bytes 786440 | tf_op jit(solution)/shard_map/ppermute | solution.py:697
  195.4 30.0 %collective-permute-start.49 = (bf16[256,1024]{1,0:T(8,128)(2,1)}, bf16[256,1024]{1,0:T(8,128)(2,1)}, u32[]{:S(2)}, u32[]{:S(2)}) collective-permute-start(bf16[256,1024]{1,0:T(8,128)(2,1)} %pad_maximum_fusion.3), channel_id=1, source_target_pairs={{0,2},{1,3},{2,0},{3,1},{4,6},{5,7},{6,4},{7,5},{8,10},{9,11},{10,... | collective-permute-start | bytes 1572872 | tf_op jit(solution)/shard_map/ppermute | solution.py:697
  208.6 20.5 %collective-permute-start.50 = (bf16[256,1024]{1,0:T(8,128)(2,1)}, bf16[256,1024]{1,0:T(8,128)(2,1)S(1)}, u32[]{:S(2)}, u32[]{:S(2)}) collective-permute-start(bf16[256,1024]{1,0:T(8,128)(2,1)} %get-tuple-element.178.refs_0_), channel_id=1, source_target_pairs={{0,2},{1,3},{2,0},{3,1},{4,6},{5,7},{6,4},{7,5},{8,10},{9,11},{10,... | collective-permute-start | bytes 1572872 | tf_op jit(solution)/shard_map/ppermute | solution.py:697
  210.9 13.8 %collective-permute-start.48 = (bf16[128,1024]{1,0:T(8,128)(2,1)}, bf16[128,1024]{1,0:T(8,128)(2,1)}, u32[]{:S(2)}, u32[]{:S(2)}) collective-permute-start(bf16[128,1024]{1,0:T(8,128)(2,1)} %get-tuple-element.209), channel_id=1, source_target_pairs={{0,1},{1,0},{2,3},{3,2},{4,5},{5,4},{6,7},{7,6},{8,9},{9,8},{10,11... | collective-permute-start | bytes 786440 | tf_op jit(solution)/shard_map/ppermute | solution.py:697
  210.9 24.9 %collective-permute-start.53 = (bf16[256,1024]{1,0:T(8,128)(2,1)}, bf16[256,1024]{1,0:T(8,128)(2,1)}, u32[]{:S(2)}, u32[]{:S(2)}) collective-permute-start(bf16[256,1024]{1,0:T(8,128)(2,1)} %get-tuple-element.178.refs_0_), channel_id=1, source_target_pairs={{0,1},{1,0},{2,3},{3,2},{4,5},{5,4},{6,7},{7,6},{8,9},{9,8},{10,11... | collective-permute-start | bytes 1572872 | tf_op jit(solution)/shard_map/ppermute | solution.py:697
  211.4 15.4 %collective-permute-start.47 = (bf16[128,1024]{1,0:T(8,128)(2,1)}, bf16[128,1024]{1,0:T(8,128)(2,1)}, u32[]{:S(2)}, u32[]{:S(2)}) collective-permute-start(bf16[128,1024]{1,0:T(8,128)(2,1)} %get-tuple-element.210), channel_id=1, source_target_pairs={{0,1},{1,0},{2,3},{3,2},{4,5},{5,4},{6,7},{7,6},{8,9},{9,8},{10,11... | collective-permute-start | bytes 786440 | tf_op jit(solution)/shard_map/ppermute | solution.py:697
  225.4 32.2 %collective-permute-start.58 = (bf16[384,1024]{1,0:T(8,128)(2,1)S(1)}, bf16[384,1024]{1,0:T(8,128)(2,1)S(1)}, u32[]{:S(2)}, u32[]{:S(2)}) collective-permute-start(bf16[384,1024]{1,0:T(8,128)(2,1)S(1)} %get-tuple-element.182), channel_id=1, source_target_pairs={{0,4},{4,0},{8,12},{12,8},{16,20},{20,16},{24,28},{28,24},{1,5},{5... | collective-permute-start | bytes 2359304 | tf_op jit(solution)/shard_map/ppermute | solution.py:697
  229.0 28.6 %collective-permute-start.55 = (bf16[256,1024]{1,0:T(8,128)(2,1)S(1)}, bf16[256,1024]{1,0:T(8,128)(2,1)S(1)}, u32[]{:S(2)}, u32[]{:S(2)}) collective-permute-start(bf16[256,1024]{1,0:T(8,128)(2,1)S(1)} %get-tuple-element.179.refs_0_), channel_id=1, source_target_pairs={{0,1},{1,0},{2,3},{3,2},{4,5},{5,4},{6,7},{7,6},{8,9},{9,8},{10,11... | collective-permute-start | bytes 1572872 | tf_op jit(solution)/shard_map/ppermute | solution.py:697
  229.1 32.1 %collective-permute-start.54 = (bf16[256,1024]{1,0:T(8,128)(2,1)S(1)}, bf16[256,1024]{1,0:T(8,128)(2,1)S(1)}, u32[]{:S(2)}, u32[]{:S(2)}) collective-permute-start(bf16[256,1024]{1,0:T(8,128)(2,1)S(1)} %get-tuple-element.179.refs_0_), channel_id=1, source_target_pairs={{0,2},{1,3},{2,0},{3,1},{4,6},{5,7},{6,4},{7,5},{8,10},{9,11},{10,... | collective-permute-start | bytes 1572872 | tf_op jit(solution)/shard_map/ppermute | solution.py:697
  241.7 31.1 %collective-permute-start.60 = (bf16[128,1024]{1,0:T(8,128)(2,1)S(1)}, bf16[128,1024]{1,0:T(8,128)(2,1)S(1)}, u32[]{:S(2)}, u32[]{:S(2)}) collective-permute-start(bf16[128,1024]{1,0:T(8,128)(2,1)S(1)} %add_convert_fusion.2), channel_id=1, source_target_pairs={{16,0},{20,4},{24,8},{28,12},{0,16},{4,20},{8,24},{12,28},{17,1},{... | collective-permute-start | bytes 786440 | tf_op jit(solution)/shard_map/ppermute | solution.py:725
  245.2 18.8 %collective-permute-start.64 = (f32[8,1024]{1,0:T(8,128)S(1)}, f32[8,1024]{1,0:T(8,128)S(1)}, u32[]{:S(2)}, u32[]{:S(2)}) collective-permute-start(f32[8,1024]{1,0:T(8,128)S(1)} %add.136), channel_id=1, source_target_pairs={{0,2},{1,3},{2,0},{3,1},{4,6},{5,7},{6,4},{7,5},{8,10},{9,11},{10,... | collective-permute-start | bytes 98312 | tf_op jit(solution)/shard_map/ppermute | solution.py:697
  262.0 23.6 %collective-permute-start.62 = (bf16[128,1024]{1,0:T(8,128)(2,1)S(1)}, bf16[128,1024]{1,0:T(8,128)(2,1)S(1)}, u32[]{:S(2)}, u32[]{:S(2)}) collective-permute-start(bf16[128,1024]{1,0:T(8,128)(2,1)S(1)} %get-tuple-element.203), channel_id=1, source_target_pairs={{8,0},{12,4},{16,8},{20,12},{24,16},{28,20},{0,24},{4,28},{9,1},{1... | collective-permute-start | bytes 786440 | tf_op jit(solution)/shard_map/ppermute | solution.py:725
  263.9 25.3 %collective-permute-start.61 = (bf16[128,1024]{1,0:T(8,128)(2,1)S(1)}, bf16[128,1024]{1,0:T(8,128)(2,1)S(1)}, u32[]{:S(2)}, u32[]{:S(2)}) collective-permute-start(bf16[128,1024]{1,0:T(8,128)(2,1)S(1)} %get-tuple-element.204), channel_id=1, source_target_pairs={{24,0},{28,4},{0,8},{4,12},{8,16},{12,20},{16,24},{20,28},{25,1},{... | collective-permute-start | bytes 786440 | tf_op jit(solution)/shard_map/ppermute | solution.py:725
  268.3 22.9 %collective-permute-start.68 = (f32[8,1024]{1,0:T(8,128)S(1)}, f32[8,1024]{1,0:T(8,128)S(1)}, u32[]{:S(2)}, u32[]{:S(2)}) collective-permute-start(f32[8,1024]{1,0:T(8,128)S(1)} %add.138), channel_id=1, source_target_pairs={{16,0},{20,4},{24,8},{28,12},{0,16},{4,20},{8,24},{12,28},{17,1},{... | collective-permute-start | bytes 98312 | tf_op jit(solution)/shard_map/ppermute | solution.py:725
  271.2 20.9 %collective-permute-start.67 = (f32[8,1024]{1,0:T(8,128)S(1)}, f32[8,1024]{1,0:T(8,128)S(1)}, u32[]{:S(2)}, u32[]{:S(2)}) collective-permute-start(f32[8,1024]{1,0:T(8,128)S(1)} %add.138), channel_id=1, source_target_pairs={{24,0},{28,4},{0,8},{4,12},{8,16},{12,20},{16,24},{20,28},{25,1},{... | collective-permute-start | bytes 98312 | tf_op jit(solution)/shard_map/ppermute | solution.py:725
  272.7 19.3 %collective-permute-start.66 = (f32[8,1024]{1,0:T(8,128)S(1)}, f32[8,1024]{1,0:T(8,128)S(1)}, u32[]{:S(2)}, u32[]{:S(2)}) collective-permute-start(f32[8,1024]{1,0:T(8,128)S(1)} %add.138), channel_id=1, source_target_pairs={{8,0},{12,4},{16,8},{20,12},{24,16},{28,20},{0,24},{4,28},{9,1},{1... | collective-permute-start | bytes 98312 | tf_op jit(solution)/shard_map/ppermute | solution.py:725
  (116 other events, 924.4 us)
Sparse Core Ops, SparseCore 0:
  53.0 79.0 all-gather.1
  180.2 113.1 reduce-scatter.1

commit v4 on v3

--- a/solution.py
+++ b/solution.py
@@ -594,7 +594,7 @@
         compiler_params=params(16),
         cost_estimate=COST,
         name="mlp",
-    )(na, *nb, ga, *gb, w)
+    )(na, *nb, in_hbm(ga), *[in_hbm(x) for x in gb], in_hbm(w))
 
 
 def turn(xt, pieces, cols):

time: 304 us -> 301 us (level)
  Pallas kernels: 93.4 us -> 99.4 us
  local copies, waits for them, and re-layouts: 32.9 us -> 28.9 us
  waiting for transfers between devices: 101 us -> 97.3 us
    pallas_call x2, Pallas kernels: 15.4 us -> 20.5 us  [mlp_both(): pl.pallas_call(functools.partial(mlp_kernel, parts=1 + len(nb)), in_specs...]
    unnamed x154, local copies, waits for them, and re-layouts: 25.4 us -> 21.4 us
  transfers between devices with their start and end apart: 71 -> 71, of which waited for: 34 -> 34; matrix products, arithmetic and copies ran while one was open for 3% -> 3% of each run, Pallas kernels for 25% -> 26%
where the time goes in v4:
time: 301 us; the launch traced here: 300 us
  Pallas kernels  99.4 us (33%)
  waiting for transfers between devices  97.3 us (32%)
  starting transfers between devices  53.8 us (18%)
  local copies, waits for them, and re-layouts  28.9 us (10%)
  between operations  15.2 us (5%)
  other arithmetic  5.36 us (2%)
    ppermute x60, waiting for transfers between devices, swap(): return lax.ppermute(x, axis, [(i, i ^ mask) for i in range(size)])  79.9 us
    ppermute x60, starting transfers between devices, swap(): return lax.ppermute(x, axis, [(i, i ^ mask) for i in range(size)])  35.1 us
    unnamed x154, local copies, waits for them, and re-layouts  21.4 us
    pallas_call x2, Pallas kernels, mlp_both(): pl.pallas_call(functools.partial(mlp_kernel, parts=1 + len(nb)), in_specs...  20.5 us
    ppermute x9, starting transfers between devices, z_move(): return lax.ppermute(x, 'fsdp', z_perm(lax.axis_size('fsdp'), shift))  18.6 us
    ppermute x9, waiting for transfers between devices, z_move(): return lax.ppermute(x, 'fsdp', z_perm(lax.axis_size('fsdp'), shift))  16 us
    pallas_call x4, Pallas kernels, place_rows(): pl.pallas_call(functools.partial(place_kernel, blocks=len(rows)), in_spec...  15.1 us
    pallas_call x2, Pallas kernels, attn_bwd(): pl.pallas_call(functools.partial(attn_bwd_kernel, parts=1 + len(gb)), in_...  13 us
  transfers between devices with their start and end apart: 71, of which 34 were waited for; matrix products, arithmetic and copies ran while one was open for 3% of the time, Pallas kernels for 26%

profile of v4, /device:TPU:0, one launch (start us, length us, event | category | flops | bytes accessed | tf_op | source)
XLA Modules:
  0.0 299.9 jit_solution(3878981399557447212)
XLA Ops:
  10.1 2.6 pick_rows.4
  14.0 2.6 pick_rows.5.keep
  16.7 2.6 pick_rows.6
  20.2 3.0 %collective-permute-start.9 = (bf16[144,1024]{1,0:T(8,128)(2,1)S(1)}, bf16[144,1024]{1,0:T(8,128)(2,1)S(1)}, u32[]{:S(2)}, u32[]{:S(2)}) collective-permute-start(bf16[144,1024]{1,0:T(8,128)(2,1)S(1)} %pack_attn.1.refs_0_.near_own), channel_id=1, source_target_pairs={{24,0},{28,4},{0,8},{4,12},{8,16},{12,20},{16,24},{20,28},{25,1},{... | collective-permute-start | bytes 884744 | tf_op jit(solution)/shard_map/ppermute | solution.py:725
  28.5 2.6 pick_rows.7.keep
  41.5 5.6 %collective-permute-done.7.far1 = bf16[128,1024]{1,0:T(8,128)(2,1)} collective-permute-done((bf16[128,1024]{1,0:T(8,128)(2,1)}, bf16[128,1024]{1,0:T(8,128)(2,1)}, u32[]{:S(2)}, u32[]{:S(2)}) %collective-permute-start.7) | collective-permute-done | bytes 262176 | tf_op jit(solution)/shard_map/ppermute | solution.py:697
  47.2 4.1 %collective-permute-done.6.far0 = bf16[128,1024]{1,0:T(8,128)(2,1)} collective-permute-done((bf16[128,1024]{1,0:T(8,128)(2,1)}, bf16[128,1024]{1,0:T(8,128)(2,1)}, u32[]{:S(2)}, u32[]{:S(2)}) %collective-permute-start.6) | collective-permute-done | bytes 262176 | tf_op jit(solution)/shard_map/ppermute | solution.py:697
  65.3 10.1 %collective-permute-done.12.refs_0_.refs_2_ = bf16[256,1024]{1,0:T(8,128)(2,1)S(1)} collective-permute-done((bf16[256,1024]{1,0:T(8,128)(2,1)S(1)}, bf16[256,1024]{1,0:T(8,128)(2,1)S(1)}, u32[]{:S(2)}, u32[]{:S(2)}) %collective-permute-start.12) | collective-permute-done | bytes 524320 | tf_op jit(solution)/shard_map/ppermute | solution.py:697
  76.9 11.0 %collective-permute-done.14.far_own = bf16[144,1024]{1,0:T(8,128)(2,1)S(1)} collective-permute-done((bf16[144,1024]{1,0:T(8,128)(2,1)S(1)}, bf16[144,1024]{1,0:T(8,128)(2,1)S(1)}, u32[]{:S(2)}, u32[]{:S(2)}) %collective-permute-start.14) | collective-permute-done | bytes 294944 | tf_op jit(solution)/shard_map/ppermute | solution.py:697
  91.2 5.4 %attn_fwd.2 = (bf16[512,768]{1,0:T(8,128)(2,1)S(1)}, bf16[512,256]{1,0:T(8,128)(2,1)S(1)}, bf16[256,1024]{1,0:T(8,128)(2,1)S(1)}, bf16[256,1024]{1,0:T(8,128)(2,1)S(1)}) custom-call(s32[4]{0:T(128)S(1)} %add_add_fusion.order, bf16[256,1024]{1,0:T(8,128)(2,1)S(1)} %collective-permute-done.12.refs_0_.refs_2_, ...), custom_call_target="tpu_custom_call" | custom-call | flops 1 | bytes 1 | tf_op jit(solution)/shard_map/attn_fwd/pallas_call | solution.py:473
  100.6 5.4 %attn_fwd.3 = (bf16[512,768]{1,0:T(8,128)(2,1)S(1)}, bf16[512,256]{1,0:T(8,128)(2,1)S(1)}, bf16[256,1024]{1,0:T(8,128)(2,1)S(1)}, bf16[256,1024]{1,0:T(8,128)(2,1)S(1)}) custom-call(s32[4]{0:T(128)S(1)} %pad_add_fusion.2.order, bf16[256,1024]{1,0:T(8,128)(2,1)S(1)} %get-tuple-element.129.refs_0_, bf16[256,1024]{1,0:T(8,128)(2,1)S(1)} %collective-permute-done.20.refs_1_, ...), custom_call_target="tpu_custom_call" | custom-call | flops 1 | bytes 1 | tf_op jit(solution)/shard_map/attn_fwd/pallas_call | solution.py:473
  108.0 4.9 %collective-permute-done.23.c = bf16[256,1024]{1,0:T(8,128)(2,1)S(1)} collective-permute-done((bf16[256,1024]{1,0:T(8,128)(2,1)S(1)}, bf16[256,1024]{1,0:T(8,128)(2,1)S(1)}, u32[]{:S(2)}, u32[]{:S(2)}) %collective-permute-start.23) | collective-permute-done | bytes 524320 | tf_op jit(solution)/shard_map/ppermute | solution.py:697
  115.8 11.1 %collective-permute-done.24.refs_0_.refs_2_ = bf16[256,1024]{1,0:T(8,128)(2,1)S(1)} collective-permute-done((bf16[256,1024]{1,0:T(8,128)(2,1)S(1)}, bf16[256,1024]{1,0:T(8,128)(2,1)S(1)}, u32[]{:S(2)}, u32[]{:S(2)}) %collective-permute-start.24) | collective-permute-done | bytes 524320 | tf_op jit(solution)/shard_map/ppermute | solution.py:697
  135.1 10.3 %mlp.2 = (bf16[512,1024]{1,0:T(8,128)(2,1)S(1)}, bf16[512,1024]{1,0:T(8,128)(2,1)S(1)}, bf16[256,1024]{1,0:T(8,128)(2,1)S(1)}, bf16[256,1024]{1,0:T(8,128)(2,1)S...) custom-call(bf16[256,1024]{1,0:T(8,128)(2,1)S(1)} %copy-done.4, bf16[128,1024]{1,0:T(8,128)(2,1)S(1)} %copy-done.36, ...), custom_call_target="tpu_custom_call" | custom-call | flops 1 | bytes 1 | tf_op jit(solution)/shard_map/mlp/pallas_call | solution.py:588
  150.0 10.2 %mlp.3 = (bf16[512,1024]{1,0:T(8,128)(2,1)S(1)}, bf16[512,1024]{1,0:T(8,128)(2,1)S(1)}, bf16[256,1024]{1,0:T(8,128)(2,1)S(1)}, bf16[256,1024]{1,0:T(8,128)(2,1)S...) custom-call(bf16[256,1024]{1,0:T(8,128)(2,1)S(1)} %copy-done.21, ...), custom_call_target="tpu_custom_call" | custom-call | flops 1 | bytes 1 | tf_op jit(solution)/shard_map/mlp/pallas_call | solution.py:588
  166.5 8.3 %mlp_grads.1 = bf16[2048,1024]{1,0:T(8,128)(2,1)S(1)} custom-call(bf16[256,1024]{1,0:T(8,128)(2,1)S(1)} %copy-done.21, bf16[256,1024]{1,0:T(8,128)(2,1)S(1)} %collective-permute-done.31.refs_1_, bf16[256,1024]{1,0:T(8,128)(2,1)S(1)} %copy-done.5, bf16[128,1024]{1,0:T(8,128)(2,1)S(1)} %copy-done.37, bf16[128,1024]{1,0:T(8,128)(2,1)S(1)} %copy-done.34, ...), custom_call_target="tpu_custom_call" | custom-call | flops 1 | bytes 1 | tf_op jit(solution)/shard_map/mlp_grads/pallas_call | solution.py:634
  176.9 3.0 collective-permute-done.40.refs_0_.refs_7_
  184.7 6.6 %attn_bwd.2 = (bf16[512,768]{1,0:T(8,128)(2,1)S(1)}, bf16[256,1024]{1,0:T(8,128)(2,1)S(1)}, bf16[256,1024]{1,0:T(8,128)(2,1)S(1)}) custom-call(s32[4]{0:T(128)S(1)} %add_add_fusion.order, bf16[256,1024]{1,0:T(8,128)(2,1)} %collective-permute-done.40.refs_0_.refs_7_, bf16[128,1024]{1,0:T(8,128)(2,1)S(1)} %collective-permute-done.42.refs_1_.refs_8_, ...), custom_call_target="tpu_custom_call" | custom-call | flops 1 | bytes 1 | tf_op jit(solution)/shard_map/attn_bwd/pallas_call | solution.py:527
  195.8 6.5 %attn_bwd.3 = (bf16[512,768]{1,0:T(8,128)(2,1)S(1)}, bf16[256,1024]{1,0:T(8,128)(2,1)S(1)}, bf16[256,1024]{1,0:T(8,128)(2,1)S(1)}) custom-call(s32[4]{0:T(128)S(1)} %pad_add_fusion.2.order, bf16[256,1024]{1,0:T(8,128)(2,1)} %get-tuple-element.158.refs_0_.refs_5_, bf16[256,1024]{1,0:T(8,128)(2,1)S(1)} %collective-permute-done.46.refs_1_.refs_6_, ...), custom_call_target="tpu_custom_call" | custom-call | flops 1 | bytes 1 | tf_op jit(solution)/shard_map/attn_bwd/pallas_call | solution.py:527
  202.3 4.5 %collective-permute-done.41.c = bf16[256,1024]{1,0:T(8,128)(2,1)S(1)} collective-permute-done((bf16[256,1024]{1,0:T(8,128)(2,1)S(1)}, bf16[256,1024]{1,0:T(8,128)(2,1)S(1)}, u32[]{:S(2)}, u32[]{:S(2)}) %collective-permute-start.41) | collective-permute-done | bytes 524320 | tf_op jit(solution)/shard_map/ppermute | solution.py:697
  218.6 5.0 %attn_grads.1 = (bf16[128,1024]{1,0:T(8,128)(2,1)S(1)}, bf16[384,1024]{1,0:T(8,128)(2,1)S(1)}, f32[128,1024]{1,0:T(8,128)S(1)}, f32[128,1024]{1,0:T(8,128)S(1)},...) custom-call(s32[5]{0:T(128)S(1)} %stack.86.info, bf16[256,1024]{1,0:T(8,128)(2,1)S(1)} %copy-done.25, ...), custom_call_target="tpu_custom_call" | custom-call | flops 1 | bytes 1 | tf_op jit(solution)/shard_map/attn_grads/pallas_call | solution.py:678
  229.5 5.0 %collective-permute-done.59 = bf16[128,1024]{1,0:T(8,128)(2,1)S(1)} collective-permute-done((bf16[128,1024]{1,0:T(8,128)(2,1)S(1)}, bf16[128,1024]{1,0:T(8,128)(2,1)S(1)}, u32[]{:S(2)}, u32[]{:S(2)}) %collective-permute-start.59) | collective-permute-done | bytes 262176 | tf_op jit(solution)/shard_map/ppermute | solution.py:697
  236.0 4.3 %place_rows.4.refs_4_ = bf16[8,256,1024]{2,1,0:T(8,128)(2,1)} custom-call(s32[4]{0:T(128)S(1)} %pad_add_fusion.2.order, bf16[8,256,128]{2,1,0:T(8,128)(2,1)S(1)} %fusion.1.onehot_t, bf16[256,1024]{1,0:T(8,128)(2,1)} %get-tuple-element.178.refs_0_, bf16[256,1024]{1,0:T(8,128)(2,1)} %collective-permute-done.53.refs_1_, bf16[8,256,1024]{2,1,0:T(8,128)(2,1)} %refs_3_.2), custom_call_target="tpu_custom_call" | custom-call | flops 1 | bytes 1 | tf_op jit(solution)/shard_map/place_rows/pallas_call | solution.py:126
  240.4 3.7 %collective-permute-start.60 = (bf16[128,1024]{1,0:T(8,128)(2,1)S(1)}, bf16[128,1024]{1,0:T(8,128)(2,1)S(1)}, u32[]{:S(2)}, u32[]{:S(2)}) collective-permute-start(bf16[128,1024]{1,0:T(8,128)(2,1)S(1)} %add_convert_fusion.2), channel_id=1, source_target_pairs={{16,0},{20,4},{24,8},{28,12},{0,16},{4,20},{8,24},{12,28},{17,1},{... | collective-permute-start | bytes 786440 | tf_op jit(solution)/shard_map/ppermute | solution.py:725
  245.6 3.6 %place_rows.5 = bf16[8,256,1024]{2,1,0:T(8,128)(2,1)} custom-call(s32[4]{0:T(128)S(1)} %add_add_fusion.order, bf16[8,256,128]{2,1,0:T(8,128)(2,1)S(1)} %fusion.1.onehot_t, bf16[256,1024]{1,0:T(8,128)(2,1)S(1)} %collective-permute-done.50.refs_0_, bf16[128,1024]{1,0:T(8,128)(2,1)S(1)} %collective-permute-done.51.refs_1_, ...), custom_call_target="tpu_custom_call", output_to_operand_aliasing={{}: (6, {})} | custom-call | flops 1 | bytes 1 | tf_op jit(solution)/shard_map/place_rows/pallas_call | solution.py:126
  249.2 7.3 %collective-permute-done.58 = bf16[384,1024]{1,0:T(8,128)(2,1)S(1)} collective-permute-done((bf16[384,1024]{1,0:T(8,128)(2,1)S(1)}, bf16[384,1024]{1,0:T(8,128)(2,1)S(1)}, u32[]{:S(2)}, u32[]{:S(2)}) %collective-permute-start.58) | collective-permute-done | bytes 786464 | tf_op jit(solution)/shard_map/ppermute | solution.py:697
  256.5 3.6 %place_rows.6.refs_4_ = bf16[8,256,1024]{2,1,0:T(8,128)(2,1)} custom-call(s32[4]{0:T(128)S(1)} %pad_add_fusion.2.order, bf16[8,256,128]{2,1,0:T(8,128)(2,1)S(1)} %fusion.1.onehot_t, bf16[256,1024]{1,0:T(8,128)(2,1)S(1)} %get-tuple-element.179.refs_0_, bf16[256,1024]{1,0:T(8,128)(2,1)S(1)} %collective-permute-done.55.refs_1_, bf16[8,256,1024]{2,1,0:T(8,128)(2,1)} %refs_3_.3), custom_call_target="tpu_custom_call" | custom-call | flops 1 | bytes 1 | tf_op jit(solution)/shard_map/place_rows/pallas_call | solution.py:126
  263.7 3.6 %place_rows.7 = bf16[8,256,1024]{2,1,0:T(8,128)(2,1)} custom-call(s32[4]{0:T(128)S(1)} %add_add_fusion.order, bf16[8,256,128]{2,1,0:T(8,128)(2,1)S(1)} %fusion.1.onehot_t, bf16[256,1024]{1,0:T(8,128)(2,1)S(1)} %collective-permute-done.54.refs_0_, bf16[128,1024]{1,0:T(8,128)(2,1)S(1)} %collective-permute-done.56.refs_1_, ...), custom_call_target="tpu_custom_call", output_to_operand_aliasing={{}: (6, {})} | custom-call | flops 1 | bytes 1 | tf_op jit(solution)/shard_map/place_rows/pallas_call | solution.py:126
  267.3 3.0 collective-permute-start.68
  271.7 2.4 collective-permute-start.66
  274.1 11.3 %collective-permute-done.62.p3 = bf16[128,1024]{1,0:T(8,128)(2,1)S(1)} collective-permute-done((bf16[128,1024]{1,0:T(8,128)(2,1)S(1)}, bf16[128,1024]{1,0:T(8,128)(2,1)S(1)}, u32[]{:S(2)}, u32[]{:S(2)}) %collective-permute-start.62) | collective-permute-done | bytes 262176 | tf_op jit(solution)/shard_map/ppermute | solution.py:725
  285.4 2.9 collective-permute-done.61.p2
  (345 shorter events, 108.7 us)
Async XLA Ops:
  7.2 124.9 %all-gather.2.cloned.1.call-start = ((), (), s32[]{:S(2)}) async-start(), calls=%async_computation.1 | async-start | bytes 4718592 | tf_op jit(solution)/shard_map/all_gather | solution.py:817
  23.2 28.1 %collective-permute-start.8 = (bf16[144,1024]{1,0:T(8,128)(2,1)S(1)}, bf16[144,1024]{1,0:T(8,128)(2,1)S(1)}, u32[]{:S(2)}, u32[]{:S(2)}) collective-permute-start(bf16[144,1024]{1,0:T(8,128)(2,1)S(1)} %pack_attn.1.refs_0_.near_own), channel_id=1, source_target_pairs={{8,0},{12,4},{16,8},{20,12},{24,16},{28,20},{0,24},{4,28},{9,1},{1... | collective-permute-start | bytes 884744 | tf_op jit(solution)/shard_map/ppermute | solution.py:725
  25.2 26.1 %collective-permute-start.4 = (bf16[144,1024]{1,0:T(8,128)(2,1)S(1)}, bf16[144,1024]{1,0:T(8,128)(2,1)S(1)}, u32[]{:S(2)}, u32[]{:S(2)}) collective-permute-start(bf16[144,1024]{1,0:T(8,128)(2,1)S(1)} %pack_attn.1.refs_0_.near_own), channel_id=1, source_target_pairs={{16,0},{20,4},{24,8},{28,12},{0,16},{4,20},{8,24},{12,28},{17,1},{... | collective-permute-start | bytes 884744 | tf_op jit(solution)/shard_map/ppermute | solution.py:725
  33.1 14.1 %collective-permute-start.7 = (bf16[128,1024]{1,0:T(8,128)(2,1)}, bf16[128,1024]{1,0:T(8,128)(2,1)}, u32[]{:S(2)}, u32[]{:S(2)}) collective-permute-start(bf16[128,1024]{1,0:T(8,128)(2,1)} %get-tuple-element.241), channel_id=1, source_target_pairs={{0,2},{1,3},{2,0},{3,1},{4,6},{5,7},{6,4},{7,5},{8,10},{9,11},{10,... | collective-permute-start | bytes 786440 | tf_op jit(solution)/shard_map/ppermute | solution.py:697
  36.5 14.8 %collective-permute-start.6 = (bf16[128,1024]{1,0:T(8,128)(2,1)}, bf16[128,1024]{1,0:T(8,128)(2,1)}, u32[]{:S(2)}, u32[]{:S(2)}) collective-permute-start(bf16[128,1024]{1,0:T(8,128)(2,1)} %get-tuple-element.242), channel_id=1, source_target_pairs={{0,2},{1,3},{2,0},{3,1},{4,6},{5,7},{6,4},{7,5},{8,10},{9,11},{10,... | collective-permute-start | bytes 786440 | tf_op jit(solution)/shard_map/ppermute | solution.py:697
  52.9 238.1 %reduce-scatter.2.cloned.1.call-start = ((), (), s32[]{:S(2)}) async-start(), calls=%async_computation.2 | async-start | bytes 4718592 | tf_op jit(solution)/shard_map/reduce_scatter | solution.py:896
  57.0 31.0 %collective-permute-start.15 = (bf16[384,1024]{1,0:T(8,128)(2,1)}, bf16[384,1024]{1,0:T(8,128)(2,1)S(1)}, u32[]{:S(2)}, u32[]{:S(2)}) collective-permute-start(bf16[384,1024]{1,0:T(8,128)(2,1)} %get-tuple-element.124.near), channel_id=1, source_target_pairs={{0,4},{4,0},{8,12},{12,8},{16,20},{20,16},{24,28},{28,24},{1,5},{5... | collective-permute-start | bytes 2359304 | tf_op jit(solution)/shard_map/ppermute | solution.py:697
  61.0 14.4 %collective-permute-start.12 = (bf16[256,1024]{1,0:T(8,128)(2,1)S(1)}, bf16[256,1024]{1,0:T(8,128)(2,1)S(1)}, u32[]{:S(2)}, u32[]{:S(2)}) collective-permute-start(bf16[256,1024]{1,0:T(8,128)(2,1)S(1)} %get-tuple-element.129.refs_0_), channel_id=1, source_target_pairs={{0,2},{1,3},{2,0},{3,1},{4,6},{5,7},{6,4},{7,5},{8,10},{9,11},{10,... | collective-permute-start | bytes 1572872 | tf_op jit(solution)/shard_map/ppermute | solution.py:697
  62.6 25.3 %collective-permute-start.14 = (bf16[144,1024]{1,0:T(8,128)(2,1)S(1)}, bf16[144,1024]{1,0:T(8,128)(2,1)S(1)}, u32[]{:S(2)}, u32[]{:S(2)}) collective-permute-start(bf16[144,1024]{1,0:T(8,128)(2,1)S(1)} %pack_attn.1.refs_0_.near_own), channel_id=1, source_target_pairs={{0,4},{4,0},{8,12},{12,8},{16,20},{20,16},{24,28},{28,24},{1,5},{5... | collective-permute-start | bytes 884744 | tf_op jit(solution)/shard_map/ppermute | solution.py:697
  75.4 14.6 %collective-permute-start.13 = (bf16[256,1024]{1,0:T(8,128)(2,1)S(1)}, bf16[256,1024]{1,0:T(8,128)(2,1)S(1)}, u32[]{:S(2)}, u32[]{:S(2)}) collective-permute-start(bf16[256,1024]{1,0:T(8,128)(2,1)S(1)} %get-tuple-element.120.refs_2_.refs_5_), channel_id=1, source_target_pairs={{0,2},{1,3},{2,0},{3,1},{4,6},{5,7},{6,4},{7,5},{8,10},{9,11},{10,... | collective-permute-start | bytes 1572872 | tf_op jit(solution)/shard_map/ppermute | solution.py:697
  98.9 14.0 %collective-permute-start.23 = (bf16[256,1024]{1,0:T(8,128)(2,1)S(1)}, bf16[256,1024]{1,0:T(8,128)(2,1)S(1)}, u32[]{:S(2)}, u32[]{:S(2)}) collective-permute-start(bf16[256,1024]{1,0:T(8,128)(2,1)S(1)} %pad_maximum_fusion), channel_id=1, source_target_pairs={{0,2},{1,3},{2,0},{3,1},{4,6},{5,7},{6,4},{7,5},{8,10},{9,11},{10,... | collective-permute-start | bytes 1572872 | tf_op jit(solution)/shard_map/ppermute | solution.py:697
  113.6 13.3 %collective-permute-start.24 = (bf16[256,1024]{1,0:T(8,128)(2,1)S(1)}, bf16[256,1024]{1,0:T(8,128)(2,1)S(1)}, u32[]{:S(2)}, u32[]{:S(2)}) collective-permute-start(bf16[256,1024]{1,0:T(8,128)(2,1)S(1)} %get-tuple-element.144.refs_0_), channel_id=1, source_target_pairs={{0,2},{1,3},{2,0},{3,1},{4,6},{5,7},{6,4},{7,5},{8,10},{9,11},{10,... | collective-permute-start | bytes 1572872 | tf_op jit(solution)/shard_map/ppermute | solution.py:697
  147.7 14.6 %collective-permute-start.35 = (bf16[256,1024]{1,0:T(8,128)(2,1)S(1)}, bf16[256,1024]{1,0:T(8,128)(2,1)S(1)}, u32[]{:S(2)}, u32[]{:S(2)}) collective-permute-start(bf16[256,1024]{1,0:T(8,128)(2,1)S(1)} %pad_maximum_fusion.1), channel_id=1, source_target_pairs={{0,2},{1,3},{2,0},{3,1},{4,6},{5,7},{6,4},{7,5},{8,10},{9,11},{10,... | collective-permute-start | bytes 1572872 | tf_op jit(solution)/shard_map/ppermute | solution.py:697
  165.6 14.3 %collective-permute-start.40 = (bf16[256,1024]{1,0:T(8,128)(2,1)}, bf16[256,1024]{1,0:T(8,128)(2,1)}, u32[]{:S(2)}, u32[]{:S(2)}) collective-permute-start(bf16[256,1024]{1,0:T(8,128)(2,1)} %get-tuple-element.158.refs_0_.refs_5_), channel_id=1, source_target_pairs={{0,2},{1,3},{2,0},{3,1},{4,6},{5,7},{6,4},{7,5},{8,10},{9,11},{10,... | collective-permute-start | bytes 1572872 | tf_op jit(solution)/shard_map/ppermute | solution.py:697
  192.0 14.8 %collective-permute-start.41 = (bf16[256,1024]{1,0:T(8,128)(2,1)S(1)}, bf16[256,1024]{1,0:T(8,128)(2,1)S(1)}, u32[]{:S(2)}, u32[]{:S(2)}) collective-permute-start(bf16[256,1024]{1,0:T(8,128)(2,1)S(1)} %pad_maximum_fusion.2), channel_id=1, source_target_pairs={{0,2},{1,3},{2,0},{3,1},{4,6},{5,7},{6,4},{7,5},{8,10},{9,11},{10,... | collective-permute-start | bytes 1572872 | tf_op jit(solution)/shard_map/ppermute | solution.py:697
  192.7 14.1 %collective-permute-start.37 = (bf16[128,1024]{1,0:T(8,128)(2,1)S(1)}, bf16[128,1024]{1,0:T(8,128)(2,1)S(1)}, u32[]{:S(2)}, u32[]{:S(2)}) collective-permute-start(bf16[128,1024]{1,0:T(8,128)(2,1)S(1)} %get-tuple-element.221), channel_id=1, source_target_pairs={{0,1},{1,0},{2,3},{3,2},{4,5},{5,4},{6,7},{7,6},{8,9},{9,8},{10,11... | collective-permute-start | bytes 786440 | tf_op jit(solution)/shard_map/ppermute | solution.py:697
  193.0 13.9 %collective-permute-start.36 = (bf16[128,1024]{1,0:T(8,128)(2,1)S(1)}, bf16[128,1024]{1,0:T(8,128)(2,1)S(1)}, u32[]{:S(2)}, u32[]{:S(2)}) collective-permute-start(bf16[128,1024]{1,0:T(8,128)(2,1)S(1)} %get-tuple-element.222), channel_id=1, source_target_pairs={{0,1},{1,0},{2,3},{3,2},{4,5},{5,4},{6,7},{7,6},{8,9},{9,8},{10,11... | collective-permute-start | bytes 786440 | tf_op jit(solution)/shard_map/ppermute | solution.py:697
  194.4 29.9 %collective-permute-start.49 = (bf16[256,1024]{1,0:T(8,128)(2,1)}, bf16[256,1024]{1,0:T(8,128)(2,1)}, u32[]{:S(2)}, u32[]{:S(2)}) collective-permute-start(bf16[256,1024]{1,0:T(8,128)(2,1)} %pad_maximum_fusion.3), channel_id=1, source_target_pairs={{0,2},{1,3},{2,0},{3,1},{4,6},{5,7},{6,4},{7,5},{8,10},{9,11},{10,... | collective-permute-start | bytes 1572872 | tf_op jit(solution)/shard_map/ppermute | solution.py:697
  208.4 20.4 %collective-permute-start.50 = (bf16[256,1024]{1,0:T(8,128)(2,1)}, bf16[256,1024]{1,0:T(8,128)(2,1)S(1)}, u32[]{:S(2)}, u32[]{:S(2)}) collective-permute-start(bf16[256,1024]{1,0:T(8,128)(2,1)} %get-tuple-element.178.refs_0_), channel_id=1, source_target_pairs={{0,2},{1,3},{2,0},{3,1},{4,6},{5,7},{6,4},{7,5},{8,10},{9,11},{10,... | collective-permute-start | bytes 1572872 | tf_op jit(solution)/shard_map/ppermute | solution.py:697
  209.8 13.8 %collective-permute-start.48 = (bf16[128,1024]{1,0:T(8,128)(2,1)}, bf16[128,1024]{1,0:T(8,128)(2,1)}, u32[]{:S(2)}, u32[]{:S(2)}) collective-permute-start(bf16[128,1024]{1,0:T(8,128)(2,1)} %get-tuple-element.209), channel_id=1, source_target_pairs={{0,1},{1,0},{2,3},{3,2},{4,5},{5,4},{6,7},{7,6},{8,9},{9,8},{10,11... | collective-permute-start | bytes 786440 | tf_op jit(solution)/shard_map/ppermute | solution.py:697
  209.9 24.7 %collective-permute-start.53 = (bf16[256,1024]{1,0:T(8,128)(2,1)}, bf16[256,1024]{1,0:T(8,128)(2,1)}, u32[]{:S(2)}, u32[]{:S(2)}) collective-permute-start(bf16[256,1024]{1,0:T(8,128)(2,1)} %get-tuple-element.178.refs_0_), channel_id=1, source_target_pairs={{0,1},{1,0},{2,3},{3,2},{4,5},{5,4},{6,7},{7,6},{8,9},{9,8},{10,11... | collective-permute-start | bytes 1572872 | tf_op jit(solution)/shard_map/ppermute | solution.py:697
  210.4 15.4 %collective-permute-start.47 = (bf16[128,1024]{1,0:T(8,128)(2,1)}, bf16[128,1024]{1,0:T(8,128)(2,1)}, u32[]{:S(2)}, u32[]{:S(2)}) collective-permute-start(bf16[128,1024]{1,0:T(8,128)(2,1)} %get-tuple-element.210), channel_id=1, source_target_pairs={{0,1},{1,0},{2,3},{3,2},{4,5},{5,4},{6,7},{7,6},{8,9},{9,8},{10,11... | collective-permute-start | bytes 786440 | tf_op jit(solution)/shard_map/ppermute | solution.py:697
  224.3 32.3 %collective-permute-start.58 = (bf16[384,1024]{1,0:T(8,128)(2,1)S(1)}, bf16[384,1024]{1,0:T(8,128)(2,1)S(1)}, u32[]{:S(2)}, u32[]{:S(2)}) collective-permute-start(bf16[384,1024]{1,0:T(8,128)(2,1)S(1)} %get-tuple-element.182), channel_id=1, source_target_pairs={{0,4},{4,0},{8,12},{12,8},{16,20},{20,16},{24,28},{28,24},{1,5},{5... | collective-permute-start | bytes 2359304 | tf_op jit(solution)/shard_map/ppermute | solution.py:697
  227.9 28.6 %collective-permute-start.55 = (bf16[256,1024]{1,0:T(8,128)(2,1)S(1)}, bf16[256,1024]{1,0:T(8,128)(2,1)S(1)}, u32[]{:S(2)}, u32[]{:S(2)}) collective-permute-start(bf16[256,1024]{1,0:T(8,128)(2,1)S(1)} %get-tuple-element.179.refs_0_), channel_id=1, source_target_pairs={{0,1},{1,0},{2,3},{3,2},{4,5},{5,4},{6,7},{7,6},{8,9},{9,8},{10,11... | collective-permute-start | bytes 1572872 | tf_op jit(solution)/shard_map/ppermute | solution.py:697
  228.7 31.4 %collective-permute-start.54 = (bf16[256,1024]{1,0:T(8,128)(2,1)S(1)}, bf16[256,1024]{1,0:T(8,128)(2,1)S(1)}, u32[]{:S(2)}, u32[]{:S(2)}) collective-permute-start(bf16[256,1024]{1,0:T(8,128)(2,1)S(1)} %get-tuple-element.179.refs_0_), channel_id=1, source_target_pairs={{0,2},{1,3},{2,0},{3,1},{4,6},{5,7},{6,4},{7,5},{8,10},{9,11},{10,... | collective-permute-start | bytes 1572872 | tf_op jit(solution)/shard_map/ppermute | solution.py:697
  240.4 31.2 %collective-permute-start.60 = (bf16[128,1024]{1,0:T(8,128)(2,1)S(1)}, bf16[128,1024]{1,0:T(8,128)(2,1)S(1)}, u32[]{:S(2)}, u32[]{:S(2)}) collective-permute-start(bf16[128,1024]{1,0:T(8,128)(2,1)S(1)} %add_convert_fusion.2), channel_id=1, source_target_pairs={{16,0},{20,4},{24,8},{28,12},{0,16},{4,20},{8,24},{12,28},{17,1},{... | collective-permute-start | bytes 786440 | tf_op jit(solution)/shard_map/ppermute | solution.py:725
  244.1 18.8 %collective-permute-start.64 = (f32[8,1024]{1,0:T(8,128)S(1)}, f32[8,1024]{1,0:T(8,128)S(1)}, u32[]{:S(2)}, u32[]{:S(2)}) collective-permute-start(f32[8,1024]{1,0:T(8,128)S(1)} %add.136), channel_id=1, source_target_pairs={{0,2},{1,3},{2,0},{3,1},{4,6},{5,7},{6,4},{7,5},{8,10},{9,11},{10,... | collective-permute-start | bytes 98312 | tf_op jit(solution)/shard_map/ppermute | solution.py:697
  260.9 24.5 %collective-permute-start.62 = (bf16[128,1024]{1,0:T(8,128)(2,1)S(1)}, bf16[128,1024]{1,0:T(8,128)(2,1)S(1)}, u32[]{:S(2)}, u32[]{:S(2)}) collective-permute-start(bf16[128,1024]{1,0:T(8,128)(2,1)S(1)} %get-tuple-element.203), channel_id=1, source_target_pairs={{8,0},{12,4},{16,8},{20,12},{24,16},{28,20},{0,24},{4,28},{9,1},{1... | collective-permute-start | bytes 786440 | tf_op jit(solution)/shard_map/ppermute | solution.py:725
  262.9 25.5 %collective-permute-start.61 = (bf16[128,1024]{1,0:T(8,128)(2,1)S(1)}, bf16[128,1024]{1,0:T(8,128)(2,1)S(1)}, u32[]{:S(2)}, u32[]{:S(2)}) collective-permute-start(bf16[128,1024]{1,0:T(8,128)(2,1)S(1)} %get-tuple-element.204), channel_id=1, source_target_pairs={{24,0},{28,4},{0,8},{4,12},{8,16},{12,20},{16,24},{20,28},{25,1},{... | collective-permute-start | bytes 786440 | tf_op jit(solution)/shard_map/ppermute | solution.py:725
  267.3 22.5 %collective-permute-start.68 = (f32[8,1024]{1,0:T(8,128)S(1)}, f32[8,1024]{1,0:T(8,128)S(1)}, u32[]{:S(2)}, u32[]{:S(2)}) collective-permute-start(f32[8,1024]{1,0:T(8,128)S(1)} %add.138), channel_id=1, source_target_pairs={{16,0},{20,4},{24,8},{28,12},{0,16},{4,20},{8,24},{12,28},{17,1},{... | collective-permute-start | bytes 98312 | tf_op jit(solution)/shard_map/ppermute | solution.py:725
  270.3 20.2 %collective-permute-start.67 = (f32[8,1024]{1,0:T(8,128)S(1)}, f32[8,1024]{1,0:T(8,128)S(1)}, u32[]{:S(2)}, u32[]{:S(2)}) collective-permute-start(f32[8,1024]{1,0:T(8,128)S(1)} %add.138), channel_id=1, source_target_pairs={{24,0},{28,4},{0,8},{4,12},{8,16},{12,20},{16,24},{20,28},{25,1},{... | collective-permute-start | bytes 98312 | tf_op jit(solution)/shard_map/ppermute | solution.py:725
  271.7 18.8 %collective-permute-start.66 = (f32[8,1024]{1,0:T(8,128)S(1)}, f32[8,1024]{1,0:T(8,128)S(1)}, u32[]{:S(2)}, u32[]{:S(2)}) collective-permute-start(f32[8,1024]{1,0:T(8,128)S(1)} %add.138), channel_id=1, source_target_pairs={{8,0},{12,4},{16,8},{20,12},{24,16},{28,20},{0,24},{4,28},{9,1},{1... | collective-permute-start | bytes 98312 | tf_op jit(solution)/shard_map/ppermute | solution.py:725
  (116 other events, 929.2 us)
Sparse Core Ops, SparseCore 0:
  53.0 79.0 all-gather.1
  180.0 110.7 reduce-scatter.1

commit v5 on v4

--- a/solution.py
+++ b/solution.py
@@ -977,7 +977,7 @@
     )
 
     if grid:
-        vec_sum = vec_part
+        vec_sum = after(vec_part, token_grad)
         for axis, mask in (("tensor", 1), ("tensor", 2)):
             vec_sum = vec_sum + swap(vec_sum, axis, mask)
         vec_sum = vec_sum + after(swap(vec_sum, "fsdp", 1), token_grad)

time: 301 us -> 312 us (1.037)
  waiting for transfers between devices: 97.3 us -> 107 us
    ppermute x60, waiting for transfers between devices: 79.9 us -> 100 us  [swap(): return lax.ppermute(x, axis, [(i, i ^ mask) for i in range(size)])]
    ppermute x9, waiting for transfers between devices: 16 us -> 5.61 us  [z_move(): return lax.ppermute(x, 'fsdp', z_perm(lax.axis_size('fsdp'), shift))]
  transfers between devices with their start and end apart: 71 -> 71, of which waited for: 34 -> 33; matrix products, arithmetic and copies ran while one was open for 3% -> 3% of each run, Pallas kernels for 26% -> 25%
where the time goes in v5:
time: 312 us; the launch traced here: 311 us
  waiting for transfers between devices  107 us (34%)
  Pallas kernels  99.4 us (32%)
  starting transfers between devices  55 us (18%)
  local copies, waits for them, and re-layouts  28.9 us (9%)
  between operations  15.2 us (5%)
  other arithmetic  5.35 us (2%)
    ppermute x60, waiting for transfers between devices, swap(): return lax.ppermute(x, axis, [(i, i ^ mask) for i in range(size)])  100 us
    ppermute x60, starting transfers between devices, swap(): return lax.ppermute(x, axis, [(i, i ^ mask) for i in range(size)])  35.7 us
    unnamed x154, local copies, waits for them, and re-layouts  21.4 us
    pallas_call x2, Pallas kernels, mlp_both(): pl.pallas_call(functools.partial(mlp_kernel, parts=1 + len(nb)), in_specs...  20.5 us
    ppermute x9, starting transfers between devices, z_move(): return lax.ppermute(x, 'fsdp', z_perm(lax.axis_size('fsdp'), shift))  19.1 us
    pallas_call x4, Pallas kernels, place_rows(): pl.pallas_call(functools.partial(place_kernel, blocks=len(rows)), in_spec...  15.1 us
    pallas_call x2, Pallas kernels, attn_bwd(): pl.pallas_call(functools.partial(attn_bwd_kernel, parts=1 + len(gb)), in_...  13 us
    pallas_call x2, Pallas kernels, attn_fwd(): pl.pallas_call(functools.partial(attn_fwd_kernel, parts=1 + len(xb)), in_...  10.7 us
  transfers between devices with their start and end apart: 71, of which 33 were waited for; matrix products, arithmetic and copies ran while one was open for 3% of the time, Pallas kernels for 25%

profile of v5, /device:TPU:0, one launch (start us, length us, event | category | flops | bytes accessed | tf_op | source)
XLA Modules:
  0.0 310.8 jit_solution(5731384014700243144)
XLA Ops:
  10.1 2.6 pick_rows.4
  14.0 2.6 pick_rows.5.keep
  16.7 2.6 pick_rows.6
  20.2 3.0 collective-permute-start.9
  28.5 2.6 pick_rows.7.keep
  41.5 5.6 %collective-permute-done.7.far1 = bf16[128,1024]{1,0:T(8,128)(2,1)} collective-permute-done((bf16[128,1024]{1,0:T(8,128)(2,1)}, bf16[128,1024]{1,0:T(8,128)(2,1)}, u32[]{:S(2)}, u32[]{:S(2)}) %collective-permute-start.7) | collective-permute-done | bytes 262176 | tf_op jit(solution)/shard_map/ppermute | solution.py:697
  47.2 4.1 %collective-permute-done.6.far0 = bf16[128,1024]{1,0:T(8,128)(2,1)} collective-permute-done((bf16[128,1024]{1,0:T(8,128)(2,1)}, bf16[128,1024]{1,0:T(8,128)(2,1)}, u32[]{:S(2)}, u32[]{:S(2)}) %collective-permute-start.6) | collective-permute-done | bytes 262176 | tf_op jit(solution)/shard_map/ppermute | solution.py:697
  54.6 2.4 collective-permute-done.10
  65.3 10.1 %collective-permute-done.12.refs_0_.refs_2_ = bf16[256,1024]{1,0:T(8,128)(2,1)S(1)} collective-permute-done((bf16[256,1024]{1,0:T(8,128)(2,1)S(1)}, bf16[256,1024]{1,0:T(8,128)(2,1)S(1)}, u32[]{:S(2)}, u32[]{:S(2)}) %collective-permute-start.12) | collective-permute-done | bytes 524320 | tf_op jit(solution)/shard_map/ppermute | solution.py:697
  76.9 11.0 %collective-permute-done.14.far_own = bf16[144,1024]{1,0:T(8,128)(2,1)S(1)} collective-permute-done((bf16[144,1024]{1,0:T(8,128)(2,1)S(1)}, bf16[144,1024]{1,0:T(8,128)(2,1)S(1)}, u32[]{:S(2)}, u32[]{:S(2)}) %collective-permute-start.14) | collective-permute-done | bytes 294944 | tf_op jit(solution)/shard_map/ppermute | solution.py:697
  91.2 5.4 %attn_fwd.2 = (bf16[512,768]{1,0:T(8,128)(2,1)S(1)}, bf16[512,256]{1,0:T(8,128)(2,1)S(1)}, bf16[256,1024]{1,0:T(8,128)(2,1)S(1)}, bf16[256,1024]{1,0:T(8,128)(2,1)S(1)}) custom-call(s32[4]{0:T(128)S(1)} %add_add_fusion.order, bf16[256,1024]{1,0:T(8,128)(2,1)S(1)} %collective-permute-done.12.refs_0_.refs_2_, ...), custom_call_target="tpu_custom_call" | custom-call | flops 1 | bytes 1 | tf_op jit(solution)/shard_map/attn_fwd/pallas_call | solution.py:473
  100.6 5.4 %attn_fwd.3 = (bf16[512,768]{1,0:T(8,128)(2,1)S(1)}, bf16[512,256]{1,0:T(8,128)(2,1)S(1)}, bf16[256,1024]{1,0:T(8,128)(2,1)S(1)}, bf16[256,1024]{1,0:T(8,128)(2,1)S(1)}) custom-call(s32[4]{0:T(128)S(1)} %pad_add_fusion.2.order, bf16[256,1024]{1,0:T(8,128)(2,1)S(1)} %get-tuple-element.130.refs_0_, bf16[256,1024]{1,0:T(8,128)(2,1)S(1)} %collective-permute-done.20.refs_1_, ...), custom_call_target="tpu_custom_call" | custom-call | flops 1 | bytes 1 | tf_op jit(solution)/shard_map/attn_fwd/pallas_call | solution.py:473
  108.0 4.9 %collective-permute-done.23.c = bf16[256,1024]{1,0:T(8,128)(2,1)S(1)} collective-permute-done((bf16[256,1024]{1,0:T(8,128)(2,1)S(1)}, bf16[256,1024]{1,0:T(8,128)(2,1)S(1)}, u32[]{:S(2)}, u32[]{:S(2)}) %collective-permute-start.23) | collective-permute-done | bytes 524320 | tf_op jit(solution)/shard_map/ppermute | solution.py:697
  115.8 11.1 %collective-permute-done.24.refs_0_.refs_2_ = bf16[256,1024]{1,0:T(8,128)(2,1)S(1)} collective-permute-done((bf16[256,1024]{1,0:T(8,128)(2,1)S(1)}, bf16[256,1024]{1,0:T(8,128)(2,1)S(1)}, u32[]{:S(2)}, u32[]{:S(2)}) %collective-permute-start.24) | collective-permute-done | bytes 524320 | tf_op jit(solution)/shard_map/ppermute | solution.py:697
  135.1 10.3 %mlp.2 = (bf16[512,1024]{1,0:T(8,128)(2,1)S(1)}, bf16[512,1024]{1,0:T(8,128)(2,1)S(1)}, bf16[256,1024]{1,0:T(8,128)(2,1)S(1)}, bf16[256,1024]{1,0:T(8,128)(2,1)S...) custom-call(bf16[256,1024]{1,0:T(8,128)(2,1)S(1)} %copy-done.4, bf16[128,1024]{1,0:T(8,128)(2,1)S(1)} %copy-done.36, ...), custom_call_target="tpu_custom_call" | custom-call | flops 1 | bytes 1 | tf_op jit(solution)/shard_map/mlp/pallas_call | solution.py:588
  150.0 10.2 %mlp.3 = (bf16[512,1024]{1,0:T(8,128)(2,1)S(1)}, bf16[512,1024]{1,0:T(8,128)(2,1)S(1)}, bf16[256,1024]{1,0:T(8,128)(2,1)S(1)}, bf16[256,1024]{1,0:T(8,128)(2,1)S...) custom-call(bf16[256,1024]{1,0:T(8,128)(2,1)S(1)} %copy-done.21, ...), custom_call_target="tpu_custom_call" | custom-call | flops 1 | bytes 1 | tf_op jit(solution)/shard_map/mlp/pallas_call | solution.py:588
  166.5 8.3 %mlp_grads.1 = bf16[2048,1024]{1,0:T(8,128)(2,1)S(1)} custom-call(bf16[256,1024]{1,0:T(8,128)(2,1)S(1)} %copy-done.21, bf16[256,1024]{1,0:T(8,128)(2,1)S(1)} %collective-permute-done.31.refs_1_, bf16[256,1024]{1,0:T(8,128)(2,1)S(1)} %copy-done.5, bf16[128,1024]{1,0:T(8,128)(2,1)S(1)} %copy-done.37, bf16[128,1024]{1,0:T(8,128)(2,1)S(1)} %copy-done.34, ...), custom_call_target="tpu_custom_call" | custom-call | flops 1 | bytes 1 | tf_op jit(solution)/shard_map/mlp_grads/pallas_call | solution.py:634
  176.9 3.0 collective-permute-done.40.refs_0_.refs_7_
  184.7 6.6 %attn_bwd.2 = (bf16[512,768]{1,0:T(8,128)(2,1)S(1)}, bf16[256,1024]{1,0:T(8,128)(2,1)S(1)}, bf16[256,1024]{1,0:T(8,128)(2,1)S(1)}) custom-call(s32[4]{0:T(128)S(1)} %add_add_fusion.order, bf16[256,1024]{1,0:T(8,128)(2,1)} %collective-permute-done.40.refs_0_.refs_7_, bf16[128,1024]{1,0:T(8,128)(2,1)S(1)} %collective-permute-done.42.refs_1_.refs_8_, ...), custom_call_target="tpu_custom_call" | custom-call | flops 1 | bytes 1 | tf_op jit(solution)/shard_map/attn_bwd/pallas_call | solution.py:527
  195.8 6.5 %attn_bwd.3 = (bf16[512,768]{1,0:T(8,128)(2,1)S(1)}, bf16[256,1024]{1,0:T(8,128)(2,1)S(1)}, bf16[256,1024]{1,0:T(8,128)(2,1)S(1)}) custom-call(s32[4]{0:T(128)S(1)} %pad_add_fusion.2.order, bf16[256,1024]{1,0:T(8,128)(2,1)} %get-tuple-element.159.refs_0_.refs_5_, bf16[256,1024]{1,0:T(8,128)(2,1)S(1)} %collective-permute-done.46.refs_1_.refs_6_, ...), custom_call_target="tpu_custom_call" | custom-call | flops 1 | bytes 1 | tf_op jit(solution)/shard_map/attn_bwd/pallas_call | solution.py:527
  202.3 4.5 %collective-permute-done.41.c = bf16[256,1024]{1,0:T(8,128)(2,1)S(1)} collective-permute-done((bf16[256,1024]{1,0:T(8,128)(2,1)S(1)}, bf16[256,1024]{1,0:T(8,128)(2,1)S(1)}, u32[]{:S(2)}, u32[]{:S(2)}) %collective-permute-start.41) | collective-permute-done | bytes 524320 | tf_op jit(solution)/shard_map/ppermute | solution.py:697
  218.6 5.0 %attn_grads.1 = (bf16[128,1024]{1,0:T(8,128)(2,1)S(1)}, bf16[384,1024]{1,0:T(8,128)(2,1)S(1)}, f32[128,1024]{1,0:T(8,128)S(1)}, f32[128,1024]{1,0:T(8,128)S(1)},...) custom-call(s32[5]{0:T(128)S(1)} %stack.86.info, bf16[256,1024]{1,0:T(8,128)(2,1)S(1)} %copy-done.25, ...), custom_call_target="tpu_custom_call" | custom-call | flops 1 | bytes 1 | tf_op jit(solution)/shard_map/attn_grads/pallas_call | solution.py:678
  229.6 27.0 %collective-permute-done.59 = bf16[128,1024]{1,0:T(8,128)(2,1)S(1)} collective-permute-done((bf16[128,1024]{1,0:T(8,128)(2,1)S(1)}, bf16[128,1024]{1,0:T(8,128)(2,1)S(1)}, u32[]{:S(2)}, u32[]{:S(2)}) %collective-permute-start.59) | collective-permute-done | bytes 262176 | tf_op jit(solution)/shard_map/ppermute | solution.py:697
  257.2 4.3 %place_rows.4.refs_4_ = bf16[8,256,1024]{2,1,0:T(8,128)(2,1)} custom-call(s32[4]{0:T(128)S(1)} %pad_add_fusion.2.order, bf16[8,256,128]{2,1,0:T(8,128)(2,1)S(1)} %fusion.1.onehot_t, bf16[256,1024]{1,0:T(8,128)(2,1)} %get-tuple-element.179.refs_0_, bf16[256,1024]{1,0:T(8,128)(2,1)} %collective-permute-done.53.refs_1_, bf16[8,256,1024]{2,1,0:T(8,128)(2,1)} %refs_3_.2), custom_call_target="tpu_custom_call" | custom-call | flops 1 | bytes 1 | tf_op jit(solution)/shard_map/place_rows/pallas_call | solution.py:126
  263.6 3.6 %place_rows.5 = bf16[8,256,1024]{2,1,0:T(8,128)(2,1)} custom-call(s32[4]{0:T(128)S(1)} %add_add_fusion.order, bf16[8,256,128]{2,1,0:T(8,128)(2,1)S(1)} %fusion.1.onehot_t, bf16[256,1024]{1,0:T(8,128)(2,1)S(1)} %collective-permute-done.50.refs_0_, bf16[128,1024]{1,0:T(8,128)(2,1)S(1)} %collective-permute-done.51.refs_1_, ...), custom_call_target="tpu_custom_call", output_to_operand_aliasing={{}: (6, {})} | custom-call | flops 1 | bytes 1 | tf_op jit(solution)/shard_map/place_rows/pallas_call | solution.py:126
  267.2 3.6 %place_rows.6.refs_4_ = bf16[8,256,1024]{2,1,0:T(8,128)(2,1)} custom-call(s32[4]{0:T(128)S(1)} %pad_add_fusion.2.order, bf16[8,256,128]{2,1,0:T(8,128)(2,1)S(1)} %fusion.1.onehot_t, bf16[256,1024]{1,0:T(8,128)(2,1)S(1)} %get-tuple-element.180.refs_0_, bf16[256,1024]{1,0:T(8,128)(2,1)S(1)} %collective-permute-done.55.refs_1_, bf16[8,256,1024]{2,1,0:T(8,128)(2,1)} %refs_3_.3), custom_call_target="tpu_custom_call" | custom-call | flops 1 | bytes 1 | tf_op jit(solution)/shard_map/place_rows/pallas_call | solution.py:126
  273.7 3.6 %place_rows.7 = bf16[8,256,1024]{2,1,0:T(8,128)(2,1)} custom-call(s32[4]{0:T(128)S(1)} %add_add_fusion.order, bf16[8,256,128]{2,1,0:T(8,128)(2,1)S(1)} %fusion.1.onehot_t, bf16[256,1024]{1,0:T(8,128)(2,1)S(1)} %collective-permute-done.54.refs_0_, bf16[128,1024]{1,0:T(8,128)(2,1)S(1)} %collective-permute-done.56.refs_1_, ...), custom_call_target="tpu_custom_call", output_to_operand_aliasing={{}: (6, {})} | custom-call | flops 1 | bytes 1 | tf_op jit(solution)/shard_map/place_rows/pallas_call | solution.py:126
  280.0 2.4 collective-permute-done.64
  284.0 2.4 collective-permute-done.65
  287.4 2.9 collective-permute-start.67
  290.3 5.1 %collective-permute-start.66 = (f32[8,1024]{1,0:T(8,128)S(1)}, f32[8,1024]{1,0:T(8,128)S(1)}, u32[]{:S(2)}, u32[]{:S(2)}) collective-permute-start(f32[8,1024]{1,0:T(8,128)S(1)} %add.138), channel_id=1, source_target_pairs={{8,0},{12,4},{16,8},{20,12},{24,16},{28,20},{0,24},{4,28},{9,1},{1... | collective-permute-start | bytes 98312 | tf_op jit(solution)/shard_map/ppermute | solution.py:725
  297.4 3.9 %collective-permute-done.68 = f32[8,1024]{1,0:T(8,128)S(1)} collective-permute-done((f32[8,1024]{1,0:T(8,128)S(1)}, f32[8,1024]{1,0:T(8,128)S(1)}, u32[]{:S(2)}, u32[]{:S(2)}) %collective-permute-start.68) | collective-permute-done | bytes 32800 | tf_op jit(solution)/shard_map/ppermute | solution.py:725
  (345 shorter events, 109.1 us)
Async XLA Ops:
  7.2 124.9 %all-gather.2.cloned.1.call-start = ((), (), s32[]{:S(2)}) async-start(), calls=%async_computation.1 | async-start | bytes 4718592 | tf_op jit(solution)/shard_map/all_gather | solution.py:817
  23.2 28.1 %collective-permute-start.8 = (bf16[144,1024]{1,0:T(8,128)(2,1)S(1)}, bf16[144,1024]{1,0:T(8,128)(2,1)S(1)}, u32[]{:S(2)}, u32[]{:S(2)}) collective-permute-start(bf16[144,1024]{1,0:T(8,128)(2,1)S(1)} %pack_attn.1.refs_0_.near_own), channel_id=1, source_target_pairs={{8,0},{12,4},{16,8},{20,12},{24,16},{28,20},{0,24},{4,28},{9,1},{1... | collective-permute-start | bytes 884744 | tf_op jit(solution)/shard_map/ppermute | solution.py:725
  25.2 26.1 %collective-permute-start.4 = (bf16[144,1024]{1,0:T(8,128)(2,1)S(1)}, bf16[144,1024]{1,0:T(8,128)(2,1)S(1)}, u32[]{:S(2)}, u32[]{:S(2)}) collective-permute-start(bf16[144,1024]{1,0:T(8,128)(2,1)S(1)} %pack_attn.1.refs_0_.near_own), channel_id=1, source_target_pairs={{16,0},{20,4},{24,8},{28,12},{0,16},{4,20},{8,24},{12,28},{17,1},{... | collective-permute-start | bytes 884744 | tf_op jit(solution)/shard_map/ppermute | solution.py:725
  33.1 14.1 %collective-permute-start.7 = (bf16[128,1024]{1,0:T(8,128)(2,1)}, bf16[128,1024]{1,0:T(8,128)(2,1)}, u32[]{:S(2)}, u32[]{:S(2)}) collective-permute-start(bf16[128,1024]{1,0:T(8,128)(2,1)} %get-tuple-element.243), channel_id=1, source_target_pairs={{0,2},{1,3},{2,0},{3,1},{4,6},{5,7},{6,4},{7,5},{8,10},{9,11},{10,... | collective-permute-start | bytes 786440 | tf_op jit(solution)/shard_map/ppermute | solution.py:697
  36.5 14.8 %collective-permute-start.6 = (bf16[128,1024]{1,0:T(8,128)(2,1)}, bf16[128,1024]{1,0:T(8,128)(2,1)}, u32[]{:S(2)}, u32[]{:S(2)}) collective-permute-start(bf16[128,1024]{1,0:T(8,128)(2,1)} %get-tuple-element.244), channel_id=1, source_target_pairs={{0,2},{1,3},{2,0},{3,1},{4,6},{5,7},{6,4},{7,5},{8,10},{9,11},{10,... | collective-permute-start | bytes 786440 | tf_op jit(solution)/shard_map/ppermute | solution.py:697
  52.9 249.0 %reduce-scatter.2.cloned.1.call-start = ((), (), s32[]{:S(2)}) async-start(), calls=%async_computation.2 | async-start | bytes 4718592 | tf_op jit(solution)/shard_map/reduce_scatter | solution.py:896
  57.0 31.0 %collective-permute-start.15 = (bf16[384,1024]{1,0:T(8,128)(2,1)}, bf16[384,1024]{1,0:T(8,128)(2,1)S(1)}, u32[]{:S(2)}, u32[]{:S(2)}) collective-permute-start(bf16[384,1024]{1,0:T(8,128)(2,1)} %get-tuple-element.125.near), channel_id=1, source_target_pairs={{0,4},{4,0},{8,12},{12,8},{16,20},{20,16},{24,28},{28,24},{1,5},{5... | collective-permute-start | bytes 2359304 | tf_op jit(solution)/shard_map/ppermute | solution.py:697
  61.0 14.4 %collective-permute-start.12 = (bf16[256,1024]{1,0:T(8,128)(2,1)S(1)}, bf16[256,1024]{1,0:T(8,128)(2,1)S(1)}, u32[]{:S(2)}, u32[]{:S(2)}) collective-permute-start(bf16[256,1024]{1,0:T(8,128)(2,1)S(1)} %get-tuple-element.130.refs_0_), channel_id=1, source_target_pairs={{0,2},{1,3},{2,0},{3,1},{4,6},{5,7},{6,4},{7,5},{8,10},{9,11},{10,... | collective-permute-start | bytes 1572872 | tf_op jit(solution)/shard_map/ppermute | solution.py:697
  62.6 25.3 %collective-permute-start.14 = (bf16[144,1024]{1,0:T(8,128)(2,1)S(1)}, bf16[144,1024]{1,0:T(8,128)(2,1)S(1)}, u32[]{:S(2)}, u32[]{:S(2)}) collective-permute-start(bf16[144,1024]{1,0:T(8,128)(2,1)S(1)} %pack_attn.1.refs_0_.near_own), channel_id=1, source_target_pairs={{0,4},{4,0},{8,12},{12,8},{16,20},{20,16},{24,28},{28,24},{1,5},{5... | collective-permute-start | bytes 884744 | tf_op jit(solution)/shard_map/ppermute | solution.py:697
  75.4 14.6 %collective-permute-start.13 = (bf16[256,1024]{1,0:T(8,128)(2,1)S(1)}, bf16[256,1024]{1,0:T(8,128)(2,1)S(1)}, u32[]{:S(2)}, u32[]{:S(2)}) collective-permute-start(bf16[256,1024]{1,0:T(8,128)(2,1)S(1)} %get-tuple-element.121.refs_2_.refs_5_), channel_id=1, source_target_pairs={{0,2},{1,3},{2,0},{3,1},{4,6},{5,7},{6,4},{7,5},{8,10},{9,11},{10,... | collective-permute-start | bytes 1572872 | tf_op jit(solution)/shard_map/ppermute | solution.py:697
  98.9 14.0 %collective-permute-start.23 = (bf16[256,1024]{1,0:T(8,128)(2,1)S(1)}, bf16[256,1024]{1,0:T(8,128)(2,1)S(1)}, u32[]{:S(2)}, u32[]{:S(2)}) collective-permute-start(bf16[256,1024]{1,0:T(8,128)(2,1)S(1)} %pad_maximum_fusion), channel_id=1, source_target_pairs={{0,2},{1,3},{2,0},{3,1},{4,6},{5,7},{6,4},{7,5},{8,10},{9,11},{10,... | collective-permute-start | bytes 1572872 | tf_op jit(solution)/shard_map/ppermute | solution.py:697
  113.6 13.3 %collective-permute-start.24 = (bf16[256,1024]{1,0:T(8,128)(2,1)S(1)}, bf16[256,1024]{1,0:T(8,128)(2,1)S(1)}, u32[]{:S(2)}, u32[]{:S(2)}) collective-permute-start(bf16[256,1024]{1,0:T(8,128)(2,1)S(1)} %get-tuple-element.145.refs_0_), channel_id=1, source_target_pairs={{0,2},{1,3},{2,0},{3,1},{4,6},{5,7},{6,4},{7,5},{8,10},{9,11},{10,... | collective-permute-start | bytes 1572872 | tf_op jit(solution)/shard_map/ppermute | solution.py:697
  115.2 13.1 %collective-permute-start.28 = (bf16[128,1024]{1,0:T(8,128)(2,1)S(1)}, bf16[128,1024]{1,0:T(8,128)(2,1)S(1)}, u32[]{:S(2)}, u32[]{:S(2)}) collective-permute-start(bf16[128,1024]{1,0:T(8,128)(2,1)S(1)} %get-tuple-element.231), channel_id=1, source_target_pairs={{0,1},{1,0},{2,3},{3,2},{4,5},{5,4},{6,7},{7,6},{8,9},{9,8},{10,11... | collective-permute-start | bytes 786440 | tf_op jit(solution)/shard_map/ppermute | solution.py:697
  147.7 14.6 %collective-permute-start.35 = (bf16[256,1024]{1,0:T(8,128)(2,1)S(1)}, bf16[256,1024]{1,0:T(8,128)(2,1)S(1)}, u32[]{:S(2)}, u32[]{:S(2)}) collective-permute-start(bf16[256,1024]{1,0:T(8,128)(2,1)S(1)} %pad_maximum_fusion.1), channel_id=1, source_target_pairs={{0,2},{1,3},{2,0},{3,1},{4,6},{5,7},{6,4},{7,5},{8,10},{9,11},{10,... | collective-permute-start | bytes 1572872 | tf_op jit(solution)/shard_map/ppermute | solution.py:697
  165.6 14.3 %collective-permute-start.40 = (bf16[256,1024]{1,0:T(8,128)(2,1)}, bf16[256,1024]{1,0:T(8,128)(2,1)}, u32[]{:S(2)}, u32[]{:S(2)}) collective-permute-start(bf16[256,1024]{1,0:T(8,128)(2,1)} %get-tuple-element.159.refs_0_.refs_5_), channel_id=1, source_target_pairs={{0,2},{1,3},{2,0},{3,1},{4,6},{5,7},{6,4},{7,5},{8,10},{9,11},{10,... | collective-permute-start | bytes 1572872 | tf_op jit(solution)/shard_map/ppermute | solution.py:697
  192.0 14.8 %collective-permute-start.41 = (bf16[256,1024]{1,0:T(8,128)(2,1)S(1)}, bf16[256,1024]{1,0:T(8,128)(2,1)S(1)}, u32[]{:S(2)}, u32[]{:S(2)}) collective-permute-start(bf16[256,1024]{1,0:T(8,128)(2,1)S(1)} %pad_maximum_fusion.2), channel_id=1, source_target_pairs={{0,2},{1,3},{2,0},{3,1},{4,6},{5,7},{6,4},{7,5},{8,10},{9,11},{10,... | collective-permute-start | bytes 1572872 | tf_op jit(solution)/shard_map/ppermute | solution.py:697
  192.7 14.1 %collective-permute-start.37 = (bf16[128,1024]{1,0:T(8,128)(2,1)S(1)}, bf16[128,1024]{1,0:T(8,128)(2,1)S(1)}, u32[]{:S(2)}, u32[]{:S(2)}) collective-permute-start(bf16[128,1024]{1,0:T(8,128)(2,1)S(1)} %get-tuple-element.223), channel_id=1, source_target_pairs={{0,1},{1,0},{2,3},{3,2},{4,5},{5,4},{6,7},{7,6},{8,9},{9,8},{10,11... | collective-permute-start | bytes 786440 | tf_op jit(solution)/shard_map/ppermute | solution.py:697
  193.0 13.9 %collective-permute-start.36 = (bf16[128,1024]{1,0:T(8,128)(2,1)S(1)}, bf16[128,1024]{1,0:T(8,128)(2,1)S(1)}, u32[]{:S(2)}, u32[]{:S(2)}) collective-permute-start(bf16[128,1024]{1,0:T(8,128)(2,1)S(1)} %get-tuple-element.224), channel_id=1, source_target_pairs={{0,1},{1,0},{2,3},{3,2},{4,5},{5,4},{6,7},{7,6},{8,9},{9,8},{10,11... | collective-permute-start | bytes 786440 | tf_op jit(solution)/shard_map/ppermute | solution.py:697
  194.4 29.8 %collective-permute-start.49 = (bf16[256,1024]{1,0:T(8,128)(2,1)}, bf16[256,1024]{1,0:T(8,128)(2,1)}, u32[]{:S(2)}, u32[]{:S(2)}) collective-permute-start(bf16[256,1024]{1,0:T(8,128)(2,1)} %pad_maximum_fusion.3), channel_id=1, source_target_pairs={{0,2},{1,3},{2,0},{3,1},{4,6},{5,7},{6,4},{7,5},{8,10},{9,11},{10,... | collective-permute-start | bytes 1572872 | tf_op jit(solution)/shard_map/ppermute | solution.py:697
  208.4 20.4 %collective-permute-start.50 = (bf16[256,1024]{1,0:T(8,128)(2,1)}, bf16[256,1024]{1,0:T(8,128)(2,1)S(1)}, u32[]{:S(2)}, u32[]{:S(2)}) collective-permute-start(bf16[256,1024]{1,0:T(8,128)(2,1)} %get-tuple-element.179.refs_0_), channel_id=1, source_target_pairs={{0,2},{1,3},{2,0},{3,1},{4,6},{5,7},{6,4},{7,5},{8,10},{9,11},{10,... | collective-permute-start | bytes 1572872 | tf_op jit(solution)/shard_map/ppermute | solution.py:697
  209.8 13.8 %collective-permute-start.48 = (bf16[128,1024]{1,0:T(8,128)(2,1)}, bf16[128,1024]{1,0:T(8,128)(2,1)}, u32[]{:S(2)}, u32[]{:S(2)}) collective-permute-start(bf16[128,1024]{1,0:T(8,128)(2,1)} %get-tuple-element.211), channel_id=1, source_target_pairs={{0,1},{1,0},{2,3},{3,2},{4,5},{5,4},{6,7},{7,6},{8,9},{9,8},{10,11... | collective-permute-start | bytes 786440 | tf_op jit(solution)/shard_map/ppermute | solution.py:697
  209.9 46.7 %collective-permute-start.53 = (bf16[256,1024]{1,0:T(8,128)(2,1)}, bf16[256,1024]{1,0:T(8,128)(2,1)}, u32[]{:S(2)}, u32[]{:S(2)}) collective-permute-start(bf16[256,1024]{1,0:T(8,128)(2,1)} %get-tuple-element.179.refs_0_), channel_id=1, source_target_pairs={{0,1},{1,0},{2,3},{3,2},{4,5},{5,4},{6,7},{7,6},{8,9},{9,8},{10,11... | collective-permute-start | bytes 1572872 | tf_op jit(solution)/shard_map/ppermute | solution.py:697
  210.4 15.4 %collective-permute-start.47 = (bf16[128,1024]{1,0:T(8,128)(2,1)}, bf16[128,1024]{1,0:T(8,128)(2,1)}, u32[]{:S(2)}, u32[]{:S(2)}) collective-permute-start(bf16[128,1024]{1,0:T(8,128)(2,1)} %get-tuple-element.212), channel_id=1, source_target_pairs={{0,1},{1,0},{2,3},{3,2},{4,5},{5,4},{6,7},{7,6},{8,9},{9,8},{10,11... | collective-permute-start | bytes 786440 | tf_op jit(solution)/shard_map/ppermute | solution.py:697
  223.6 43.6 %collective-permute-start.58 = (bf16[384,1024]{1,0:T(8,128)(2,1)S(1)}, bf16[384,1024]{1,0:T(8,128)(2,1)S(1)}, u32[]{:S(2)}, u32[]{:S(2)}) collective-permute-start(bf16[384,1024]{1,0:T(8,128)(2,1)S(1)} %get-tuple-element.183), channel_id=1, source_target_pairs={{0,4},{4,0},{8,12},{12,8},{16,20},{20,16},{24,28},{28,24},{1,5},{5... | collective-permute-start | bytes 2359304 | tf_op jit(solution)/shard_map/ppermute | solution.py:697
  224.3 32.3 %collective-permute-start.59 = (bf16[128,1024]{1,0:T(8,128)(2,1)S(1)}, bf16[128,1024]{1,0:T(8,128)(2,1)S(1)}, u32[]{:S(2)}, u32[]{:S(2)}) collective-permute-start(bf16[128,1024]{1,0:T(8,128)(2,1)S(1)} %get-tuple-element.172), channel_id=1, source_target_pairs={{0,4},{4,0},{8,12},{12,8},{16,20},{20,16},{24,28},{28,24},{1,5},{5... | collective-permute-start | bytes 786440 | tf_op jit(solution)/shard_map/ppermute | solution.py:697
  227.9 39.3 %collective-permute-start.55 = (bf16[256,1024]{1,0:T(8,128)(2,1)S(1)}, bf16[256,1024]{1,0:T(8,128)(2,1)S(1)}, u32[]{:S(2)}, u32[]{:S(2)}) collective-permute-start(bf16[256,1024]{1,0:T(8,128)(2,1)S(1)} %get-tuple-element.180.refs_0_), channel_id=1, source_target_pairs={{0,1},{1,0},{2,3},{3,2},{4,5},{5,4},{6,7},{7,6},{8,9},{9,8},{10,11... | collective-permute-start | bytes 1572872 | tf_op jit(solution)/shard_map/ppermute | solution.py:697
  228.7 42.1 %collective-permute-start.54 = (bf16[256,1024]{1,0:T(8,128)(2,1)S(1)}, bf16[256,1024]{1,0:T(8,128)(2,1)S(1)}, u32[]{:S(2)}, u32[]{:S(2)}) collective-permute-start(bf16[256,1024]{1,0:T(8,128)(2,1)S(1)} %get-tuple-element.180.refs_0_), channel_id=1, source_target_pairs={{0,2},{1,3},{2,0},{3,1},{4,6},{5,7},{6,4},{7,5},{8,10},{9,11},{10,... | collective-permute-start | bytes 1572872 | tf_op jit(solution)/shard_map/ppermute | solution.py:697
  261.5 28.7 %collective-permute-start.60 = (bf16[128,1024]{1,0:T(8,128)(2,1)S(1)}, bf16[128,1024]{1,0:T(8,128)(2,1)S(1)}, u32[]{:S(2)}, u32[]{:S(2)}) collective-permute-start(bf16[128,1024]{1,0:T(8,128)(2,1)S(1)} %add_convert_fusion.2), channel_id=1, source_target_pairs={{16,0},{20,4},{24,8},{28,12},{0,16},{4,20},{8,24},{12,28},{17,1},{... | collective-permute-start | bytes 786440 | tf_op jit(solution)/shard_map/ppermute | solution.py:725
  271.6 25.0 %collective-permute-start.62 = (bf16[128,1024]{1,0:T(8,128)(2,1)S(1)}, bf16[128,1024]{1,0:T(8,128)(2,1)S(1)}, u32[]{:S(2)}, u32[]{:S(2)}) collective-permute-start(bf16[128,1024]{1,0:T(8,128)(2,1)S(1)} %get-tuple-element.205), channel_id=1, source_target_pairs={{8,0},{12,4},{16,8},{20,12},{24,16},{28,20},{0,24},{4,28},{9,1},{1... | collective-permute-start | bytes 786440 | tf_op jit(solution)/shard_map/ppermute | solution.py:725
  273.1 23.4 %collective-permute-start.61 = (bf16[128,1024]{1,0:T(8,128)(2,1)S(1)}, bf16[128,1024]{1,0:T(8,128)(2,1)S(1)}, u32[]{:S(2)}, u32[]{:S(2)}) collective-permute-start(bf16[128,1024]{1,0:T(8,128)(2,1)S(1)} %get-tuple-element.206), channel_id=1, source_target_pairs={{24,0},{28,4},{0,8},{4,12},{8,16},{12,20},{16,24},{20,28},{25,1},{... | collective-permute-start | bytes 786440 | tf_op jit(solution)/shard_map/ppermute | solution.py:725
  286.4 14.9 %collective-permute-start.68 = (f32[8,1024]{1,0:T(8,128)S(1)}, f32[8,1024]{1,0:T(8,128)S(1)}, u32[]{:S(2)}, u32[]{:S(2)}) collective-permute-start(f32[8,1024]{1,0:T(8,128)S(1)} %add.138), channel_id=1, source_target_pairs={{16,0},{20,4},{24,8},{28,12},{0,16},{4,20},{8,24},{12,28},{17,1},{... | collective-permute-start | bytes 98312 | tf_op jit(solution)/shard_map/ppermute | solution.py:725
  287.4 13.9 %collective-permute-start.67 = (f32[8,1024]{1,0:T(8,128)S(1)}, f32[8,1024]{1,0:T(8,128)S(1)}, u32[]{:S(2)}, u32[]{:S(2)}) collective-permute-start(f32[8,1024]{1,0:T(8,128)S(1)} %add.138), channel_id=1, source_target_pairs={{24,0},{28,4},{0,8},{4,12},{8,16},{12,20},{16,24},{20,28},{25,1},{... | collective-permute-start | bytes 98312 | tf_op jit(solution)/shard_map/ppermute | solution.py:725
  (116 other events, 936.6 us)
Sparse Core Ops, SparseCore 0:
  53.0 79.0 all-gather.1
  180.0 111.8 reduce-scatter.1
